TPU v7x, 256 devices: a whole 4x4x8 slice. The times are simulated.
256 devices in a mesh: ctx: 32 (over y, z), head: 8 (over x, core).
Axes of the slice: x: 4, y: 4, z: 8, core: 2. Of those that a mesh axis runs over, the one named last changes fastest.
Arguments:
- qkv: bfloat16 [32768, 3, 32, 128], P(('ctx', 'head')), may hold values from -50 to 50, as said below
- lengths: int32 [8], replicated, may hold values from 1 to 16384, 32768 in all
- reg: float32 [32], replicated, may hold values from 0.5 to 2
Outputs:
- mixed: bfloat16 [32768, 32, 128], P(('ctx', 'head'))
Inputs may be any that keep to these rules, and one draw needn't show every extreme that they name: `qkv`: entries of queries, keys and values; each head's channels have scales that differ by up to a factor of ten or more. `lengths`: the longest document has exactly 16384 tokens.
All inputs are finite; a program needn't handle non-finite values.
Results may differ from a plain program's by a relative error of at most 0.0056.
Values may be sent and summed in bfloat16 or wider, within the bound.
No kernel may reach another device: no remote copies, remote signals or barrier semaphores. Data moves between devices by JAX's collectives and lax.ppermute only.
A program may use at most 128 MiB of HBM per device.

v0:
```python
import math

import jax
import jax.numpy as jnp
from jax import lax
from jax.sharding import PartitionSpec as P

ITERS = 10


HIGHEST = lax.Precision.HIGHEST


def carried_in(part, axis, combine, identity):
    place = lax.axis_index(axis)
    gathered = jax.tree.map(lambda a: lax.all_gather(a, axis), part)
    state = jax.tree.map(lambda a, e: jnp.zeros_like(a) + jnp.asarray(e, a.dtype), part, identity)

    def one(turn, state):
        return combine(
            state, jax.tree.map(lambda a: lax.dynamic_index_in_dim(a, turn, 0, False), gathered)
        )

    return lax.fori_loop(0, place, one, state)


def normalize(rows):
    rows = rows.astype(jnp.float32)
    return (
        rows
        * lax.rsqrt(jnp.mean(rows * rows, axis=-1, keepdims=True) + 1e-06)
        / math.sqrt(rows.shape[-1])
    )


def prepare(stacked):
    row_count = stacked.shape[0]
    width = stacked.shape[-1]
    queries = normalize(stacked[:, 0].reshape(row_count, -1, width))
    key_rows = normalize(stacked[:, 1].reshape(row_count, -1, width)).astype(jnp.bfloat16)
    value_rows = stacked[:, 2].reshape(row_count, -1, width)
    return (queries, key_rows, value_rows)


def doc_marks(lengths, offset, row_count):
    doc_ends = jnp.cumsum(lengths)
    starts = doc_ends - lengths
    places = offset + jnp.arange(row_count, dtype=jnp.int32)
    start_mark = jnp.any(places[:, None] == starts[None, :], axis=1)
    segment = jnp.sum((starts[None, :] <= places[:, None]).astype(jnp.int32), axis=1)
    return (starts, start_mark, segment)


def combine(earlier, later):
    keep = 1.0 - later[0]
    return (
        jnp.maximum(earlier[0], later[0]),
        keep * earlier[1] + later[1],
        keep * earlier[2] + later[2],
    )


def block_sums(key_rows, value_rows, segment, start_mark):
    in_tail = (segment == segment[:, -1:]).astype(jnp.bfloat16)
    reset_flag = jnp.max(start_mark.astype(jnp.float32), axis=1)
    weighted = key_rows * in_tail[:, :, None, None]
    key_sum = jnp.einsum("cbhd,cbhe->chde", weighted, key_rows, preferred_element_type=jnp.float32)
    value_sum = jnp.einsum(
        "cbhd,cbhe->chde",
        value_rows * in_tail[:, :, None, None],
        key_rows,
        preferred_element_type=jnp.float32,
    )
    return (reset_flag, key_sum, value_sum)


def solve_blocks(
    queries, key_rows, value_rows, segment, start_mark, key_entry, value_entry, damping
):
    block_len = queries.shape[1]
    valid = (jnp.cumsum(start_mark.astype(jnp.int32), axis=1) == 0).astype(jnp.float32)[
        :, :, None, None
    ]
    lower = jnp.arange(block_len)[:, None] >= jnp.arange(block_len)[None, :]
    same = ((segment[:, :, None] == segment[:, None, :]) & lower[None]).astype(jnp.float32)[:, None]

    def block_scores(vectors):
        scores = (
            jnp.einsum(
                "cbhd,cihd->chbi",
                vectors.astype(jnp.bfloat16),
                key_rows,
                preferred_element_type=jnp.float32,
            )
            * same
        )
        return scores.astype(jnp.bfloat16)

    solution = jnp.zeros_like(queries)
    residual = queries
    direction = queries
    res_norm = jnp.sum(residual * residual, axis=-1)
    for sweep in range(ITERS):
        operate_from_state = (
            jnp.einsum("chde,cbhe->cbhd", key_entry, direction, precision=HIGHEST) * valid
        )
        operate_in_block = jnp.einsum(
            "chbi,cihd->cbhd", block_scores(direction), key_rows, preferred_element_type=jnp.float32
        )
        image = operate_from_state + operate_in_block + damping[None, None, :, None] * direction
        step_len = res_norm / (jnp.sum(direction * image, axis=-1) + 1e-06)
        solution = solution + step_len[..., None] * direction
        residual = residual - step_len[..., None] * image
        new_norm = jnp.sum(residual * residual, axis=-1)
        direction = residual + (new_norm / (res_norm + 1e-06))[..., None] * direction
        res_norm = new_norm
    from_state = jnp.einsum("chde,cbhe->cbhd", value_entry, solution, precision=HIGHEST) * valid
    in_block = jnp.einsum(
        "chbi,cihd->cbhd", block_scores(solution), value_rows, preferred_element_type=jnp.float32
    )
    return from_state + in_block


def mesa_local(queries, key_rows, value_rows, lengths, damping, offset, carry_in):
    row_count, head_count, width = queries.shape
    block_len = math.gcd(row_count, 256)
    block_count = row_count // block_len
    starts, start_mark, segment = doc_marks(lengths, offset, row_count)
    shape = (block_count, block_len, head_count, width)
    queries = queries.reshape(shape)
    key_rows = key_rows.reshape(shape)
    value_rows = value_rows.reshape(shape)
    segment = segment.reshape(block_count, block_len)
    start_mark = start_mark.reshape(block_count, block_len)
    reset_flag, key_sum, value_sum = block_sums(key_rows, value_rows, segment, start_mark)
    zeros = jnp.zeros((head_count, width, width), jnp.float32)
    running = (jnp.zeros((), jnp.float32), zeros, zeros)
    prefixes = []
    for member in range(block_count):
        prefixes.append(running)
        running = combine(running, (reset_flag[member], key_sum[member], value_sum[member]))
    entry = carry_in(running, starts, offset, row_count)
    entered = [combine(entry, item) for item in prefixes]
    key_entry = jnp.stack([item[1] for item in entered])
    value_entry = jnp.stack([item[2] for item in entered])

    def one_block(pieces):
        query_block, key_block, value_block, segment_block, mark_block, key_state, value_state = (
            pieces
        )
        return solve_blocks(
            query_block[None],
            key_block[None],
            value_block[None],
            segment_block[None],
            mark_block[None],
            key_state[None],
            value_state[None],
            damping,
        )[0]

    result = lax.map(
        one_block, (queries, key_rows, value_rows, segment, start_mark, key_entry, value_entry)
    )
    return result.reshape(row_count, head_count, width).astype(jnp.bfloat16)


def empty_state(running):
    return (jnp.zeros((), jnp.float32), jnp.zeros_like(running[1]), jnp.zeros_like(running[2]))


def body(qkv, lengths, reg):
    group_count = lax.axis_size("head")
    grouped = qkv.reshape(qkv.shape[0], 3, group_count, qkv.shape[2] // group_count, qkv.shape[3])
    queries, key_rows, value_rows = prepare(
        lax.all_to_all(grouped, "head", split_axis=2, concat_axis=0, tiled=True)
    )
    row_count = queries.shape[0]
    head_count = queries.shape[1]
    my_index = lax.axis_index("ctx")
    offset = my_index * row_count
    damping = lax.dynamic_slice_in_dim(reg, lax.axis_index("head") * head_count, head_count)

    def carry_in(running, starts, offset, row_count):
        return carried_in(running, "ctx", combine, empty_state(running))

    mixed = mesa_local(queries, key_rows, value_rows, lengths, damping, offset, carry_in)
    return lax.all_to_all(mixed, "head", split_axis=0, concat_axis=1, tiled=True)


def solution(mesh):
    in_specs = (P(("ctx", "head"), None, None, None), P(), P())
    out_specs = P(("ctx", "head"), None, None)
    return jax.shard_map(body, mesh=mesh, in_specs=in_specs, out_specs=out_specs, check_vma=False)
```

profile of v0, /device:TPU:248, one launch (start us, length us, event | category | flops | bytes accessed | tf_op | source)
XLA Modules:
  0.0 609.8 jit_solution(480572297779198474)
XLA Ops:
  6.5 4.8 copy.171
  11.3 4.4 all-to-all-start
  19.7 34.4 %all-to-all-done = bf16[128,3,8,4,128]{4,0,3,1,2:T(8,128)(2,1)S(1)} async-done(((bf16[128,3,8,4,128]{4,0,3,1,2:T(8,128)(2,1)}), bf16[128,3,8,4,128]{4,0,3,1,2:T(8,128)(2,1)S(1)}, u32[]{:S(2)}, u32[]{:S(2)}) %all-to-all-start) | async-done | bytes 3145760 | tf_op jit(solution)/shard_map/all_to_all | solution.py:176
  68.2 70.5 %all-reduce = f32[32]{0:T(128)S(1)} all-reduce(f32[32]{0:T(128)S(1)} %get-tuple-element.247), channel_id=1, replica_groups=mesh['ctx'=32,'head'=8] {'ctx'}, use_global_device_ids=true, to_apply=%add | all-reduce | flops 32 | bytes 256
  141.4 11.4 %all-gather.5.cloned.1.call-done = f32[32,4,128,128]{3,2,1,0:T(8,128)} async-done(((f32[1,4,128,128]{3,2,1,0:T(8,128)}), f32[32,4,128,128]{3,2,1,0:T(8,128)}) %all-gather.5.cloned.1.call-update) | async-done | bytes 8388624 | tf_op jit(solution)/shard_map/all_gather | solution.py:16
  152.8 97.4 %all-gather.3.cloned.1.call-done = f32[32,4,128,128]{3,2,1,0:T(8,128)} async-done(((f32[1,4,128,128]{3,2,1,0:T(8,128)}), f32[32,4,128,128]{3,2,1,0:T(8,128)}) %all-gather.3.cloned.1.call-update) | async-done | bytes 8388624 | tf_op jit(solution)/shard_map/all_gather | solution.py:16
  250.2 76.4 %while.24 = (s32[]{:T(128)}, f32[4,128,128]{2,1,0:T(8,128)S(1)}, f32[4,128,128]{2,1,0:T(8,128)S(1)}, s32[]{:T(128)}, f32[32]{0:T(128)S(1)}, /*index=5*/f32[32,4,...) while((s32[]{:T(128)}, f32[4,128,128]{2,1,0:T(8,128)S(1)}, ...), condition=%wide.region_7.8_spmd, body=%wide.region_6.7_spmd.sunk | while | flops 262150 | bytes 1573039 | solution.py:24
  330.2 248.9 %while.25 = (s32[]{:T(128)}, bf16[4,256,4,128]{3,1,0,2:T(8,128)(2,1)}, f32[4,256,4,128]{3,1,0,2:T(8,128)}, f32[4,4,128,128]{3,2,1,0:T(8,128)}, pred[4,256]{1,0:T...) while((s32[]{:T(128)}, ...), condition=%wide.region_31.32_spmd, body=%wide.region_8.31_spmd.sunk | while | flops 3717384960 | bytes 124740720 | solution.py:162
  355.1 2.5 convolution_bitcast_fusion.38
  361.7 2.6 convolution_bitcast_fusion.39
  368.3 2.5 convolution_bitcast_fusion.40
  385.1 3.2 multiply_add_fusion.29
  417.4 2.5 convolution_bitcast_fusion.38
  430.4 2.5 convolution_bitcast_fusion.40
  437.0 2.5 convolution_bitcast_fusion.41
  447.2 3.2 multiply_add_fusion.29
  479.6 2.5 convolution_bitcast_fusion.38
  492.6 2.6 convolution_bitcast_fusion.40
  499.2 2.5 convolution_bitcast_fusion.41
  509.5 3.2 multiply_add_fusion.29
  541.8 2.5 convolution_bitcast_fusion.38
  554.8 2.5 convolution_bitcast_fusion.40
  571.7 3.2 multiply_add_fusion.29
  581.1 20.0 %all_to_all.36 = bf16[1024,4,128]{2,1,0:T(4,128)(2,1)S(1)} all-to-all(bf16[1024,4,128]{2,1,0:T(4,128)(2,1)S(1)} %copy.183), channel_id=1, replica_groups=mesh['ctx'=32,'head'=8] {'head'}, dimensions={0} | all-to-all | bytes 2097152 | tf_op jit(solution)/shard_map/all_to_all | solution.py:188
  (550 shorter events, 286.1 us)
Async XLA Ops:
  11.3 4.5 copy-start.24
  11.3 42.8 %all-to-all-start = ((bf16[128,3,8,4,128]{4,0,3,1,2:T(8,128)(2,1)}), bf16[128,3,8,4,128]{4,0,3,1,2:T(8,128)(2,1)S(1)}, u32[]{:S(2)}, u32[]{:S(2)}) async-start(bf16[128,3,8,4,128]{4,0,3,1,2:T(8,128)(2,1)} %copy.171), calls=%async_computation | async-start | bytes 6291456 | tf_op jit(solution)/shard_map/all_to_all | solution.py:176
  15.7 137.1 %all-gather.5.cloned.1.call-start = ((), (), s32[]{:S(2)}) async-start(), calls=%async_computation.3 | async-start | bytes 8650752 | tf_op jit(solution)/shard_map/all_gather | solution.py:16
  60.1 190.1 %all-gather.3.cloned.1.call-start = ((), (), s32[]{:S(2)}) async-start(), calls=%async_computation.2 | async-start | bytes 8650752 | tf_op jit(solution)/shard_map/all_gather | solution.py:16
  60.1 4.7 copy-start.26
  60.1 7.9 %copy-start.25 = (f32[32]{0:T(128)S(1)}, f32[32]{0:T(128)}, u32[]{:S(2)}) copy-start(f32[32]{0:T(128)} %param.9) | copy-start | bytes 388
  250.2 76.5 %copy-start.21 = (f32[4,4,128,128]{3,2,1,0:T(8,128)S(1)}, f32[4,4,128,128]{3,2,1,0:T(8,128)}, u32[]{:S(2)}) copy-start(f32[4,4,128,128]{3,2,1,0:T(8,128)} %copy-done.20) | copy-start | bytes 3145732
  351.1 3.1 copy-start.1
  357.7 3.1 copy-start.2
  364.2 3.1 copy-start.3
  370.8 3.2 copy-start.4
  377.3 2.4 copy-start.5
  413.4 3.1 copy-start.1
  419.9 3.1 copy-start.2
  426.4 3.1 copy-start.3
  432.9 3.2 copy-start.4
  475.6 3.1 copy-start.1
  482.1 3.1 copy-start.2
  488.6 3.1 copy-start.3
  495.2 3.2 copy-start.4
  537.8 3.1 copy-start.1
  544.3 3.1 copy-start.2
  550.8 3.1 copy-start.3
  557.4 3.2 copy-start.4
  (63 other events, 96.4 us)
Sparse Core Ops, SparseCore 0:
  60.2 92.5 all-gather.4
  155.4 94.7 all-gather.2
where the time goes:
time: 613 us; the launch traced here: 610 us
  matrix products  179 us (29%)
  waiting for transfers between devices  143 us (23%)
  blocking collectives  90.5 us (15%)
  other arithmetic  89.8 us (15%)
  local copies, waits for them, and re-layouts  62.2 us (10%)
  loops' own time  22.5 us (4%)
  between operations  17.9 us (3%)
    all_gather x2, waiting for transfers between devices, carried_in(): gathered = jax.tree.map(lambda a: lax.all_gather(a, axis), part)  109 us
    dot_general x40, matrix products, solve_blocks(): jnp.einsum('chbi,cihd->cbhd', block_scores(direction), key_rows, preferre...  82.9 us
    dot_general x40, matrix products, solve_blocks(): jnp.einsum('chde,cbhe->cbhd', key_entry, direction, precision=HIGHEST)  81.1 us
    unnamed x1, blocking collectives  70.5 us
    add x32, other arithmetic, combine(): keep * earlier[2] + later[2]  37.3 us
    all_to_all x1, waiting for transfers between devices, body(): lax.all_to_all(grouped, 'head', split_axis=2, concat_axis=0, tiled=True)  34.4 us
    add x36, other arithmetic, solve_blocks(): residual + (new_norm / (res_norm + 1e-06))[..., None] * direction  21.9 us
    another operation x1, loops' own time, carried_in(): return lax.fori_loop(0, place, one, state)  20.8 us
  transfers between devices with their start and end apart: 3, of which 3 were waited for; matrix products, arithmetic and copies ran while one was open for 2% of the time, Pallas kernels for 0%

commit v1 on v0

v1 whole, which is shorter than its diff:
```python
import functools
import math

import jax
import jax.numpy as jnp
from jax import lax
from jax.experimental import pallas as pl
from jax.experimental.pallas import tpu as pltpu
from jax.sharding import PartitionSpec as P

ITERS = 10
BLOCK = 256
HD = 128
F32 = jnp.float32
BF = jnp.bfloat16


def dot(a, b):
    return lax.dot_general(a, b, (((1,), (0,)), ((), ())), preferred_element_type=F32)


def doc_of(info, place):
    doc = jnp.zeros_like(place)
    for j in range(info.shape[0] - 1):
        doc = doc + (place >= info[1 + j]).astype(jnp.int32)
    return doc


def sums_kernel(head_count, info, k_ref, v_ref, prefix_ref, total_ref):
    first = info[0]
    blocks = k_ref.shape[0] // 2
    last_docs = [doc_of(info, first + (b + 1) * BLOCK - 1) for b in range(blocks)]
    lanes = lax.broadcasted_iota(jnp.int32, (1, BLOCK), 1)
    for h in range(head_count):
        key_sums, value_sums = [], []
        for b in range(blocks):
            tail = (doc_of(info, first + b * BLOCK + lanes) == last_docs[b]).astype(F32).astype(BF)
            k = k_ref[2 * b : 2 * b + 2, h].reshape(BLOCK, HD)
            v = v_ref[2 * b : 2 * b + 2, h].reshape(BLOCK, HD)
            key_sums.append(dot(k.T * tail, k))
            value_sums.append(dot(v.T * tail, k))
        for which, sums in enumerate((key_sums, value_sums)):
            running = jnp.zeros((HD, HD), F32)
            for b in range(blocks):
                prefix_ref[b, h, which] = running
                if b == 0:
                    running = sums[0]
                else:
                    same = (last_docs[b] == last_docs[b - 1]).astype(F32)
                    running = same * running + sums[b]
            total_ref[h, which] = running.astype(total_ref.dtype)


def sums_call(info, k, v):
    head_count = k.shape[1]
    blocks = k.shape[0] // 2
    return pl.pallas_call(
        functools.partial(sums_kernel, head_count),
        grid_spec=pltpu.PrefetchScalarGridSpec(
            num_scalar_prefetch=1,
            grid=(1,),
            in_specs=[pl.BlockSpec(k.shape, lambda i, *_: (0, 0, 0, 0))] * 2,
            out_specs=[
                pl.BlockSpec((blocks, head_count, 2, HD, HD), lambda i, *_: (0, 0, 0, 0, 0)),
                pl.BlockSpec((head_count, 2, HD, HD), lambda i, *_: (0, 0, 0, 0)),
            ],
        ),
        out_shape=[
            jax.ShapeDtypeStruct((blocks, head_count, 2, HD, HD), F32),
            jax.ShapeDtypeStruct((head_count, 2, HD, HD), BF),
        ],
        name="block_sums",
    )(info, k, v)


def solve_kernel(
    head_count, info, reg_ref, q_ref, k_ref, v_ref, prefix_ref, entry_ref, out_ref,
    lhs, key_t, same, valid, direction, residual, solution, norm,
):
    b = pl.program_id(0)
    first = info[0]
    start = first + b * BLOCK
    before = doc_of(info, start - 1)
    carry = (doc_of(info, first - 1) == before).astype(F32)
    lane = start + lax.broadcasted_iota(jnp.int32, (1, BLOCK), 1)
    row = start + lax.broadcasted_iota(jnp.int32, (BLOCK, 1), 0)
    lane_doc = doc_of(info, lane)
    valid[...] = (lane_doc == before).astype(F32)
    same[...] = ((doc_of(info, row) == lane_doc) & (row <= lane)).astype(F32).astype(BF)
    for h in range(head_count):
        k = k_ref[:, h].reshape(BLOCK, HD)
        state = prefix_ref[0, h, 0] + carry * entry_ref[h, 0].astype(F32)
        high = state.astype(BF)
        lhs[h, 0:BLOCK] = k
        lhs[h, BLOCK : BLOCK + HD] = high
        lhs[h, BLOCK + HD : BLOCK + 2 * HD] = (state - high.astype(F32)).astype(BF)
        key_t[h] = k.T
        q = q_ref[:, h].reshape(BLOCK, HD).T.astype(F32)
        q = q * lax.rsqrt(jnp.mean(q * q, axis=0, keepdims=True) + 1e-06) / math.sqrt(HD)
        direction[h] = q
        residual[h] = q
        solution[h] = jnp.zeros_like(q)
        norm[h] = jnp.sum(q * q, axis=0, keepdims=True)

    def iterate(_, carried):
        held = []
        for h in range(head_count):
            p = direction[h]
            high = p.astype(BF)
            low = (p - high.astype(F32)).astype(BF)
            full = dot(lhs[h], high)
            rest = dot(lhs[h, BLOCK : BLOCK + HD], low)
            score = full[0:BLOCK].astype(BF) * same[...]
            held.append((p, full[BLOCK : BLOCK + HD] + full[BLOCK + HD :] + rest, score))
        for h in range(head_count):
            p, from_state, score = held[h]
            image = from_state * valid[...] + dot(key_t[h], score) + reg_ref[h] * p
            old = norm[h]
            step = old / (jnp.sum(p * image, axis=0, keepdims=True) + 1e-06)
            solution[h] = solution[h] + step * p
            r = residual[h] - step * image
            residual[h] = r
            new = jnp.sum(r * r, axis=0, keepdims=True)
            direction[h] = r + (new / (old + 1e-06)) * p
            norm[h] = new
        return carried

    lax.fori_loop(0, ITERS, iterate, 0)
    for h in range(head_count):
        x = solution[h]
        high = x.astype(BF)
        low = (x - high.astype(F32)).astype(BF)
        state = prefix_ref[0, h, 1] + carry * entry_ref[h, 1].astype(F32)
        state_high = state.astype(BF)
        state_low = (state - state_high.astype(F32)).astype(BF)
        score = dot(lhs[h, 0:BLOCK], high).astype(BF) * same[...]
        from_state = dot(state_high, high) + dot(state_low, high) + dot(state_high, low)
        v = v_ref[:, h].reshape(BLOCK, HD)
        result = from_state * valid[...] + dot(v.T, score)
        out_ref[:, h] = result.T.astype(BF).reshape(2, HD, HD)


def solve_call(info, damping, q, k, v, prefix, entry):
    head_count = q.shape[1]
    blocks = q.shape[0] // 2
    tokens = pl.BlockSpec((2, head_count, HD, HD), lambda b, *_: (b, 0, 0, 0))
    vectors = pltpu.VMEM((head_count, HD, BLOCK), F32)
    return pl.pallas_call(
        functools.partial(solve_kernel, head_count),
        grid_spec=pltpu.PrefetchScalarGridSpec(
            num_scalar_prefetch=2,
            grid=(blocks,),
            in_specs=[
                tokens,
                tokens,
                tokens,
                pl.BlockSpec((1, head_count, 2, HD, HD), lambda b, *_: (b, 0, 0, 0, 0)),
                pl.BlockSpec((head_count, 2, HD, HD), lambda b, *_: (0, 0, 0, 0)),
            ],
            out_specs=tokens,
            scratch_shapes=[
                pltpu.VMEM((head_count, BLOCK + 2 * HD, HD), BF),
                pltpu.VMEM((head_count, HD, BLOCK), BF),
                pltpu.VMEM((BLOCK, BLOCK), BF),
                pltpu.VMEM((1, BLOCK), F32),
                vectors,
                vectors,
                vectors,
                pltpu.VMEM((head_count, 1, BLOCK), F32),
            ],
        ),
        out_shape=jax.ShapeDtypeStruct(q.shape, BF),
        name="solve_blocks",
    )(info, damping, q, k, v, prefix, entry)


def normalize(rows):
    rows = rows.astype(F32)
    return (
        rows
        * lax.rsqrt(jnp.mean(rows * rows, axis=-1, keepdims=True) + 1e-06)
        / math.sqrt(rows.shape[-1])
    )


def body(qkv, lengths, reg):
    groups = lax.axis_size("head")
    places = lax.axis_size("ctx")
    rows, _, heads, width = qkv.shape
    mine = heads // groups
    local = rows * groups
    place = lax.axis_index("ctx")
    starts = (jnp.cumsum(lengths) - lengths).astype(jnp.int32)
    info = jnp.concatenate([jnp.reshape(place * local, (1,)).astype(jnp.int32), starts])
    damping = lax.dynamic_slice_in_dim(reg, lax.axis_index("head") * mine, mine)

    split = qkv.reshape(rows, 3, groups, mine, width)
    keys = normalize(split[:, 1]).astype(BF)
    key_value = jnp.stack([keys, split[:, 2]]).transpose(2, 0, 3, 1, 4)
    query = split[:, 0].transpose(1, 2, 0, 3)

    key_value = lax.all_to_all(key_value, "head", 0, 0, tiled=True)
    query = lax.all_to_all(query, "head", 0, 0, tiled=True)
    k, v = key_value[:, 0], key_value[:, 1]
    prefix, total = sums_call(info, k, v)

    ends = local * jnp.arange(1, places + 1, dtype=jnp.int32) - 1
    last = jnp.sum((starts[None, :] <= ends[:, None]).astype(jnp.int32), axis=1)
    order = jnp.arange(places)
    wanted = jnp.concatenate([jnp.zeros((1,), jnp.int32), last[:-1]])
    weight = ((order[None, :] < order[:, None]) & (wanted[:, None] == last[None, :])).astype(BF)
    sliced = lax.all_to_all(total.reshape(places, -1, width), "ctx", 0, 0, tiled=True)
    entries = jnp.einsum("pc,crw->prw", weight, sliced, preferred_element_type=F32).astype(BF)
    entry = lax.all_to_all(entries, "ctx", 0, 0, tiled=True).reshape(total.shape)

    mixed = solve_call(info, damping, query, k, v, prefix, entry)
    mixed = lax.all_to_all(mixed, "head", 0, 0, tiled=True)
    return mixed.reshape(heads, rows, width).transpose(1, 0, 2)


def solution(mesh):
    in_specs = (P(("ctx", "head"), None, None, None), P(), P())
    out_specs = P(("ctx", "head"), None, None)
    return jax.shard_map(body, mesh=mesh, in_specs=in_specs, out_specs=out_specs, check_vma=False)
```

time: 613 us -> 171 us (0.28)
  the two profiles are of different devices: /device:TPU:248 before, /device:TPU:1 now
where the time goes in v1:
time: 171 us; the launch traced here: 170 us
  waiting for transfers between devices  48.2 us (28%)
  Pallas kernels  47.9 us (28%)
  blocking collectives  42.1 us (25%)
  starting transfers between devices  18.2 us (11%)
  local copies, waits for them, and re-layouts  11 us (6%)
  other arithmetic  2.5 us (1%)
    pallas_call x1, Pallas kernels, solve_call(): pl.pallas_call(functools.partial(solve_kernel, head_count), grid_spec=plt...  43.5 us
    all_to_all x1, waiting for transfers between devices, body(): key_value = lax.all_to_all(key_value, 'head', 0, 0, tiled=True)  25.5 us
    all_to_all x1, blocking collectives, body(): mixed = lax.all_to_all(mixed, 'head', 0, 0, tiled=True)  22.1 us
    all_to_all x1, blocking collectives, body(): lax.all_to_all(total.reshape(places, -1, width), 'ctx', 0, 0, tiled=True)  20 us
    all_to_all x1, waiting for transfers between devices, body(): query = lax.all_to_all(query, 'head', 0, 0, tiled=True)  13.7 us
    all_to_all x1, waiting for transfers between devices, body(): lax.all_to_all(entries, 'ctx', 0, 0, tiled=True).reshape(total.shape)  9 us
    all_to_all x1, starting transfers between devices, body(): query = lax.all_to_all(query, 'head', 0, 0, tiled=True)  7.13 us
    all_to_all x1, starting transfers between devices, body(): key_value = lax.all_to_all(key_value, 'head', 0, 0, tiled=True)  6.84 us
  transfers between devices with their start and end apart: 3, of which 3 were waited for; matrix products, arithmetic and copies ran while one was open for 2% of the time, Pallas kernels for 0%

profile of v1, /device:TPU:1, one launch (start us, length us, event | category | flops | bytes accessed | tf_op | source)
XLA Modules:
  0.0 170.2 jit_solution(9424302647136224376)
XLA Ops:
  0.0 3.1 %copy.15 = bf16[128,3,32,128]{3,0,2,1:T(8,128)(2,1)S(1)} copy(bf16[128,3,32,128]{3,2,1,0:T(8,128)(2,1)} %param.3) | data formatting | bytes 6291456 | tf_op args[0]
  3.1 0.6 fusion.3
  3.7 1.2 slice_bitcast_fusion.2
  4.9 0.7 fusion.2
  5.6 0.2 maximum_bitcast_fusion
  5.8 1.5 copy.16
  7.3 6.8 %all-to-all-start.1 = ((bf16[8,2,4,128,128]{4,3,2,1,0:T(8,128)(2,1)}), bf16[8,2,4,128,128]{4,3,2,1,0:T(8,128)(2,1)S(1)}, u32[]{:S(2)}, u32[]{:S(2)}) async-start(bf16[8,2,4,128,128]{4,3,2,1,0:T(8,128)(2,1)} %copy.16), calls=%async_computation.1 | async-start | bytes 4194304 | tf_op jit(solution)/shard_map/all_to_all | solution.py:202
  14.1 0.2 reduce-window.9
  14.3 0.6 pad_add_fusion.info
  14.9 25.5 %all-to-all-done.1 = bf16[8,2,4,128,128]{4,3,2,1,0:T(8,128)(2,1)S(1)} async-done(((bf16[8,2,4,128,128]{4,3,2,1,0:T(8,128)(2,1)}), bf16[8,2,4,128,128]{4,3,2,1,0:T(8,128)(2,1)S(1)}, u32[]{:S(2)}, u32[]{:S(2)}) %all-to-all-start.1) | async-done | bytes 2097184 | tf_op jit(solution)/shard_map/all_to_all | solution.py:202
  40.4 1.4 slice_bitcast_fusion
  41.8 4.3 %block_sums.1 = (f32[4,4,2,128,128]{4,3,2,1,0:T(8,128)}, bf16[4,2,128,128]{3,2,1,0:T(8,128)(2,1)}) custom-call(s32[9]{0:T(128)} %pad_add_fusion.info, bf16[8,4,128,128]{3,2,1,0:T(8,128)(2,1)} %get-tuple-element.12.k_ref, bf16[8,4,128,128]{3,2,1,0:T(8,128)(2,1)} %get-tuple-element.11.v_ref), custom_call_target="tpu_custom_call" | custom-call | tf_op jit(solution)/shard_map/block_sums/pallas_call | solution.py:57
  46.2 20.0 %all_to_all.25 = bf16[32,32,128]{2,1,0:T(8,128)(2,1)S(1)} all-to-all(bf16[32,32,128]{2,1,0:T(8,128)(2,1)} %bitcast.44), channel_id=1, replica_groups=mesh['ctx'=32,'head'=8] {'ctx'}, dimensions={0} | all-to-all | bytes 524288 | tf_op jit(solution)/shard_map/all_to_all | solution.py:212
  66.2 7.1 %all-to-all-start = ((bf16[8,4,128,128]{3,2,1,0:T(8,128)(2,1)}), bf16[8,4,128,128]{3,2,1,0:T(8,128)(2,1)S(1)}, u32[]{:S(2)}, u32[]{:S(2)}) async-start(bf16[8,4,128,128]{3,2,1,0:T(8,128)(2,1)} %get-tuple-element.10), calls=%async_computation | async-start | bytes 2097152 | tf_op jit(solution)/shard_map/all_to_all | solution.py:203
  73.5 0.3 convolution_convert_fusion
  73.8 0.8 copy.20
  74.6 13.7 %all-to-all-done.q_ref = bf16[8,4,128,128]{3,2,1,0:T(8,128)(2,1)S(1)} async-done(((bf16[8,4,128,128]{3,2,1,0:T(8,128)(2,1)}), bf16[8,4,128,128]{3,2,1,0:T(8,128)(2,1)S(1)}, u32[]{:S(2)}, u32[]{:S(2)}) %all-to-all-start) | async-done | bytes 1048608 | tf_op jit(solution)/shard_map/all_to_all | solution.py:203
  88.3 4.2 %all-to-all-start.3 = ((bf16[32,32,128]{2,1,0:T(8,128)(2,1)}), bf16[32,32,128]{2,1,0:T(8,128)(2,1)S(1)}, u32[]{:S(2)}, u32[]{:S(2)}) async-start(bf16[32,32,128]{2,1,0:T(8,128)(2,1)} %copy.20), calls=%async_computation.3 | async-start | bytes 524288 | tf_op jit(solution)/shard_map/all_to_all | solution.py:214
  92.6 0.6 dynamic_slice.3.reg_ref
  93.2 9.0 %all-to-all-done.3 = bf16[32,32,128]{2,1,0:T(8,128)(2,1)S(1)} async-done(((bf16[32,32,128]{2,1,0:T(8,128)(2,1)}), bf16[32,32,128]{2,1,0:T(8,128)(2,1)S(1)}, u32[]{:S(2)}, u32[]{:S(2)}) %all-to-all-start.3) | async-done | bytes 262176 | tf_op jit(solution)/shard_map/all_to_all | solution.py:214
  102.2 0.7 copy-done.1
  102.9 43.5 %solve_blocks.1 = bf16[8,4,128,128]{3,2,1,0:T(8,128)(2,1)} custom-call(s32[9]{0:T(128)} %pad_add_fusion.info, f32[4]{0:T(128)} %dynamic_slice.3.reg_ref, bf16[8,4,128,128]{3,2,1,0:T(8,128)(2,1)} %copy-done, bf16[8,4,128,128]{3,2,1,0:T(8,128)(2,1)} %get-tuple-element.12.k_ref, bf16[8,4,128,128]{3,2,1,0:T(8,128)(2,1)} %get-tuple-element.11.v_ref, ...), custom_call_target="tpu_custom_call" | custom-call | tf_op jit(solution)/shard_map/solve_blocks/pallas_call | solution.py:148
  146.4 22.1 %all_to_all.26 = bf16[8,4,128,128]{3,2,1,0:T(8,128)(2,1)S(1)} all-to-all(bf16[8,4,128,128]{3,2,1,0:T(8,128)(2,1)} %solve_blocks.1), channel_id=1, replica_groups=mesh['ctx'=32,'head'=8] {'head'}, dimensions={0} | all-to-all | bytes 2097152 | tf_op jit(solution)/shard_map/all_to_all | solution.py:217
  168.5 1.6 copy.27
  (12 shorter events, 0.2 us)
Async XLA Ops:
  7.3 6.8 %copy-start.2 = (s32[8]{0:T(128)S(1)}, s32[8]{0:T(128)}, u32[]{:S(2)}) copy-start(s32[8]{0:T(128)} %param.4) | copy-start | bytes 100
  7.3 33.1 %all-to-all-start.1 = ((bf16[8,2,4,128,128]{4,3,2,1,0:T(8,128)(2,1)}), bf16[8,2,4,128,128]{4,3,2,1,0:T(8,128)(2,1)S(1)}, u32[]{:S(2)}, u32[]{:S(2)}) async-start(bf16[8,2,4,128,128]{4,3,2,1,0:T(8,128)(2,1)} %copy.16), calls=%async_computation.1 | async-start | bytes 4194304 | tf_op jit(solution)/shard_map/all_to_all | solution.py:202
  46.2 46.4 %copy-start.3 = (f32[32]{0:T(128)S(1)}, f32[32]{0:T(128)}, u32[]{:S(2)}) copy-start(f32[32]{0:T(128)} %param.5) | copy-start | bytes 388
  66.2 22.1 %all-to-all-start = ((bf16[8,4,128,128]{3,2,1,0:T(8,128)(2,1)}), bf16[8,4,128,128]{3,2,1,0:T(8,128)(2,1)S(1)}, u32[]{:S(2)}, u32[]{:S(2)}) async-start(bf16[8,4,128,128]{3,2,1,0:T(8,128)(2,1)} %get-tuple-element.10), calls=%async_computation | async-start | bytes 2097152 | tf_op jit(solution)/shard_map/all_to_all | solution.py:203
  88.3 13.9 %copy-start = (bf16[8,4,128,128]{3,2,1,0:T(8,128)(2,1)}, bf16[8,4,128,128]{3,2,1,0:T(8,128)(2,1)S(1)}, u32[]{:S(2)}) copy-start(bf16[8,4,128,128]{3,2,1,0:T(8,128)(2,1)S(1)} %all-to-all-done.q_ref) | copy-start | bytes 3145732
  88.3 13.9 %all-to-all-start.3 = ((bf16[32,32,128]{2,1,0:T(8,128)(2,1)}), bf16[32,32,128]{2,1,0:T(8,128)(2,1)S(1)}, u32[]{:S(2)}, u32[]{:S(2)}) async-start(bf16[32,32,128]{2,1,0:T(8,128)(2,1)} %copy.20), calls=%async_computation.3 | async-start | bytes 524288 | tf_op jit(solution)/shard_map/all_to_all | solution.py:214
  102.2 0.7 copy-start.1

commit v2 on v1

v2 whole, which is shorter than its diff:
```python
import functools
import math

import jax
import jax.numpy as jnp
from jax import lax
from jax.experimental import pallas as pl
from jax.experimental.pallas import tpu as pltpu
from jax.sharding import PartitionSpec as P

ITERS = 10
PAIRS = ((0, 1), (3, 2))
BLOCK = 256
HD = 128
NX = 4
NY = 4
NZ = 8
PER = 4
F32 = jnp.float32
BF = jnp.bfloat16
VMEM = pl.BlockSpec(memory_space=pltpu.VMEM)
SMEM = pl.BlockSpec(memory_space=pltpu.SMEM)


def dot(a, b):
    return lax.dot_general(a, b, (((1,), (0,)), ((), ())), preferred_element_type=F32)


def call(kernel, outs, name, scratch=(), scalars=2, flops=0):
    def run(*args):
        moved = sum(math.prod(s) * d.dtype.itemsize for s, d in ((a.shape, a) for a in args))
        return pl.pallas_call(
            kernel,
            in_specs=[SMEM] * scalars + [VMEM] * (len(args) - scalars),
            out_specs=jax.tree.map(lambda _: VMEM, outs),
            out_shape=outs,
            scratch_shapes=list(scratch),
            cost_estimate=pl.CostEstimate(flops=flops, bytes_accessed=moved, transcendentals=0),
            name=name,
        )(*args)

    return run


def spot(info):
    return info[0] // 2, info[0] % 2, info[1] // NZ, info[1] % NZ


def doc_of(lengths, place):
    doc = jnp.zeros_like(place)
    start = jnp.int32(0)
    for j in range(lengths.shape[0]):
        doc = doc + (place >= start).astype(jnp.int32)
        start = start + lengths[j]
    return doc


def places_of(info, axis):
    x, core, _, _ = spot(info)
    shape = (1, BLOCK) if axis == 1 else (BLOCK, 1)
    entry = lax.broadcasted_iota(jnp.int32, shape, axis)
    half = BLOCK // 2
    base = (info[1] * NX + x) * BLOCK
    return base + jnp.where(entry < half, entry + core * half, entry - core * half)


def diagonals():
    row = lax.broadcasted_iota(jnp.int32, (HD, HD), 0)
    lane = lax.broadcasted_iota(jnp.int32, (HD, HD), 1)
    return row == lane, lane == lax.rem(row + 1, HD)


def rounded(state):
    eye, beside = diagonals()
    whole = state + pltpu.roll(state, HD - 1, 1)
    rest = whole - whole.astype(BF).astype(F32)
    return jnp.where(eye, whole, jnp.where(beside, pltpu.roll(rest, 1, 1), state)).astype(BF)


def started(state):
    _, beside = diagonals()
    return jnp.where(beside, 0.0, state)


def pack_kernel(info, x_ref, kv_own, q_own, kv_other, q_other, stage):
    _, core, _, _ = spot(info)
    rows = x_ref.shape[0]
    for kind in range(3):
        for other in range(2):
            half = core if other == 0 else 1 - core
            first = pl.multiple_of(kind * 32 + half * 16, 16)
            part = x_ref[:, pl.ds(first, 16), :].astype(F32)
            if kind == 1:
                part = (
                    part
                    * lax.rsqrt(jnp.mean(part * part, axis=-1, keepdims=True) + 1e-06)
                    / math.sqrt(HD)
                )
            stage[...] = part.reshape(rows * 16, HD)
            for h in range(16):
                tile = stage[pl.ds(h, rows, stride=16), :].astype(BF)
                if kind == 0:
                    (q_own, q_other)[other][h] = tile
                else:
                    (kv_own, kv_other)[other][kind - 1, h] = tile


def sums_kernel(info, lengths, own, other, out0, out1, out2, out3):
    x, _, _, _ = spot(info)
    place = places_of(info, 1)
    last = (info[1] * NX + x + 1) * BLOCK - 1
    tail = (doc_of(lengths, place) == doc_of(lengths, last)).astype(F32).astype(BF)
    for shift, out in enumerate((out0, out1, out2, out3)):
        for j in range(PER):
            h = lax.rem(x + shift, NX) * PER + j
            k = jnp.concatenate([own[0, h], other[0, h]], axis=0)
            v = jnp.concatenate([own[1, h], other[1, h]], axis=0)
            out[j, 0] = rounded(started(dot(k.T * tail, k)))
            out[j, 1] = dot(v.T * tail, k).astype(BF)


def block_order(info, parts, stage):
    x, _, _, _ = spot(info)
    for shift, part in enumerate(parts):
        stage[lax.rem(x - shift + NX, NX)] = part[...]


def totals_kernel(info, lengths, p0, p1, p2, p3, *rest):
    outs, (stage, ready) = rest[:NZ], rest[NZ:]
    _, _, _, z = spot(info)
    block_order(info, (p0, p1, p2, p3), stage)
    first = info[1] * NX * BLOCK
    docs = [doc_of(lengths, first + (b + 1) * BLOCK - 1) for b in range(NX)]
    for j in range(PER):
        for which in range(2):
            total = jnp.zeros((HD, HD), F32)
            for b in range(NX):
                keep = (docs[b] == docs[NX - 1]).astype(F32)
                total = total + keep * stage[b, j, which].astype(F32)
            ready[2 * j + which] = rounded(total) if which == 0 else total.astype(BF)
    for shift, out in enumerate(outs):
        out[...] = ready[lax.rem(z + shift, NZ)]


def row_order(info, parts, stage):
    _, _, _, z = spot(info)
    for shift, part in enumerate(parts):
        stage[lax.rem(z - shift + NZ, NZ)] = part[...]


def row_docs(info, lengths):
    _, _, y, _ = spot(info)
    width = NX * BLOCK
    return [doc_of(lengths, (y * NZ + place + 1) * width - 1) for place in range(-1, NZ)]


def row_kernel(info, lengths, *rest):
    parts, (out,) = rest[:NZ], rest[NZ : NZ + 1]
    stage = rest[NZ + 1]
    row_order(info, parts, stage)
    docs = row_docs(info, lengths)
    total = jnp.zeros((HD, HD), F32)
    for place in range(NZ):
        keep = (docs[place + 1] == docs[NZ]).astype(F32)
        total = total + keep * stage[place].astype(F32)
    out[...] = total


def entries_kernel(info, lengths, *rest):
    parts, (one, two), outs, (stage, ready) = rest[:NZ], rest[NZ : NZ + 2], rest[NZ + 2 : -2], rest[-2:]
    _, _, y, z = spot(info)
    row_order(info, parts, stage)
    docs = row_docs(info, lengths)
    span = NZ * NX * BLOCK
    through = (doc_of(lengths, (y - 1) * span - 1) == docs[0]).astype(F32)
    carry = one[...] + through * two[...]
    symmetric = z % 2 == 0
    running = carry
    for place in range(NZ):
        ready[place] = jnp.where(symmetric, rounded(running), running.astype(BF))
        same = (docs[place + 1] == docs[place]).astype(F32)
        running = same * running + stage[place].astype(F32)
    for shift, out in enumerate(outs):
        out[...] = ready[lax.rem(z + shift, NZ)]


def states_kernel(info, lengths, p0, p1, p2, p3, *rest):
    parts, outs, (stage, entry, ready) = rest[:NZ], rest[NZ : NZ + NX], rest[NZ + NX :]
    x, _, _, z = spot(info)
    block_order(info, (p0, p1, p2, p3), stage)
    row_order(info, parts, entry)
    first = info[1] * NX * BLOCK
    docs = [doc_of(lengths, first + b * BLOCK - 1) for b in range(NX + 1)]
    for j in range(PER):
        for which in range(2):
            running = entry[2 * j + which].astype(F32)
            for b in range(NX):
                ready[b, j, which] = rounded(running) if which == 0 else running.astype(BF)
                if b < NX - 1:
                    same = (docs[b + 1] == docs[b]).astype(F32)
                    running = same * running + stage[b, j, which].astype(F32)
    for shift, out in enumerate(outs):
        out[...] = ready[lax.rem(x + shift, NX)]


def solve_kernel(
    shifts, info, lengths, reg, kv_own, kv_other, q_own, q_other, s0, s1, out_own, out_other,
    lhs, key_t, same, valid, diagonal, direction, residual, solution, norm,
):
    x, core, _, _ = spot(info)
    before = doc_of(lengths, (info[1] * NX + x) * BLOCK - 1)
    lane = places_of(info, 1)
    row = places_of(info, 0)
    lane_doc = doc_of(lengths, lane)
    valid[...] = (lane_doc == before).astype(F32)
    same[...] = ((doc_of(lengths, row) == lane_doc) & (row <= lane)).astype(F32).astype(BF)
    eye, beside = diagonals()
    count = 2 * PER

    def head(i):
        return lax.rem(x - shifts[i // PER] + NX, NX) * PER + i % PER

    def state(i, which):
        return (s0, s1)[i // PER][i % PER, which]

    for i in range(count):
        h = head(i)
        k = jnp.concatenate([kv_own[0, h], kv_other[0, h]], axis=0)
        keys = state(i, 0).astype(F32)
        mirrored = keys.T
        lhs[i, 0:BLOCK] = k
        lhs[i, BLOCK:] = jnp.where(eye, 0.0, jnp.where(beside, mirrored, keys)).astype(BF)
        key_t[i] = k.T
        middle = jnp.sum(jnp.where(eye | beside, keys, 0.0), axis=1, keepdims=True)
        diagonal[i] = middle * valid[...] + reg[core * 16 + h]
        q = jnp.concatenate([q_own[h], q_other[h]], axis=0).T.astype(F32)
        q = q * lax.rsqrt(jnp.mean(q * q, axis=0, keepdims=True) + 1e-06) / math.sqrt(HD)
        direction[i] = q
        residual[i] = q
        solution[i] = jnp.zeros_like(q)
        norm[i] = jnp.sum(q * q, axis=0, keepdims=True)

    def apply(i):
        full = dot(lhs[i], direction[i].astype(BF))
        return full[BLOCK:], full[0:BLOCK].astype(BF) * same[...]

    def update(i, from_state, score):
        p = direction[i]
        image = from_state * valid[...] + dot(key_t[i], score) + diagonal[i] * p
        old = norm[i]
        step = old / (jnp.sum(p * image, axis=0, keepdims=True) + 1e-06)
        solution[i] = solution[i] + step * p
        r = residual[i] - step * image
        residual[i] = r
        new = jnp.sum(r * r, axis=0, keepdims=True)
        direction[i] = r + (new / (old + 1e-06)) * p
        norm[i] = new

    def iterate(_, carried):
        held = {}
        for i in range(count + 2):
            if i < count:
                held[i] = apply(i)
            if i >= 2:
                update(i - 2, *held.pop(i - 2))
        return carried

    lax.fori_loop(0, ITERS, iterate, 0)
    for i in range(count):
        h = head(i)
        u = solution[i]
        high = u.astype(BF)
        low = (u - high.astype(F32)).astype(BF)
        score = dot(lhs[i, 0:BLOCK], high).astype(BF) * same[...]
        values = state(i, 1)
        from_state = dot(values, high) + dot(values, low)
        v = jnp.concatenate([kv_own[1, h], kv_other[1, h]], axis=0)
        result = (from_state * valid[...] + dot(v.T, score)).T.astype(BF)
        out_own[i] = result[0 : BLOCK // 2]
        out_other[i] = result[BLOCK // 2 :]


def unpack_kernel(info, own0, own1, other0, other1, out_ref, stage):
    x, core, _, _ = spot(info)
    rows = out_ref.shape[0]
    for other in range(2):
        for i in range(16):
            shift = PAIRS[i // 8][i // PER % 2]
            h = lax.rem(x - shift + NX, NX) * PER + i % PER
            part = ((own0, own1), (other0, other1))[other][i // 8]
            stage[pl.ds(h, rows, stride=16), :] = part[i % 8].astype(F32)
        half = core if other == 0 else 1 - core
        first = pl.multiple_of(half * 16, 16)
        out_ref[:, pl.ds(first, 16), :] = stage[...].reshape(rows, 16, HD).astype(BF)


def body(qkv, lengths, reg):
    rows, _, heads, width = qkv.shape
    half = heads // 2
    index = jnp.arange(2, dtype=jnp.int32)
    info = jnp.where(index == 0, lax.axis_index("head"), lax.axis_index("ctx")).astype(jnp.int32)

    def array(shape, dtype=BF):
        return jax.ShapeDtypeStruct(shape, dtype)

    def swap(a):
        return lax.ppermute(a, "head", [(i, i ^ 1) for i in range(2 * NX)])

    def along_x(a, shift):
        return lax.ppermute(
            a, "head", [(i, (i + 2 * shift) % (2 * NX)) for i in range(2 * NX)]
        )

    def along_z(a, shift):
        return lax.ppermute(
            a, "ctx", [(y * NZ + z, y * NZ + (z + shift) % NZ) for y in range(NY) for z in range(NZ)]
        )

    def along_y(a, shift):
        return lax.ppermute(
            a, "ctx", [(y * NZ + z, (y + shift) * NZ + z) for y in range(NY - shift) for z in range(NZ)]
        )

    def spread(parts, move):
        return [parts[0]] + [move(part, shift) for shift, part in enumerate(parts) if shift]

    kv, q = array((2, half, rows, width)), array((half, rows, width))
    kv_own, q_own, kv_send, q_send = call(
        pack_kernel, [kv, q, kv, q], "pack", [pltpu.VMEM((rows * half, width), F32)], scalars=1
    )(info, qkv.reshape(rows, 3 * heads, width))
    kv_other = swap(kv_send)
    q_other = swap(q_send)

    states = array((PER, 2, width, width))
    parts = call(sums_kernel, [states] * NX, "block_sums")(info, lengths, kv_own, kv_other)
    parts = spread(parts, along_x)

    square = array((width, width))
    stage = pltpu.VMEM((NX, PER, 2, width, width), BF)
    squares = pltpu.VMEM((NZ, width, width), BF)
    slices = call(totals_kernel, [square] * NZ, "ctx_totals", [stage, squares])(
        info, lengths, *parts
    )
    slices = spread(slices, along_z)
    (ending,) = call(row_kernel, [array((width, width), F32)], "row_total", [squares])(
        info, lengths, *slices
    )
    carried = [along_y(ending, 1), along_y(ending, 2)]
    entries = call(entries_kernel, [square] * NZ, "entries", [squares, squares])(
        info, lengths, *slices, *carried
    )
    entries = spread(entries, along_z)
    before = call(states_kernel, [states] * NX, "block_states", [stage, squares, stage])(
        info, lengths, *parts, *entries
    )
    before = spread(before, along_x)

    vectors = pltpu.VMEM((2 * PER, width, BLOCK), F32)
    result = array((2 * PER, rows, width))
    own, other = [], []
    for shifts in PAIRS:
        mine, others = call(
            functools.partial(solve_kernel, shifts),
            [result, result],
            "solve",
            [
                pltpu.VMEM((2 * PER, BLOCK + width, width), BF),
                pltpu.VMEM((2 * PER, width, BLOCK), BF),
                pltpu.VMEM((BLOCK, BLOCK), BF),
                pltpu.VMEM((1, BLOCK), F32),
                vectors,
                vectors,
                vectors,
                vectors,
                pltpu.VMEM((2 * PER, 1, BLOCK), F32),
            ],
            scalars=3,
            flops=10**10,
        )(info, lengths, reg, kv_own, kv_other, q_own, q_other, before[shifts[0]], before[shifts[1]])
        own.append(mine)
        other.append(swap(others))
    return call(
        unpack_kernel,
        array((rows, heads, width)),
        "unpack",
        [pltpu.VMEM((rows * half, width), F32)],
        scalars=1,
    )(info, *own, *other)


def solution(mesh):
    in_specs = (P(("ctx", "head"), None, None, None), P(), P())
    out_specs = P(("ctx", "head"), None, None)
    return jax.shard_map(body, mesh=mesh, in_specs=in_specs, out_specs=out_specs, check_vma=False)
```

time: 171 us -> 145 us (0.85)
  blocking collectives: 42.1 us -> 0 us
  starting transfers between devices: 18.2 us -> 53 us
  waiting for transfers between devices: 48.2 us -> 25.2 us
  Pallas kernels: 47.9 us -> 59.1 us
  local copies, waits for them, and re-layouts: 11 us -> 6.36 us
  other arithmetic: 2.5 us -> 0.58 us
    ppermute x0 -> x26, starting transfers between devices: none -> 53 us  [the longest x14 26.6 us: along_z(): lax.ppermute(a, 'ctx', [(y * NZ + z, y * NZ + (z + shift) % NZ) for y in...]
    all_to_all x3 -> x0, waiting for transfers between devices: 48.2 us -> none  [the longest x1 25.5 us: body(): key_value = lax.all_to_all(key_value, 'head', 0, 0, tiled=True)]
    all_to_all x2 -> x0, blocking collectives: 42.1 us -> none  [the longest x1 22.1 us: body(): mixed = lax.all_to_all(mixed, 'head', 0, 0, tiled=True)]
    ppermute x0 -> x26, waiting for transfers between devices: none -> 25.2 us  [the longest x6 13.4 us: along_x(): lax.ppermute(a, 'head', [(i, (i + 2 * shift) % (2 * NX)) for i in range(2...]
    all_to_all x3 -> x0, starting transfers between devices: 18.2 us -> none  [the longest x1 7.13 us: body(): query = lax.all_to_all(query, 'head', 0, 0, tiled=True)]
    pallas_call x2 -> x9, Pallas kernels: 47.9 us -> 59.1 us  [run(): pl.pallas_call(kernel, in_specs=[SMEM] * scalars + [VMEM] * (len(args) -...]
    unnamed x9 -> x52, local copies, waits for them, and re-layouts: 3.8 us -> 6.36 us
  transfers between devices with their start and end apart: 3 -> 26, of which waited for: 3 -> 11; matrix products, arithmetic and copies ran while one was open for 2% -> 0% of each run, Pallas kernels for 0% -> 31%
where the time goes in v2:
time: 145 us; the launch traced here: 144 us
  Pallas kernels  59.1 us (41%)
  starting transfers between devices  53 us (37%)
  waiting for transfers between devices  25.2 us (17%)
  local copies, waits for them, and re-layouts  6.36 us (4%)
    pallas_call x9, Pallas kernels, run(): pl.pallas_call(kernel, in_specs=[SMEM] * scalars + [VMEM] * (len(args) -...  59.1 us
    ppermute x14, starting transfers between devices, along_z(): lax.ppermute(a, 'ctx', [(y * NZ + z, y * NZ + (z + shift) % NZ) for y in...  26.6 us
    ppermute x6, waiting for transfers between devices, along_x(): lax.ppermute(a, 'head', [(i, (i + 2 * shift) % (2 * NX)) for i in range(2...  13.4 us
    ppermute x4, starting transfers between devices, swap(): return lax.ppermute(a, 'head', [(i, i ^ 1) for i in range(2 * NX)])  12 us
    ppermute x6, starting transfers between devices, along_x(): lax.ppermute(a, 'head', [(i, (i + 2 * shift) % (2 * NX)) for i in range(2...  7.36 us
    ppermute x2, starting transfers between devices, along_y(): lax.ppermute(a, 'ctx', [(y * NZ + z, (y + shift) * NZ + z) for y in range...  7.11 us
    unnamed x52, local copies, waits for them, and re-layouts  6.36 us
    ppermute x14, waiting for transfers between devices, along_z(): lax.ppermute(a, 'ctx', [(y * NZ + z, y * NZ + (z + shift) % NZ) for y in...  5.96 us
  transfers between devices with their start and end apart: 26, of which 11 were waited for; matrix products, arithmetic and copies ran while one was open for 0% of the time, Pallas kernels for 31%

profile of v2, /device:TPU:1, one launch (start us, length us, event | category | flops | bytes accessed | tf_op | source)
XLA Modules:
  0.0 144.4 jit_solution(16653783382786345487)
XLA Ops:
  0.6 6.7 %pack.1 = (bf16[2,16,128,128]{3,2,1,0:T(8,128)(2,1)}, bf16[16,128,128]{2,1,0:T(8,128)(2,1)}, bf16[2,16,128,128]{3,2,1,0:T(8,128)(2,1)}, bf16[16,128,128]{2,1,0:T(8,128)(2,1)}) custom-call(s32[2]{0:T(128)} %compare_select_fusion.info, bf16[128,96,128]{2,1,0:T(8,128)(2,1)} %bitcast.1), custom_call_target="tpu_custom_call" | custom-call | bytes 3145736 | tf_op jit(solution)/shard_map/pack/pallas_call | solution.py:32
  7.3 3.2 %collective-permute-start = (bf16[2,16,128,128]{3,2,1,0:T(8,128)(2,1)}, bf16[2,16,128,128]{3,2,1,0:T(8,128)(2,1)S(1)}, u32[]{:S(2)}, u32[]{:S(2)}) collective-permute-start(bf16[2,16,128,128]{3,2,1,0:T(8,128)(2,1)} %get-tuple-element.38), channel_id=1, source_target_pairs={{0,1},{1,0},{2,3},{3,2},{4,5},{5,4},{6,7},{7,6},{8,9},{9,8},{10,11... | collective-permute-start | bytes 3145736 | tf_op jit(solution)/shard_map/ppermute | solution.py:307
  10.5 2.5 %collective-permute-done.other.kv_other = bf16[2,16,128,128]{3,2,1,0:T(8,128)(2,1)S(1)} collective-permute-done((bf16[2,16,128,128]{3,2,1,0:T(8,128)(2,1)}, bf16[2,16,128,128]{3,2,1,0:T(8,128)(2,1)S(1)}, u32[]{:S(2)}, u32[]{:S(2)}) %collective-permute-start) | collective-permute-done | bytes 1048608 | tf_op jit(solution)/shard_map/ppermute | solution.py:307
  14.0 5.2 %block_sums.1 = (bf16[4,2,128,128]{3,2,1,0:T(8,128)(2,1)}, bf16[4,2,128,128]{3,2,1,0:T(8,128)(2,1)}, bf16[4,2,128,128]{3,2,1,0:T(8,128)(2,1)}, bf16[4,2,128,128]{3,2,1,0:T(8,128)(2,1)}) custom-call(s32[2]{0:T(128)} %compare_select_fusion.info, s32[8]{0:T(128)} %lengths.13, bf16[2,16,128,128]{3,2,1,0:T(8,128)(2,1)} %get-tuple-element.37.own.kv_own, ...), custom_call_target="tpu_custom_call" | custom-call | bytes 2097192 | tf_op jit(solution)/shard_map/block_sums/pallas_call | solution.py:32
  23.5 5.3 %collective-permute-done.2.p1 = bf16[4,2,128,128]{3,2,1,0:T(8,128)(2,1)S(1)} collective-permute-done((bf16[4,2,128,128]{3,2,1,0:T(8,128)(2,1)}, bf16[4,2,128,128]{3,2,1,0:T(8,128)(2,1)S(1)}, u32[]{:S(2)}, u32[]{:S(2)}) %collective-permute-start.2) | collective-permute-done | bytes 262176 | tf_op jit(solution)/shard_map/ppermute | solution.py:310
  28.8 4.2 %collective-permute-done.3.p2 = bf16[4,2,128,128]{3,2,1,0:T(8,128)(2,1)S(1)} collective-permute-done((bf16[4,2,128,128]{3,2,1,0:T(8,128)(2,1)}, bf16[4,2,128,128]{3,2,1,0:T(8,128)(2,1)S(1)}, u32[]{:S(2)}, u32[]{:S(2)}) %collective-permute-start.3) | collective-permute-done | bytes 262176 | tf_op jit(solution)/shard_map/ppermute | solution.py:310
  34.8 2.3 %ctx_totals.1 = (bf16[128,128]{1,0:T(8,128)(2,1)}, bf16[128,128]{1,0:T(8,128)(2,1)}, bf16[128,128]{1,0:T(8,128)(2,1)}, bf16[128,128]{1,0:T(8,128)(2,1)}, bf16[12...) custom-call(s32[2]{0:T(128)} %compare_select_fusion.info, ...), custom_call_target="tpu_custom_call" | custom-call | bytes 1048616 | tf_op jit(solution)/shard_map/ctx_totals/pallas_call | solution.py:32
  37.8 3.0 %collective-permute-start.6 = (bf16[128,128]{1,0:T(8,128)(2,1)}, bf16[128,128]{1,0:T(8,128)(2,1)S(1)}, u32[]{:S(2)}, u32[]{:S(2)}) collective-permute-start(bf16[128,128]{1,0:T(8,128)(2,1)} %get-tuple-element.47), channel_id=1, source_target_pairs={{0,16},{8,24},{16,32},{24,40},{32,48},{40,56},{48,0},{56,8},{64,80... | collective-permute-start | bytes 98312 | tf_op jit(solution)/shard_map/ppermute | solution.py:315
  40.8 3.8 %collective-permute-start.7 = (bf16[128,128]{1,0:T(8,128)(2,1)}, bf16[128,128]{1,0:T(8,128)(2,1)S(1)}, u32[]{:S(2)}, u32[]{:S(2)}) collective-permute-start(bf16[128,128]{1,0:T(8,128)(2,1)} %get-tuple-element.48), channel_id=1, source_target_pairs={{0,24},{8,32},{16,40},{24,48},{32,56},{40,0},{48,8},{56,16},{64,88... | collective-permute-start | bytes 98312 | tf_op jit(solution)/shard_map/ppermute | solution.py:315
  45.0 4.5 %collective-permute-start.9 = (bf16[128,128]{1,0:T(8,128)(2,1)}, bf16[128,128]{1,0:T(8,128)(2,1)S(1)}, u32[]{:S(2)}, u32[]{:S(2)}) collective-permute-start(bf16[128,128]{1,0:T(8,128)(2,1)} %get-tuple-element.50), channel_id=1, source_target_pairs={{0,40},{8,48},{16,56},{24,0},{32,8},{40,16},{48,24},{56,32},{64,10... | collective-permute-start | bytes 98312 | tf_op jit(solution)/shard_map/ppermute | solution.py:315
  49.5 2.4 %collective-permute-start.10 = (bf16[128,128]{1,0:T(8,128)(2,1)}, bf16[128,128]{1,0:T(8,128)(2,1)S(1)}, u32[]{:S(2)}, u32[]{:S(2)}) collective-permute-start(bf16[128,128]{1,0:T(8,128)(2,1)} %get-tuple-element.51), channel_id=1, source_target_pairs={{0,48},{8,56},{16,0},{24,8},{32,16},{40,24},{48,32},{56,40},{64,11... | collective-permute-start | bytes 98312 | tf_op jit(solution)/shard_map/ppermute | solution.py:315
  52.7 2.2 %collective-permute-done.10.rest_6_ = bf16[128,128]{1,0:T(8,128)(2,1)S(1)} collective-permute-done((bf16[128,128]{1,0:T(8,128)(2,1)}, bf16[128,128]{1,0:T(8,128)(2,1)S(1)}, u32[]{:S(2)}, u32[]{:S(2)}) %collective-permute-start.10) | collective-permute-done | bytes 32800 | tf_op jit(solution)/shard_map/ppermute | solution.py:315
  57.6 4.8 %collective-permute-start.13 = (f32[128,128]{1,0:T(8,128)}, f32[128,128]{1,0:T(8,128)S(1)}, u32[]{:S(2)}, u32[]{:S(2)}) collective-permute-start(f32[128,128]{1,0:T(8,128)} %row_total.1), channel_id=1, source_target_pairs={{0,128},{8,136},{16,144},{24,152},{32,160},{40,168},{48,176},{56,1... | collective-permute-start | bytes 196616 | tf_op jit(solution)/shard_map/ppermute | solution.py:320
  62.4 2.3 %collective-permute-start.12 = (f32[128,128]{1,0:T(8,128)}, f32[128,128]{1,0:T(8,128)S(1)}, u32[]{:S(2)}, u32[]{:S(2)}) collective-permute-start(f32[128,128]{1,0:T(8,128)} %row_total.1), channel_id=1, source_target_pairs={{0,64},{8,72},{16,80},{24,88},{32,96},{40,104},{48,112},{56,120},{... | collective-permute-start | bytes 196616 | tf_op jit(solution)/shard_map/ppermute | solution.py:320
  67.0 2.3 %entries.1 = (bf16[128,128]{1,0:T(8,128)(2,1)}, bf16[128,128]{1,0:T(8,128)(2,1)}, bf16[128,128]{1,0:T(8,128)(2,1)}, bf16[128,128]{1,0:T(8,128)(2,1)}, bf16[128,1...) custom-call(s32[2]{0:T(128)} %compare_select_fusion.info, ...), custom_call_target="tpu_custom_call" | custom-call | bytes 393256 | tf_op jit(solution)/shard_map/entries/pallas_call | solution.py:32
  71.1 3.3 %collective-permute-start.16 = (bf16[128,128]{1,0:T(8,128)(2,1)}, bf16[128,128]{1,0:T(8,128)(2,1)S(1)}, u32[]{:S(2)}, u32[]{:S(2)}) collective-permute-start(bf16[128,128]{1,0:T(8,128)(2,1)} %get-tuple-element.56), channel_id=1, source_target_pairs={{0,24},{8,32},{16,40},{24,48},{32,56},{40,0},{48,8},{56,16},{64,88... | collective-permute-start | bytes 98312 | tf_op jit(solution)/shard_map/ppermute | solution.py:315
  75.4 4.1 %collective-permute-start.18 = (bf16[128,128]{1,0:T(8,128)(2,1)}, bf16[128,128]{1,0:T(8,128)(2,1)S(1)}, u32[]{:S(2)}, u32[]{:S(2)}) collective-permute-start(bf16[128,128]{1,0:T(8,128)(2,1)} %get-tuple-element.58), channel_id=1, source_target_pairs={{0,40},{8,48},{16,56},{24,0},{32,8},{40,16},{48,24},{56,32},{64,10... | collective-permute-start | bytes 98312 | tf_op jit(solution)/shard_map/ppermute | solution.py:315
  84.3 3.6 %block_states.1 = (bf16[4,2,128,128]{3,2,1,0:T(8,128)(2,1)}, bf16[4,2,128,128]{3,2,1,0:T(8,128)(2,1)}, bf16[4,2,128,128]{3,2,1,0:T(8,128)(2,1)}, bf16[4,2,128,128]{3,2,1,0:T(8,128)(2,1)}) custom-call(s32[2]{0:T(128)} %compare_select_fusion.info, s32[8]{0:T(128)} %lengths.13, bf16[4,2,128,128]{3,2,1,0:T(8,128)(2,1)} %get-tuple-element.41.p0, ...), custom_call_target="tpu_custom_call" | custom-call | bytes 1310760 | tf_op jit(solution)/shard_map/block_states/pallas_call | solution.py:32
  89.1 2.0 %collective-permute-start.22 = (bf16[4,2,128,128]{3,2,1,0:T(8,128)(2,1)}, bf16[4,2,128,128]{3,2,1,0:T(8,128)(2,1)S(1)}, u32[]{:S(2)}, u32[]{:S(2)}) collective-permute-start(bf16[4,2,128,128]{3,2,1,0:T(8,128)(2,1)} %get-tuple-element.64), channel_id=1, source_target_pairs={{0,6},{1,7},{2,0},{3,1},{4,2},{5,3},{6,4},{7,5},{8,14},{9,15},{10,... | collective-permute-start | bytes 786440 | tf_op jit(solution)/shard_map/ppermute | solution.py:310
  92.2 2.8 %collective-permute-done.21.s1 = bf16[4,2,128,128]{3,2,1,0:T(8,128)(2,1)S(1)} collective-permute-done((bf16[4,2,128,128]{3,2,1,0:T(8,128)(2,1)}, bf16[4,2,128,128]{3,2,1,0:T(8,128)(2,1)S(1)}, u32[]{:S(2)}, u32[]{:S(2)}) %collective-permute-start.21) | collective-permute-done | bytes 262176 | tf_op jit(solution)/shard_map/ppermute | solution.py:310
  95.7 17.2 %solve.2 = (bf16[8,128,128]{2,1,0:T(8,128)(2,1)}, bf16[8,128,128]{2,1,0:T(8,128)(2,1)}) custom-call(s32[2]{0:T(128)} %compare_select_fusion.info, s32[8]{0:T(128)} %lengths.13, f32[32]{0:T(128)} %reg.3, bf16[2,16,128,128]{3,2,1,0:T(8,128)(2,1)} %get-tuple-element.37.own.kv_own, bf16[2,16,128,128]{3,2,1,0:T(8,128)(2,1)} %copy-done.3, ...), custom_call_target="tpu_custom_call" | custom-call | flops 10000000000 | bytes 3670184 | tf_op jit(solution)/shard_map/solve/pallas_call | solution.py:32
  112.8 7.6 %collective-permute-start.24 = (bf16[8,128,128]{2,1,0:T(8,128)(2,1)}, bf16[8,128,128]{2,1,0:T(8,128)(2,1)S(1)}, u32[]{:S(2)}, u32[]{:S(2)}) collective-permute-start(bf16[8,128,128]{2,1,0:T(8,128)(2,1)} %get-tuple-element.67), channel_id=1, source_target_pairs={{0,1},{1,0},{2,3},{3,2},{4,5},{5,4},{6,7},{7,6},{8,9},{9,8},{10,11... | collective-permute-start | bytes 786440 | tf_op jit(solution)/shard_map/ppermute | solution.py:307
  121.8 17.1 %solve.3 = (bf16[8,128,128]{2,1,0:T(8,128)(2,1)}, bf16[8,128,128]{2,1,0:T(8,128)(2,1)}) custom-call(s32[2]{0:T(128)} %compare_select_fusion.info, s32[8]{0:T(128)} %lengths.13, f32[32]{0:T(128)} %reg.3, bf16[2,16,128,128]{3,2,1,0:T(8,128)(2,1)} %get-tuple-element.37.own.kv_own, bf16[2,16,128,128]{3,2,1,0:T(8,128)(2,1)} %copy-done.3, ...), custom_call_target="tpu_custom_call" | custom-call | flops 10000000000 | bytes 3670184 | tf_op jit(solution)/shard_map/solve/pallas_call | solution.py:32
  141.4 3.0 %unpack.1 = bf16[128,32,128]{2,1,0:T(8,128)(2,1)} custom-call(s32[2]{0:T(128)} %compare_select_fusion.info, bf16[8,128,128]{2,1,0:T(8,128)(2,1)} %get-tuple-element.63.own0, bf16[8,128,128]{2,1,0:T(8,128)(2,1)} %get-tuple-element.66.own1, bf16[8,128,128]{2,1,0:T(8,128)(2,1)} %copy-done.4, bf16[8,128,128]{2,1,0:T(8,128)(2,1)} %copy-done.5), custom_call_target="tpu_custom_call" | custom-call | bytes 1048584 | tf_op jit(solution)/shard_map/unpack/pallas_call | solution.py:32
  (90 shorter events, 28.9 us)
Async XLA Ops:
  7.3 5.7 %collective-permute-start = (bf16[2,16,128,128]{3,2,1,0:T(8,128)(2,1)}, bf16[2,16,128,128]{3,2,1,0:T(8,128)(2,1)S(1)}, u32[]{:S(2)}, u32[]{:S(2)}) collective-permute-start(bf16[2,16,128,128]{3,2,1,0:T(8,128)(2,1)} %get-tuple-element.38), channel_id=1, source_target_pairs={{0,1},{1,0},{2,3},{3,2},{4,5},{5,4},{6,7},{7,6},{8,9},{9,8},{10,11... | collective-permute-start | bytes 3145736 | tf_op jit(solution)/shard_map/ppermute | solution.py:307
  19.2 9.6 %collective-permute-start.2 = (bf16[4,2,128,128]{3,2,1,0:T(8,128)(2,1)}, bf16[4,2,128,128]{3,2,1,0:T(8,128)(2,1)S(1)}, u32[]{:S(2)}, u32[]{:S(2)}) collective-permute-start(bf16[4,2,128,128]{3,2,1,0:T(8,128)(2,1)} %get-tuple-element.42), channel_id=1, source_target_pairs={{0,2},{1,3},{2,4},{3,5},{4,6},{5,7},{6,0},{7,1},{8,10},{9,11},{10,... | collective-permute-start | bytes 786440 | tf_op jit(solution)/shard_map/ppermute | solution.py:310
  19.2 13.8 %collective-permute-start.3 = (bf16[4,2,128,128]{3,2,1,0:T(8,128)(2,1)}, bf16[4,2,128,128]{3,2,1,0:T(8,128)(2,1)S(1)}, u32[]{:S(2)}, u32[]{:S(2)}) collective-permute-start(bf16[4,2,128,128]{3,2,1,0:T(8,128)(2,1)} %get-tuple-element.43), channel_id=1, source_target_pairs={{0,4},{1,5},{2,6},{3,7},{4,0},{5,1},{6,2},{7,3},{8,12},{9,13},{10,... | collective-permute-start | bytes 786440 | tf_op jit(solution)/shard_map/ppermute | solution.py:310
  21.1 13.0 %collective-permute-start.4 = (bf16[4,2,128,128]{3,2,1,0:T(8,128)(2,1)}, bf16[4,2,128,128]{3,2,1,0:T(8,128)(2,1)S(1)}, u32[]{:S(2)}, u32[]{:S(2)}) collective-permute-start(bf16[4,2,128,128]{3,2,1,0:T(8,128)(2,1)} %get-tuple-element.44), channel_id=1, source_target_pairs={{0,6},{1,7},{2,0},{3,1},{4,2},{5,3},{6,4},{7,5},{8,14},{9,15},{10,... | collective-permute-start | bytes 786440 | tf_op jit(solution)/shard_map/ppermute | solution.py:310
  22.3 69.9 %collective-permute-start.1 = (bf16[16,128,128]{2,1,0:T(8,128)(2,1)}, bf16[16,128,128]{2,1,0:T(8,128)(2,1)S(1)}, u32[]{:S(2)}, u32[]{:S(2)}) collective-permute-start(bf16[16,128,128]{2,1,0:T(8,128)(2,1)} %get-tuple-element.40), channel_id=1, source_target_pairs={{0,1},{1,0},{2,3},{3,2},{4,5},{5,4},{6,7},{7,6},{8,9},{9,8},{10,11... | collective-permute-start | bytes 1572872 | tf_op jit(solution)/shard_map/ppermute | solution.py:307
  37.2 7.9 %collective-permute-start.5 = (bf16[128,128]{1,0:T(8,128)(2,1)}, bf16[128,128]{1,0:T(8,128)(2,1)S(1)}, u32[]{:S(2)}, u32[]{:S(2)}) collective-permute-start(bf16[128,128]{1,0:T(8,128)(2,1)} %get-tuple-element.46), channel_id=1, source_target_pairs={{0,8},{8,16},{16,24},{24,32},{32,40},{40,48},{48,56},{56,0},{64,72... | collective-permute-start | bytes 98312 | tf_op jit(solution)/shard_map/ppermute | solution.py:315
  37.8 11.7 %collective-permute-start.6 = (bf16[128,128]{1,0:T(8,128)(2,1)}, bf16[128,128]{1,0:T(8,128)(2,1)S(1)}, u32[]{:S(2)}, u32[]{:S(2)}) collective-permute-start(bf16[128,128]{1,0:T(8,128)(2,1)} %get-tuple-element.47), channel_id=1, source_target_pairs={{0,16},{8,24},{16,32},{24,40},{32,48},{40,56},{48,0},{56,8},{64,80... | collective-permute-start | bytes 98312 | tf_op jit(solution)/shard_map/ppermute | solution.py:315
  40.8 11.1 %collective-permute-start.7 = (bf16[128,128]{1,0:T(8,128)(2,1)}, bf16[128,128]{1,0:T(8,128)(2,1)S(1)}, u32[]{:S(2)}, u32[]{:S(2)}) collective-permute-start(bf16[128,128]{1,0:T(8,128)(2,1)} %get-tuple-element.48), channel_id=1, source_target_pairs={{0,24},{8,32},{16,40},{24,48},{32,56},{40,0},{48,8},{56,16},{64,88... | collective-permute-start | bytes 98312 | tf_op jit(solution)/shard_map/ppermute | solution.py:315
  44.6 8.1 %collective-permute-start.8 = (bf16[128,128]{1,0:T(8,128)(2,1)}, bf16[128,128]{1,0:T(8,128)(2,1)S(1)}, u32[]{:S(2)}, u32[]{:S(2)}) collective-permute-start(bf16[128,128]{1,0:T(8,128)(2,1)} %get-tuple-element.49), channel_id=1, source_target_pairs={{0,32},{8,40},{16,48},{24,56},{32,0},{40,8},{48,16},{56,24},{64,96... | collective-permute-start | bytes 98312 | tf_op jit(solution)/shard_map/ppermute | solution.py:315
  45.0 7.6 %collective-permute-start.9 = (bf16[128,128]{1,0:T(8,128)(2,1)}, bf16[128,128]{1,0:T(8,128)(2,1)S(1)}, u32[]{:S(2)}, u32[]{:S(2)}) collective-permute-start(bf16[128,128]{1,0:T(8,128)(2,1)} %get-tuple-element.50), channel_id=1, source_target_pairs={{0,40},{8,48},{16,56},{24,0},{32,8},{40,16},{48,24},{56,32},{64,10... | collective-permute-start | bytes 98312 | tf_op jit(solution)/shard_map/ppermute | solution.py:315
  49.5 5.3 %collective-permute-start.10 = (bf16[128,128]{1,0:T(8,128)(2,1)}, bf16[128,128]{1,0:T(8,128)(2,1)S(1)}, u32[]{:S(2)}, u32[]{:S(2)}) collective-permute-start(bf16[128,128]{1,0:T(8,128)(2,1)} %get-tuple-element.51), channel_id=1, source_target_pairs={{0,48},{8,56},{16,0},{24,8},{32,16},{40,24},{48,32},{56,40},{64,11... | collective-permute-start | bytes 98312 | tf_op jit(solution)/shard_map/ppermute | solution.py:315
  57.6 7.1 %collective-permute-start.13 = (f32[128,128]{1,0:T(8,128)}, f32[128,128]{1,0:T(8,128)S(1)}, u32[]{:S(2)}, u32[]{:S(2)}) collective-permute-start(f32[128,128]{1,0:T(8,128)} %row_total.1), channel_id=1, source_target_pairs={{0,128},{8,136},{16,144},{24,152},{32,160},{40,168},{48,176},{56,1... | collective-permute-start | bytes 196616 | tf_op jit(solution)/shard_map/ppermute | solution.py:320
  62.4 3.9 %collective-permute-start.12 = (f32[128,128]{1,0:T(8,128)}, f32[128,128]{1,0:T(8,128)S(1)}, u32[]{:S(2)}, u32[]{:S(2)}) collective-permute-start(f32[128,128]{1,0:T(8,128)} %row_total.1), channel_id=1, source_target_pairs={{0,64},{8,72},{16,80},{24,88},{32,96},{40,104},{48,112},{56,120},{... | collective-permute-start | bytes 196616 | tf_op jit(solution)/shard_map/ppermute | solution.py:320
  69.3 6.1 %collective-permute-start.14 = (bf16[128,128]{1,0:T(8,128)(2,1)}, bf16[128,128]{1,0:T(8,128)(2,1)S(1)}, u32[]{:S(2)}, u32[]{:S(2)}) collective-permute-start(bf16[128,128]{1,0:T(8,128)(2,1)} %get-tuple-element.54), channel_id=1, source_target_pairs={{0,8},{8,16},{16,24},{24,32},{32,40},{40,48},{48,56},{56,0},{64,72... | collective-permute-start | bytes 98312 | tf_op jit(solution)/shard_map/ppermute | solution.py:315
  69.9 9.6 %collective-permute-start.15 = (bf16[128,128]{1,0:T(8,128)(2,1)}, bf16[128,128]{1,0:T(8,128)(2,1)S(1)}, u32[]{:S(2)}, u32[]{:S(2)}) collective-permute-start(bf16[128,128]{1,0:T(8,128)(2,1)} %get-tuple-element.55), channel_id=1, source_target_pairs={{0,16},{8,24},{16,32},{24,40},{32,48},{40,56},{48,0},{56,8},{64,80... | collective-permute-start | bytes 98312 | tf_op jit(solution)/shard_map/ppermute | solution.py:315
  71.1 8.8 %collective-permute-start.16 = (bf16[128,128]{1,0:T(8,128)(2,1)}, bf16[128,128]{1,0:T(8,128)(2,1)S(1)}, u32[]{:S(2)}, u32[]{:S(2)}) collective-permute-start(bf16[128,128]{1,0:T(8,128)(2,1)} %get-tuple-element.56), channel_id=1, source_target_pairs={{0,24},{8,32},{16,40},{24,48},{32,56},{40,0},{48,8},{56,16},{64,88... | collective-permute-start | bytes 98312 | tf_op jit(solution)/shard_map/ppermute | solution.py:315
  74.5 7.5 %collective-permute-start.17 = (bf16[128,128]{1,0:T(8,128)(2,1)}, bf16[128,128]{1,0:T(8,128)(2,1)S(1)}, u32[]{:S(2)}, u32[]{:S(2)}) collective-permute-start(bf16[128,128]{1,0:T(8,128)(2,1)} %get-tuple-element.57), channel_id=1, source_target_pairs={{0,32},{8,40},{16,48},{24,56},{32,0},{40,8},{48,16},{56,24},{64,96... | collective-permute-start | bytes 98312 | tf_op jit(solution)/shard_map/ppermute | solution.py:315
  75.4 6.6 %collective-permute-start.18 = (bf16[128,128]{1,0:T(8,128)(2,1)}, bf16[128,128]{1,0:T(8,128)(2,1)S(1)}, u32[]{:S(2)}, u32[]{:S(2)}) collective-permute-start(bf16[128,128]{1,0:T(8,128)(2,1)} %get-tuple-element.58), channel_id=1, source_target_pairs={{0,40},{8,48},{16,56},{24,0},{32,8},{40,16},{48,24},{56,32},{64,10... | collective-permute-start | bytes 98312 | tf_op jit(solution)/shard_map/ppermute | solution.py:315
  79.5 4.2 %collective-permute-start.19 = (bf16[128,128]{1,0:T(8,128)(2,1)}, bf16[128,128]{1,0:T(8,128)(2,1)S(1)}, u32[]{:S(2)}, u32[]{:S(2)}) collective-permute-start(bf16[128,128]{1,0:T(8,128)(2,1)} %get-tuple-element.59), channel_id=1, source_target_pairs={{0,48},{8,56},{16,0},{24,8},{32,16},{40,24},{48,32},{56,40},{64,11... | collective-permute-start | bytes 98312 | tf_op jit(solution)/shard_map/ppermute | solution.py:315
  79.9 3.8 %collective-permute-start.20 = (bf16[128,128]{1,0:T(8,128)(2,1)}, bf16[128,128]{1,0:T(8,128)(2,1)S(1)}, u32[]{:S(2)}, u32[]{:S(2)}) collective-permute-start(bf16[128,128]{1,0:T(8,128)(2,1)} %get-tuple-element.60), channel_id=1, source_target_pairs={{0,56},{8,0},{16,8},{24,16},{32,24},{40,32},{48,40},{56,48},{64,12... | collective-permute-start | bytes 98312 | tf_op jit(solution)/shard_map/ppermute | solution.py:315
  87.9 7.0 %collective-permute-start.21 = (bf16[4,2,128,128]{3,2,1,0:T(8,128)(2,1)}, bf16[4,2,128,128]{3,2,1,0:T(8,128)(2,1)S(1)}, u32[]{:S(2)}, u32[]{:S(2)}) collective-permute-start(bf16[4,2,128,128]{3,2,1,0:T(8,128)(2,1)} %get-tuple-element.62), channel_id=1, source_target_pairs={{0,2},{1,3},{2,4},{3,5},{4,6},{5,7},{6,0},{7,1},{8,10},{9,11},{10,... | collective-permute-start | bytes 786440 | tf_op jit(solution)/shard_map/ppermute | solution.py:310
  89.1 31.3 %collective-permute-start.22 = (bf16[4,2,128,128]{3,2,1,0:T(8,128)(2,1)}, bf16[4,2,128,128]{3,2,1,0:T(8,128)(2,1)S(1)}, u32[]{:S(2)}, u32[]{:S(2)}) collective-permute-start(bf16[4,2,128,128]{3,2,1,0:T(8,128)(2,1)} %get-tuple-element.64), channel_id=1, source_target_pairs={{0,6},{1,7},{2,0},{3,1},{4,2},{5,3},{6,4},{7,5},{8,14},{9,15},{10,... | collective-permute-start | bytes 786440 | tf_op jit(solution)/shard_map/ppermute | solution.py:310
  91.1 29.4 %collective-permute-start.23 = (bf16[4,2,128,128]{3,2,1,0:T(8,128)(2,1)}, bf16[4,2,128,128]{3,2,1,0:T(8,128)(2,1)S(1)}, u32[]{:S(2)}, u32[]{:S(2)}) collective-permute-start(bf16[4,2,128,128]{3,2,1,0:T(8,128)(2,1)} %get-tuple-element.65), channel_id=1, source_target_pairs={{0,4},{1,5},{2,6},{3,7},{4,0},{5,1},{6,2},{7,3},{8,12},{9,13},{10,... | collective-permute-start | bytes 786440 | tf_op jit(solution)/shard_map/ppermute | solution.py:310
  112.8 26.1 %collective-permute-start.24 = (bf16[8,128,128]{2,1,0:T(8,128)(2,1)}, bf16[8,128,128]{2,1,0:T(8,128)(2,1)S(1)}, u32[]{:S(2)}, u32[]{:S(2)}) collective-permute-start(bf16[8,128,128]{2,1,0:T(8,128)(2,1)} %get-tuple-element.67), channel_id=1, source_target_pairs={{0,1},{1,0},{2,3},{3,2},{4,5},{5,4},{6,7},{7,6},{8,9},{9,8},{10,11... | collective-permute-start | bytes 786440 | tf_op jit(solution)/shard_map/ppermute | solution.py:307
  (28 other events, 70.0 us)

commit v3 on v2

v3 whole, which is shorter than its diff:
```python
import functools
import math

import jax
import jax.numpy as jnp
from jax import lax
from jax.experimental import pallas as pl
from jax.experimental.pallas import tpu as pltpu
from jax.sharding import PartitionSpec as P

ITERS = 10
GROUPS = ((0,), (1, 3), (2,))
BLOCK = 256
HD = 128
NX = 4
NY = 4
NZ = 8
PER = 4
F32 = jnp.float32
BF = jnp.bfloat16
VMEM = pl.BlockSpec(memory_space=pltpu.VMEM)
SMEM = pl.BlockSpec(memory_space=pltpu.SMEM)


def dot(a, b):
    return lax.dot_general(a, b, (((1,), (0,)), ((), ())), preferred_element_type=F32)


def call(kernel, outs, name, scratch=(), scalars=2, flops=0, limit=16):
    def run(*args):
        moved = sum(math.prod(s) * d.dtype.itemsize for s, d in ((a.shape, a) for a in args))
        return pl.pallas_call(
            kernel,
            in_specs=[SMEM] * scalars + [VMEM] * (len(args) - scalars),
            out_specs=jax.tree.map(lambda _: VMEM, outs),
            out_shape=outs,
            scratch_shapes=list(scratch),
            cost_estimate=pl.CostEstimate(flops=flops, bytes_accessed=moved, transcendentals=0),
            compiler_params=pltpu.CompilerParams(vmem_limit_bytes=limit << 20),
            name=name,
        )(*args)

    return run


def spot(info):
    return info[0] // 2, info[0] % 2, info[1] // NZ, info[1] % NZ


def doc_of(lengths, place):
    doc = jnp.zeros_like(place)
    start = jnp.int32(0)
    for j in range(lengths.shape[0]):
        doc = doc + (place >= start).astype(jnp.int32)
        start = start + lengths[j]
    return doc


def places_of(info, axis):
    x, core, _, _ = spot(info)
    shape = (1, BLOCK) if axis == 1 else (BLOCK, 1)
    entry = lax.broadcasted_iota(jnp.int32, shape, axis)
    half = BLOCK // 2
    base = (info[1] * NX + x) * BLOCK
    return base + jnp.where(entry < half, entry + core * half, entry - core * half)


def diagonals():
    row = lax.broadcasted_iota(jnp.int32, (HD, HD), 0)
    lane = lax.broadcasted_iota(jnp.int32, (HD, HD), 1)
    return row == lane, lane == lax.rem(row + 1, HD)


def rounded(state):
    eye, beside = diagonals()
    whole = state + pltpu.roll(state, HD - 1, 1)
    rest = whole - whole.astype(BF).astype(F32)
    return jnp.where(eye, whole, jnp.where(beside, pltpu.roll(rest, 1, 1), state)).astype(BF)


def started(state):
    _, beside = diagonals()
    return jnp.where(beside, 0.0, state)


def pack_kernel(info, x_ref, kv_own, q_own, kv_other, q_other, stage):
    _, core, _, _ = spot(info)
    rows = x_ref.shape[0]
    for kind in range(3):
        for other in range(2):
            half = core if other == 0 else 1 - core
            first = pl.multiple_of(kind * 32 + half * 16, 16)
            part = x_ref[:, pl.ds(first, 16), :].astype(F32)
            if kind == 1:
                part = (
                    part
                    * lax.rsqrt(jnp.mean(part * part, axis=-1, keepdims=True) + 1e-06)
                    / math.sqrt(HD)
                )
            stage[...] = part.reshape(rows * 16, HD)
            for h in range(16):
                tile = stage[pl.ds(h, rows, stride=16), :].astype(BF)
                if kind == 0:
                    (q_own, q_other)[other][h] = tile
                else:
                    (kv_own, kv_other)[other][kind - 1, h] = tile


def sums_kernel(shift, info, lengths, own, other, out):
    x, _, _, _ = spot(info)
    place = places_of(info, 1)
    last = (info[1] * NX + x + 1) * BLOCK - 1
    tail = (doc_of(lengths, place) == doc_of(lengths, last)).astype(F32).astype(BF)
    for j in range(PER):
        h = lax.rem(x + shift, NX) * PER + j
        k = jnp.concatenate([own[0, h], other[0, h]], axis=0)
        v = jnp.concatenate([own[1, h], other[1, h]], axis=0)
        out[j, 0] = rounded(started(dot(k.T * tail, k)))
        out[j, 1] = dot(v.T * tail, k).astype(BF)


def weighted(out, terms):
    for j in range(PER):
        for which in range(2):
            total = jnp.zeros((HD, HD), F32)
            for weight, part in terms:
                total = total + weight * part[j, which].astype(F32)
            out[j, which] = rounded(total) if which == 0 else total.astype(BF)


def block_docs(info, lengths):
    first = info[1] * NX * BLOCK
    return [doc_of(lengths, first + b * BLOCK - 1) for b in range(NX + 1)]


def pick(values, place):
    out = values[0]
    for i in range(1, len(values)):
        out = jnp.where(place == i, values[i], out)
    return out


def totals_kernel(info, lengths, p0, p1, p2, p3, out):
    x, _, _, _ = spot(info)
    docs = block_docs(info, lengths)
    terms = []
    for shift, part in enumerate((p0, p1, p2, p3)):
        doc = pick(docs[1:], lax.rem(x - shift + NX, NX))
        terms.append(((doc == docs[NX]).astype(F32), part))
    weighted(out, terms)


def entries_kernel(info, lengths, parts, out):
    count, rows, _ = parts.shape
    width = NX * BLOCK
    docs = [doc_of(lengths, c * width - 1) for c in range(count + 1)]
    per = HD // rows
    symmetric = (info[1] // per) % 2 == 0
    row = (info[1] % per) * rows + lax.broadcasted_iota(jnp.int32, (rows, HD), 0)
    lane = lax.broadcasted_iota(jnp.int32, (rows, HD), 1)
    eye = (row == lane) & symmetric
    beside = (lane == lax.rem(row + 1, HD)) & symmetric
    running = jnp.zeros((rows, HD), F32)
    for c in range(count):
        whole = running + pltpu.roll(running, HD - 1, 1)
        rest = pltpu.roll(whole - whole.astype(BF).astype(F32), 1, 1)
        out[c] = jnp.where(eye, whole, jnp.where(beside, rest, running)).astype(BF)
        same = (docs[c + 1] == docs[c]).astype(F32)
        running = same * running + parts[c].astype(F32)


def states_kernel(shift, info, lengths, p0, p1, p2, p3, entry, out):
    x, _, _, _ = spot(info)
    docs = block_docs(info, lengths)
    mine = lax.rem(x + shift, NX)
    wanted = pick(docs[:NX], mine)
    terms = [((docs[0] == wanted).astype(F32), entry)]
    for back, part in enumerate((p0, p1, p2, p3)):
        b = lax.rem(x - back + NX, NX)
        terms.append((((b < mine) & (pick(docs[1:], b) == wanted)).astype(F32), part))
    weighted(out, terms)


def solve_kernel(
    shifts, info, lengths, reg, kv_own, kv_other, q_own, q_other, *rest,
):
    states, rest = rest[: len(shifts)], rest[len(shifts) :]
    out_own, out_other, lhs, key_t, same, valid = rest[:6]
    diagonal, direction, residual, solution, norm = rest[6:]
    x, core, _, _ = spot(info)
    before = doc_of(lengths, (info[1] * NX + x) * BLOCK - 1)
    lane = places_of(info, 1)
    row = places_of(info, 0)
    lane_doc = doc_of(lengths, lane)
    valid[...] = (lane_doc == before).astype(F32)
    same[...] = ((doc_of(lengths, row) == lane_doc) & (row <= lane)).astype(F32).astype(BF)
    eye, beside = diagonals()
    count = len(shifts) * PER

    def head(i):
        return lax.rem(x - shifts[i // PER] + NX, NX) * PER + i % PER

    def state(i, which):
        return states[i // PER][i % PER, which]

    for i in range(count):
        h = head(i)
        k = jnp.concatenate([kv_own[0, h], kv_other[0, h]], axis=0)
        keys = state(i, 0).astype(F32)
        mirrored = keys.T
        lhs[i, 0:BLOCK] = k
        lhs[i, BLOCK:] = jnp.where(eye, 0.0, jnp.where(beside, mirrored, keys)).astype(BF)
        key_t[i] = k.T
        middle = jnp.sum(jnp.where(eye | beside, keys, 0.0), axis=1, keepdims=True)
        diagonal[i] = middle * valid[...] + reg[core * 16 + h]
        q = jnp.concatenate([q_own[h], q_other[h]], axis=0).T.astype(F32)
        q = q * lax.rsqrt(jnp.mean(q * q, axis=0, keepdims=True) + 1e-06) / math.sqrt(HD)
        direction[i] = q
        residual[i] = q
        solution[i] = jnp.zeros_like(q)
        norm[i] = jnp.sum(q * q, axis=0, keepdims=True)

    def apply(i):
        full = dot(lhs[i], direction[i].astype(BF))
        return full[BLOCK:], full[0:BLOCK].astype(BF) * same[...]

    def update(i, from_state, score):
        p = direction[i]
        image = from_state * valid[...] + dot(key_t[i], score) + diagonal[i] * p
        old = norm[i]
        step = old / (jnp.sum(p * image, axis=0, keepdims=True) + 1e-06)
        solution[i] = solution[i] + step * p
        r = residual[i] - step * image
        residual[i] = r
        new = jnp.sum(r * r, axis=0, keepdims=True)
        direction[i] = r + (new / (old + 1e-06)) * p
        norm[i] = new

    def iterate(_, carried):
        held = {}
        for i in range(count + 2):
            if i < count:
                held[i] = apply(i)
            if i >= 2:
                update(i - 2, *held.pop(i - 2))
        return carried

    lax.fori_loop(0, ITERS, iterate, 0)
    for i in range(count):
        h = head(i)
        u = solution[i]
        high = u.astype(BF)
        low = (u - high.astype(F32)).astype(BF)
        score = dot(lhs[i, 0:BLOCK], high).astype(BF) * same[...]
        values = state(i, 1)
        from_state = dot(values, high) + dot(values, low)
        v = jnp.concatenate([kv_own[1, h], kv_other[1, h]], axis=0)
        result = (from_state * valid[...] + dot(v.T, score)).T.astype(BF)
        out_own[i] = result[0 : BLOCK // 2]
        out_other[i] = result[BLOCK // 2 :]


def unpack_kernel(info, *rest):
    parts, (out_ref, stage) = rest[:-2], rest[-2:]
    x, core, _, _ = spot(info)
    rows = out_ref.shape[0]
    for other in range(2):
        for g, shifts in enumerate(GROUPS):
            part = parts[2 * g + other]
            for i in range(len(shifts) * PER):
                h = lax.rem(x - shifts[i // PER] + NX, NX) * PER + i % PER
                stage[pl.ds(h, rows, stride=16), :] = part[i].astype(F32)
        half = core if other == 0 else 1 - core
        first = pl.multiple_of(half * 16, 16)
        out_ref[:, pl.ds(first, 16), :] = stage[...].reshape(rows, 16, HD).astype(BF)


def body(qkv, lengths, reg):
    rows, _, heads, width = qkv.shape
    half = heads // 2
    index = jnp.arange(2, dtype=jnp.int32)
    info = jnp.where(index == 0, lax.axis_index("head"), lax.axis_index("ctx")).astype(jnp.int32)

    def array(shape, dtype=BF):
        return jax.ShapeDtypeStruct(shape, dtype)

    def swap(a):
        return lax.ppermute(a, "head", [(i, i ^ 1) for i in range(2 * NX)])

    def along_x(a, shift):
        return lax.ppermute(
            a, "head", [(i, (i + 2 * shift) % (2 * NX)) for i in range(2 * NX)]
        )

    kv, q = array((2, half, rows, width)), array((half, rows, width))
    kv_own, q_own, kv_send, q_send = call(
        pack_kernel, [kv, q, kv, q], "pack", [pltpu.VMEM((rows * half, width), F32)], scalars=1
    )(info, qkv.reshape(rows, 3 * heads, width))
    kv_other = swap(kv_send)
    q_other = swap(q_send)

    states = array((PER, 2, width, width))
    order = (2, 1, 3, 0)
    parts = [None] * NX
    for shift in order:
        part = call(functools.partial(sums_kernel, shift), states, "block_sums")(
            info, lengths, kv_own, kv_other
        )
        parts[shift] = along_x(part, shift) if shift else part
    total = call(totals_kernel, states, "ctx_totals")(info, lengths, *parts)
    places = lax.axis_size("ctx")
    slices = lax.all_to_all(total.reshape(places, -1, width), "ctx", 0, 0, tiled=True)
    entries = call(entries_kernel, array(slices.shape), "entries")(info, lengths, slices)
    entry = lax.all_to_all(entries, "ctx", 0, 0, tiled=True).reshape(states.shape)
    before = [None] * NX
    for shift in order:
        part = call(functools.partial(states_kernel, shift), states, "block_states")(
            info, lengths, *parts, entry
        )
        before[shift] = along_x(part, shift) if shift else part

    results = []
    for shifts in GROUPS:
        count = len(shifts) * PER
        vectors = pltpu.VMEM((count, width, BLOCK), F32)
        result = array((count, rows, width))
        mine, others = call(
            functools.partial(solve_kernel, shifts),
            [result, result],
            "solve",
            [
                pltpu.VMEM((count, BLOCK + width, width), BF),
                pltpu.VMEM((count, width, BLOCK), BF),
                pltpu.VMEM((BLOCK, BLOCK), BF),
                pltpu.VMEM((1, BLOCK), F32),
                vectors,
                vectors,
                vectors,
                vectors,
                pltpu.VMEM((count, 1, BLOCK), F32),
            ],
            scalars=3,
            flops=10**9 * count,
            limit=24,
        )(info, lengths, reg, kv_own, kv_other, q_own, q_other, *(before[s] for s in shifts))
        results += [mine, swap(others)]
    return call(
        unpack_kernel,
        array((rows, heads, width)),
        "unpack",
        [pltpu.VMEM((rows * half, width), F32)],
        scalars=1,
    )(info, *results)


def solution(mesh):
    in_specs = (P(("ctx", "head"), None, None, None), P(), P())
    out_specs = P(("ctx", "head"), None, None)
    return jax.shard_map(body, mesh=mesh, in_specs=in_specs, out_specs=out_specs, check_vma=False)
```

time: 145 us -> 119 us (0.82)
  starting transfers between devices: 53 us -> 28.6 us
  blocking collectives: 0 us -> 15.6 us
  Pallas kernels: 59.1 us -> 51.4 us
  waiting for transfers between devices: 25.2 us -> 20.6 us
  local copies, waits for them, and re-layouts: 6.36 us -> 2.6 us
    ppermute x16 -> x0, starting transfers between devices: 33.7 us -> none  [the longest x14 26.6 us: along_z(): lax.ppermute(a, 'ctx', [(y * NZ + z, y * NZ + (z + shift) % NZ) for y in...]
    all_to_all x0 -> x1, blocking collectives: none -> 15.6 us  [body(): lax.all_to_all(entries, 'ctx', 0, 0, tiled=True).reshape(states.shape)]
    all_to_all x0 -> x1, starting transfers between devices: none -> 9.6 us  [body(): lax.all_to_all(total.reshape(places, -1, width), 'ctx', 0, 0, tiled=True)]
    all_to_all x0 -> x1, waiting for transfers between devices: none -> 7.78 us  [body(): lax.all_to_all(total.reshape(places, -1, width), 'ctx', 0, 0, tiled=True)]
    pallas_call x9 -> x15, Pallas kernels: 59.1 us -> 51.4 us  [run(): pl.pallas_call(kernel, in_specs=[SMEM] * scalars + [VMEM] * (len(args) -...]
    ppermute x16 -> x0, waiting for transfers between devices: 7.57 us -> none  [the longest x14 5.96 us: along_z(): lax.ppermute(a, 'ctx', [(y * NZ + z, y * NZ + (z + shift) % NZ) for y in...]
    ppermute x6, waiting for transfers between devices: 13.4 us -> 9.43 us  [along_x(): lax.ppermute(a, 'head', [(i, (i + 2 * shift) % (2 * NX)) for i in range(2...]
    unnamed x52 -> x14, local copies, waits for them, and re-layouts: 6.36 us -> 2.6 us
  transfers between devices with their start and end apart: 26 -> 12, of which waited for: 11 -> 6; matrix products, arithmetic and copies ran while one was open for 0% -> 0% of each run, Pallas kernels for 31% -> 36%
where the time goes in v3:
time: 119 us
  Pallas kernels  51.4 us (43%)
  starting transfers between devices  28.6 us (24%)
  waiting for transfers between devices  20.6 us (17%)
  blocking collectives  15.6 us (13%)
  local copies, waits for them, and re-layouts  2.6 us (2%)
    pallas_call x15, Pallas kernels, run(): pl.pallas_call(kernel, in_specs=[SMEM] * scalars + [VMEM] * (len(args) -...  51.4 us
    all_to_all x1, blocking collectives, body(): lax.all_to_all(entries, 'ctx', 0, 0, tiled=True).reshape(states.shape)  15.6 us
    ppermute x5, starting transfers between devices, swap(): return lax.ppermute(a, 'head', [(i, i ^ 1) for i in range(2 * NX)])  9.95 us
    all_to_all x1, starting transfers between devices, body(): lax.all_to_all(total.reshape(places, -1, width), 'ctx', 0, 0, tiled=True)  9.6 us
    ppermute x6, waiting for transfers between devices, along_x(): lax.ppermute(a, 'head', [(i, (i + 2 * shift) % (2 * NX)) for i in range(2...  9.43 us
    ppermute x6, starting transfers between devices, along_x(): lax.ppermute(a, 'head', [(i, (i + 2 * shift) % (2 * NX)) for i in range(2...  9.02 us
    all_to_all x1, waiting for transfers between devices, body(): lax.all_to_all(total.reshape(places, -1, width), 'ctx', 0, 0, tiled=True)  7.78 us
    ppermute x5, waiting for transfers between devices, swap(): return lax.ppermute(a, 'head', [(i, i ^ 1) for i in range(2 * NX)])  3.41 us
  transfers between devices with their start and end apart: 12, of which 6 were waited for; matrix products, arithmetic and copies ran while one was open for 0% of the time, Pallas kernels for 36%

profile of v3, /device:TPU:1, one launch (start us, length us, event | category | flops | bytes accessed | tf_op | source)
XLA Modules:
  0.0 119.0 jit_solution(3129271639759309688)
XLA Ops:
  0.0 1.9 %copy-done = bf16[128,3,32,128]{3,2,1,0:T(8,128)(2,1)S(1)} copy-done((bf16[128,3,32,128]{3,2,1,0:T(8,128)(2,1)S(1)}, bf16[128,3,32,128]{3,2,1,0:T(8,128)(2,1)}, u32[]{:S(2)}) %copy-start) | copy-done | bytes 3145752
  1.9 4.0 %pack.1 = (bf16[2,16,128,128]{3,2,1,0:T(8,128)(2,1)S(1)}, bf16[16,128,128]{2,1,0:T(8,128)(2,1)S(1)}, bf16[2,16,128,128]{3,2,1,0:T(8,128)(2,1)S(1)}, bf16[16,128,128]{2,1,0:T(8,128)(2,1)S(1)}) custom-call(s32[2]{0:T(128)S(1)} %compare_select_fusion.info, bf16[128,96,128]{2,1,0:T(8,128)(2,1)S(1)} %bitcast.7), custom_call_target="tpu_custom_call" | custom-call | bytes 3145736 | tf_op jit(solution)/shard_map/pack/pallas_call | solution.py:32
  6.0 3.3 %collective-permute-start = (bf16[2,16,128,128]{3,2,1,0:T(8,128)(2,1)S(1)}, bf16[2,16,128,128]{3,2,1,0:T(8,128)(2,1)S(1)}, u32[]{:S(2)}, u32[]{:S(2)}) collective-permute-start(bf16[2,16,128,128]{3,2,1,0:T(8,128)(2,1)S(1)} %get-tuple-element.16), channel_id=1, source_target_pairs={{0,1},{1,0},{2,3},{3,2},{4,5},{5,4},{6,7},{7,6},{8,9},{9,8},{10,11... | collective-permute-start | bytes 3145736 | tf_op jit(solution)/shard_map/ppermute | solution.py:288
  9.2 2.3 %collective-permute-done.other.kv_other = bf16[2,16,128,128]{3,2,1,0:T(8,128)(2,1)S(1)} collective-permute-done((bf16[2,16,128,128]{3,2,1,0:T(8,128)(2,1)S(1)}, bf16[2,16,128,128]{3,2,1,0:T(8,128)(2,1)S(1)}, u32[]{:S(2)}, u32[]{:S(2)}) %collective-permute-start) | collective-permute-done | bytes 1048608 | tf_op jit(solution)/shard_map/ppermute | solution.py:288
  11.5 1.0 block_sums.5
  12.6 1.0 block_sums.6
  13.7 2.0 %collective-permute-start.3 = (bf16[4,2,128,128]{3,2,1,0:T(8,128)(2,1)S(1)}, bf16[4,2,128,128]{3,2,1,0:T(8,128)(2,1)S(1)}, u32[]{:S(2)}, u32[]{:S(2)}) collective-permute-start(bf16[4,2,128,128]{3,2,1,0:T(8,128)(2,1)S(1)} %block_sums.6), channel_id=1, source_target_pairs={{0,4},{1,5},{2,6},{3,7},{4,0},{5,1},{6,2},{7,3},{8,12},{9,13},{10,... | collective-permute-start | bytes 786440 | tf_op jit(solution)/shard_map/ppermute | solution.py:291
  16.7 1.2 %collective-permute-start.4 = (bf16[4,2,128,128]{3,2,1,0:T(8,128)(2,1)S(1)}, bf16[4,2,128,128]{3,2,1,0:T(8,128)(2,1)S(1)}, u32[]{:S(2)}, u32[]{:S(2)}) collective-permute-start(bf16[4,2,128,128]{3,2,1,0:T(8,128)(2,1)S(1)} %block_sums.7), channel_id=1, source_target_pairs={{0,6},{1,7},{2,0},{3,1},{4,2},{5,3},{6,4},{7,5},{8,14},{9,15},{10,... | collective-permute-start | bytes 786440 | tf_op jit(solution)/shard_map/ppermute | solution.py:291
  19.0 3.1 %collective-permute-done.2.p1 = bf16[4,2,128,128]{3,2,1,0:T(8,128)(2,1)S(1)} collective-permute-done((bf16[4,2,128,128]{3,2,1,0:T(8,128)(2,1)S(1)}, bf16[4,2,128,128]{3,2,1,0:T(8,128)(2,1)S(1)}, u32[]{:S(2)}, u32[]{:S(2)}) %collective-permute-start.2) | collective-permute-done | bytes 262176 | tf_op jit(solution)/shard_map/ppermute | solution.py:291
  22.0 4.2 %collective-permute-done.3.p2 = bf16[4,2,128,128]{3,2,1,0:T(8,128)(2,1)S(1)} collective-permute-done((bf16[4,2,128,128]{3,2,1,0:T(8,128)(2,1)S(1)}, bf16[4,2,128,128]{3,2,1,0:T(8,128)(2,1)S(1)}, u32[]{:S(2)}, u32[]{:S(2)}) %collective-permute-start.3) | collective-permute-done | bytes 262176 | tf_op jit(solution)/shard_map/ppermute | solution.py:291
  26.3 2.1 %collective-permute-done.4.p3 = bf16[4,2,128,128]{3,2,1,0:T(8,128)(2,1)S(1)} collective-permute-done((bf16[4,2,128,128]{3,2,1,0:T(8,128)(2,1)S(1)}, bf16[4,2,128,128]{3,2,1,0:T(8,128)(2,1)S(1)}, u32[]{:S(2)}, u32[]{:S(2)}) %collective-permute-start.4) | collective-permute-done | bytes 262176 | tf_op jit(solution)/shard_map/ppermute | solution.py:291
  30.0 9.6 %all-to-all-start = ((bf16[32,32,128]{2,1,0:T(8,128)(2,1)}), bf16[32,32,128]{2,1,0:T(8,128)(2,1)S(1)}, u32[]{:S(2)}, u32[]{:S(2)}) async-start(bf16[32,32,128]{2,1,0:T(8,128)(2,1)} %bitcast.8), calls=%async_computation | async-start | bytes 524288 | tf_op jit(solution)/shard_map/all_to_all | solution.py:312
  39.6 1.9 %collective-permute-start.1 = (bf16[16,128,128]{2,1,0:T(8,128)(2,1)}, bf16[16,128,128]{2,1,0:T(8,128)(2,1)}, u32[]{:S(2)}, u32[]{:S(2)}) collective-permute-start(bf16[16,128,128]{2,1,0:T(8,128)(2,1)} %copy-done.5), channel_id=1, source_target_pairs={{0,1},{1,0},{2,3},{3,2},{4,5},{5,4},{6,7},{7,6},{8,9},{9,8},{10,11... | collective-permute-start | bytes 1572872 | tf_op jit(solution)/shard_map/ppermute | solution.py:288
  41.5 7.8 %all-to-all-done.parts = bf16[32,32,128]{2,1,0:T(8,128)(2,1)S(1)} async-done(((bf16[32,32,128]{2,1,0:T(8,128)(2,1)}), bf16[32,32,128]{2,1,0:T(8,128)(2,1)S(1)}, u32[]{:S(2)}, u32[]{:S(2)}) %all-to-all-start) | async-done | bytes 262176 | tf_op jit(solution)/shard_map/all_to_all | solution.py:312
  49.3 1.1 entries.1
  50.4 15.6 %all_to_all.10 = bf16[32,32,128]{2,1,0:T(8,128)(2,1)S(1)} all-to-all(bf16[32,32,128]{2,1,0:T(8,128)(2,1)S(1)} %entries.1), channel_id=1, replica_groups=mesh['ctx'=32,'head'=8] {'ctx'}, dimensions={0} | all-to-all | bytes 524288 | tf_op jit(solution)/shard_map/all_to_all | solution.py:314
  67.0 3.5 %collective-permute-start.6 = (bf16[4,2,128,128]{3,2,1,0:T(8,128)(2,1)S(1)}, bf16[4,2,128,128]{3,2,1,0:T(8,128)(2,1)S(1)}, u32[]{:S(2)}, u32[]{:S(2)}) collective-permute-start(bf16[4,2,128,128]{3,2,1,0:T(8,128)(2,1)S(1)} %block_states.5), channel_id=1, source_target_pairs={{0,2},{1,3},{2,4},{3,5},{4,6},{5,7},{6,0},{7,1},{8,10},{9,11},{10,... | collective-permute-start | bytes 786440 | tf_op jit(solution)/shard_map/ppermute | solution.py:291
  73.0 9.8 %solve.3 = (bf16[4,128,128]{2,1,0:T(8,128)(2,1)S(1)}, bf16[4,128,128]{2,1,0:T(8,128)(2,1)S(1)}) custom-call(s32[2]{0:T(128)S(1)} %compare_select_fusion.info, s32[8]{0:T(128)S(1)} %copy-done.2, f32[32]{0:T(128)S(1)} %copy-done.6, bf16[2,16,128,128]{3,2,1,0:T(8,128)(2,1)S(1)} %get-tuple-element.15.own.kv_own, ...), custom_call_target="tpu_custom_call" | custom-call | flops 4000000000 | bytes 3408040 | tf_op jit(solution)/shard_map/solve/pallas_call | solution.py:32
  82.9 4.1 %collective-permute-start.5 = (bf16[4,128,128]{2,1,0:T(8,128)(2,1)S(1)}, bf16[4,128,128]{2,1,0:T(8,128)(2,1)S(1)}, u32[]{:S(2)}, u32[]{:S(2)}) collective-permute-start(bf16[4,128,128]{2,1,0:T(8,128)(2,1)S(1)} %get-tuple-element.20), channel_id=1, source_target_pairs={{0,1},{1,0},{2,3},{3,2},{4,5},{5,4},{6,7},{7,6},{8,9},{9,8},{10,11... | collective-permute-start | bytes 393224 | tf_op jit(solution)/shard_map/ppermute | solution.py:288
  87.9 1.6 %collective-permute-start.9 = (bf16[4,2,128,128]{3,2,1,0:T(8,128)(2,1)S(1)}, bf16[4,2,128,128]{3,2,1,0:T(8,128)(2,1)S(1)}, u32[]{:S(2)}, u32[]{:S(2)}) collective-permute-start(bf16[4,2,128,128]{3,2,1,0:T(8,128)(2,1)S(1)} %block_states.7), channel_id=1, source_target_pairs={{0,4},{1,5},{2,6},{3,7},{4,0},{5,1},{6,2},{7,3},{8,12},{9,13},{10,... | collective-permute-start | bytes 786440 | tf_op jit(solution)/shard_map/ppermute | solution.py:291
  89.5 15.4 %solve.4 = (bf16[8,128,128]{2,1,0:T(8,128)(2,1)S(1)}, bf16[8,128,128]{2,1,0:T(8,128)(2,1)S(1)}) custom-call(s32[2]{0:T(128)S(1)} %compare_select_fusion.info, s32[8]{0:T(128)S(1)} %copy-done.2, f32[32]{0:T(128)S(1)} %copy-done.6, bf16[2,16,128,128]{3,2,1,0:T(8,128)(2,1)S(1)} %get-tuple-element.15.own.kv_own, ...), custom_call_target="tpu_custom_call" | custom-call | flops 8000000000 | bytes 3670184 | tf_op jit(solution)/shard_map/solve/pallas_call | solution.py:32
  105.3 9.8 %solve.5 = (bf16[4,128,128]{2,1,0:T(8,128)(2,1)S(1)}, bf16[4,128,128]{2,1,0:T(8,128)(2,1)S(1)}) custom-call(s32[2]{0:T(128)S(1)} %compare_select_fusion.info, s32[8]{0:T(128)S(1)} %copy-done.2, f32[32]{0:T(128)S(1)} %copy-done.6, bf16[2,16,128,128]{3,2,1,0:T(8,128)(2,1)S(1)} %get-tuple-element.15.own.kv_own, ...), custom_call_target="tpu_custom_call" | custom-call | flops 4000000000 | bytes 3408040 | tf_op jit(solution)/shard_map/solve/pallas_call | solution.py:32
  115.5 1.1 collective-permute-done.10.rest_5_
  116.6 2.4 %unpack.1 = bf16[128,32,128]{2,1,0:T(8,128)(2,1)} custom-call(s32[2]{0:T(128)S(1)} %compare_select_fusion.info, bf16[4,128,128]{2,1,0:T(8,128)(2,1)S(1)} %get-tuple-element.19.rest_0_, bf16[4,128,128]{2,1,0:T(8,128)(2,1)S(1)} %collective-permute-done.5.rest_1_, bf16[8,128,128]{2,1,0:T(8,128)(2,1)S(1)} %get-tuple-element.21.rest_2_, ...), custom_call_target="tpu_custom_call" | custom-call | bytes 1048584 | tf_op jit(solution)/shard_map/unpack/pallas_call | solution.py:32
  (31 shorter events, 8.9 us)
Async XLA Ops:
  0.0 11.5 %copy-start.2 = (s32[8]{0:T(128)S(1)}, s32[8]{0:T(128)}, u32[]{:S(2)}) copy-start(s32[8]{0:T(128)} %lengths.25) | copy-start | bytes 100
  0.0 1.9 %copy-start = (bf16[128,3,32,128]{3,2,1,0:T(8,128)(2,1)S(1)}, bf16[128,3,32,128]{3,2,1,0:T(8,128)(2,1)}, u32[]{:S(2)}) copy-start(bf16[128,3,32,128]{3,2,1,0:T(8,128)(2,1)} %param.3) | copy-start | bytes 9437188
  5.9 10.8 %copy-start.3 = (bf16[16,128,128]{2,1,0:T(8,128)(2,1)}, bf16[16,128,128]{2,1,0:T(8,128)(2,1)S(1)}, u32[]{:S(2)}) copy-start(bf16[16,128,128]{2,1,0:T(8,128)(2,1)S(1)} %get-tuple-element.17.q_own) | copy-start | bytes 1572868
  5.9 10.8 %copy-start.5 = (bf16[16,128,128]{2,1,0:T(8,128)(2,1)}, bf16[16,128,128]{2,1,0:T(8,128)(2,1)S(1)}, u32[]{:S(2)}) copy-start(bf16[16,128,128]{2,1,0:T(8,128)(2,1)S(1)} %get-tuple-element.18) | copy-start | bytes 1572868
  6.0 5.6 %collective-permute-start = (bf16[2,16,128,128]{3,2,1,0:T(8,128)(2,1)S(1)}, bf16[2,16,128,128]{3,2,1,0:T(8,128)(2,1)S(1)}, u32[]{:S(2)}, u32[]{:S(2)}) collective-permute-start(bf16[2,16,128,128]{3,2,1,0:T(8,128)(2,1)S(1)} %get-tuple-element.16), channel_id=1, source_target_pairs={{0,1},{1,0},{2,3},{3,2},{4,5},{5,4},{6,7},{7,6},{8,9},{9,8},{10,11... | collective-permute-start | bytes 3145736 | tf_op jit(solution)/shard_map/ppermute | solution.py:288
  12.6 9.5 %collective-permute-start.2 = (bf16[4,2,128,128]{3,2,1,0:T(8,128)(2,1)S(1)}, bf16[4,2,128,128]{3,2,1,0:T(8,128)(2,1)S(1)}, u32[]{:S(2)}, u32[]{:S(2)}) collective-permute-start(bf16[4,2,128,128]{3,2,1,0:T(8,128)(2,1)S(1)} %block_sums.5), channel_id=1, source_target_pairs={{0,2},{1,3},{2,4},{3,5},{4,6},{5,7},{6,0},{7,1},{8,10},{9,11},{10,... | collective-permute-start | bytes 786440 | tf_op jit(solution)/shard_map/ppermute | solution.py:291
  13.7 12.6 %collective-permute-start.3 = (bf16[4,2,128,128]{3,2,1,0:T(8,128)(2,1)S(1)}, bf16[4,2,128,128]{3,2,1,0:T(8,128)(2,1)S(1)}, u32[]{:S(2)}, u32[]{:S(2)}) collective-permute-start(bf16[4,2,128,128]{3,2,1,0:T(8,128)(2,1)S(1)} %block_sums.6), channel_id=1, source_target_pairs={{0,4},{1,5},{2,6},{3,7},{4,0},{5,1},{6,2},{7,3},{8,12},{9,13},{10,... | collective-permute-start | bytes 786440 | tf_op jit(solution)/shard_map/ppermute | solution.py:291
  16.7 11.7 %collective-permute-start.4 = (bf16[4,2,128,128]{3,2,1,0:T(8,128)(2,1)S(1)}, bf16[4,2,128,128]{3,2,1,0:T(8,128)(2,1)S(1)}, u32[]{:S(2)}, u32[]{:S(2)}) collective-permute-start(bf16[4,2,128,128]{3,2,1,0:T(8,128)(2,1)S(1)} %block_sums.7), channel_id=1, source_target_pairs={{0,6},{1,7},{2,0},{3,1},{4,2},{5,3},{6,4},{7,5},{8,14},{9,15},{10,... | collective-permute-start | bytes 786440 | tf_op jit(solution)/shard_map/ppermute | solution.py:291
  29.3 0.7 copy-start.1
  30.0 43.0 %copy-start.6 = (f32[32]{0:T(128)S(1)}, f32[32]{0:T(128)}, u32[]{:S(2)}) copy-start(f32[32]{0:T(128)} %reg.5) | copy-start | bytes 388
  30.0 19.3 %all-to-all-start = ((bf16[32,32,128]{2,1,0:T(8,128)(2,1)}), bf16[32,32,128]{2,1,0:T(8,128)(2,1)S(1)}, u32[]{:S(2)}, u32[]{:S(2)}) async-start(bf16[32,32,128]{2,1,0:T(8,128)(2,1)} %bitcast.8), calls=%async_computation | async-start | bytes 524288 | tf_op jit(solution)/shard_map/all_to_all | solution.py:312
  39.6 33.4 %collective-permute-start.1 = (bf16[16,128,128]{2,1,0:T(8,128)(2,1)}, bf16[16,128,128]{2,1,0:T(8,128)(2,1)}, u32[]{:S(2)}, u32[]{:S(2)}) collective-permute-start(bf16[16,128,128]{2,1,0:T(8,128)(2,1)} %copy-done.5), channel_id=1, source_target_pairs={{0,1},{1,0},{2,3},{3,2},{4,5},{5,4},{6,7},{7,6},{8,9},{9,8},{10,11... | collective-permute-start | bytes 1572872 | tf_op jit(solution)/shard_map/ppermute | solution.py:288
  49.3 23.7 %copy-start.4 = (bf16[16,128,128]{2,1,0:T(8,128)(2,1)S(1)}, bf16[16,128,128]{2,1,0:T(8,128)(2,1)}, u32[]{:S(2)}) copy-start(bf16[16,128,128]{2,1,0:T(8,128)(2,1)} %copy-done.3) | copy-start | bytes 1572868
  67.0 22.5 %collective-permute-start.6 = (bf16[4,2,128,128]{3,2,1,0:T(8,128)(2,1)S(1)}, bf16[4,2,128,128]{3,2,1,0:T(8,128)(2,1)S(1)}, u32[]{:S(2)}, u32[]{:S(2)}) collective-permute-start(bf16[4,2,128,128]{3,2,1,0:T(8,128)(2,1)S(1)} %block_states.5), channel_id=1, source_target_pairs={{0,2},{1,3},{2,4},{3,5},{4,6},{5,7},{6,0},{7,1},{8,10},{9,11},{10,... | collective-permute-start | bytes 786440 | tf_op jit(solution)/shard_map/ppermute | solution.py:291
  71.5 18.1 %collective-permute-start.7 = (bf16[4,2,128,128]{3,2,1,0:T(8,128)(2,1)S(1)}, bf16[4,2,128,128]{3,2,1,0:T(8,128)(2,1)S(1)}, u32[]{:S(2)}, u32[]{:S(2)}) collective-permute-start(bf16[4,2,128,128]{3,2,1,0:T(8,128)(2,1)S(1)} %block_states.6), channel_id=1, source_target_pairs={{0,6},{1,7},{2,0},{3,1},{4,2},{5,3},{6,4},{7,5},{8,14},{9,15},{10,... | collective-permute-start | bytes 786440 | tf_op jit(solution)/shard_map/ppermute | solution.py:291
  82.9 32.6 %collective-permute-start.5 = (bf16[4,128,128]{2,1,0:T(8,128)(2,1)S(1)}, bf16[4,128,128]{2,1,0:T(8,128)(2,1)S(1)}, u32[]{:S(2)}, u32[]{:S(2)}) collective-permute-start(bf16[4,128,128]{2,1,0:T(8,128)(2,1)S(1)} %get-tuple-element.20), channel_id=1, source_target_pairs={{0,1},{1,0},{2,3},{3,2},{4,5},{5,4},{6,7},{7,6},{8,9},{9,8},{10,11... | collective-permute-start | bytes 393224 | tf_op jit(solution)/shard_map/ppermute | solution.py:288
  87.9 17.4 %collective-permute-start.9 = (bf16[4,2,128,128]{3,2,1,0:T(8,128)(2,1)S(1)}, bf16[4,2,128,128]{3,2,1,0:T(8,128)(2,1)S(1)}, u32[]{:S(2)}, u32[]{:S(2)}) collective-permute-start(bf16[4,2,128,128]{3,2,1,0:T(8,128)(2,1)S(1)} %block_states.7), channel_id=1, source_target_pairs={{0,4},{1,5},{2,6},{3,7},{4,0},{5,1},{6,2},{7,3},{8,12},{9,13},{10,... | collective-permute-start | bytes 786440 | tf_op jit(solution)/shard_map/ppermute | solution.py:291
  105.0 11.6 %collective-permute-start.8 = (bf16[8,128,128]{2,1,0:T(8,128)(2,1)S(1)}, bf16[8,128,128]{2,1,0:T(8,128)(2,1)S(1)}, u32[]{:S(2)}, u32[]{:S(2)}) collective-permute-start(bf16[8,128,128]{2,1,0:T(8,128)(2,1)S(1)} %get-tuple-element.22), channel_id=1, source_target_pairs={{0,1},{1,0},{2,3},{3,2},{4,5},{5,4},{6,7},{7,6},{8,9},{9,8},{10,11... | collective-permute-start | bytes 786440 | tf_op jit(solution)/shard_map/ppermute | solution.py:288
  115.2 1.4 %collective-permute-start.10 = (bf16[4,128,128]{2,1,0:T(8,128)(2,1)S(1)}, bf16[4,128,128]{2,1,0:T(8,128)(2,1)S(1)}, u32[]{:S(2)}, u32[]{:S(2)}) collective-permute-start(bf16[4,128,128]{2,1,0:T(8,128)(2,1)S(1)} %get-tuple-element.24), channel_id=1, source_target_pairs={{0,1},{1,0},{2,3},{3,2},{4,5},{5,4},{6,7},{7,6},{8,9},{9,8},{10,11... | collective-permute-start | bytes 393224 | tf_op jit(solution)/shard_map/ppermute | solution.py:288

commit v4 on v3

--- a/solution.py
+++ b/solution.py
@@ -9,6 +9,7 @@
 from jax.sharding import PartitionSpec as P
 
 ITERS = 10
+UNROLL = 2
 GROUPS = ((0,), (1, 3), (2,))
 BLOCK = 256
 HD = 128
@@ -83,27 +84,41 @@
     return jnp.where(beside, 0.0, state)
 
 
-def pack_kernel(info, x_ref, kv_own, q_own, kv_other, q_other, stage):
-    _, core, _, _ = spot(info)
+def pack_kernel(keys_first, info, x_ref, out_ref, stage):
     rows = x_ref.shape[0]
-    for kind in range(3):
-        for other in range(2):
-            half = core if other == 0 else 1 - core
-            first = pl.multiple_of(kind * 32 + half * 16, 16)
-            part = x_ref[:, pl.ds(first, 16), :].astype(F32)
-            if kind == 1:
-                part = (
-                    part
-                    * lax.rsqrt(jnp.mean(part * part, axis=-1, keepdims=True) + 1e-06)
-                    / math.sqrt(HD)
-                )
-            stage[...] = part.reshape(rows * 16, HD)
-            for h in range(16):
-                tile = stage[pl.ds(h, rows, stride=16), :].astype(BF)
-                if kind == 0:
-                    (q_own, q_other)[other][h] = tile
-                else:
-                    (kv_own, kv_other)[other][kind - 1, h] = tile
+    part = x_ref[...].astype(F32)
+    stage[...] = part.reshape(rows * 16, HD)
+    if keys_first:
+
+        @pl.when(pl.program_id(0) == 0)
+        def _():
+            scale = lax.rsqrt(jnp.mean(part * part, axis=-1, keepdims=True) + 1e-06)
+            stage[...] = (part * scale / math.sqrt(HD)).reshape(rows * 16, HD)
+
+    for h in range(16):
+        out_ref[0, h] = stage[pl.ds(h, rows, stride=16), :].astype(BF)
+
+
+def pack(info, qkv, first, count, other):
+    rows = qkv.shape[0]
+
+    def place(g, info):
+        core = info[0] % 2
+        return 0, 2 * (first + g) + (1 - core if other else core), 0
+
+    return pl.pallas_call(
+        functools.partial(pack_kernel, first == 1),
+        grid_spec=pltpu.PrefetchScalarGridSpec(
+            num_scalar_prefetch=1,
+            grid=(count,),
+            in_specs=[pl.BlockSpec((rows, 16, HD), place)],
+            out_specs=pl.BlockSpec((1, 16, rows, HD), lambda g, info: (g, 0, 0, 0)),
+            scratch_shapes=[pltpu.VMEM((rows * 16, HD), F32)],
+        ),
+        out_shape=jax.ShapeDtypeStruct((count, 16, rows, HD), BF),
+        compiler_params=pltpu.CompilerParams(vmem_limit_bytes=12 << 20),
+        name="pack",
+    )(info, qkv)
 
 
 def sums_kernel(shift, info, lengths, own, other, out):
@@ -181,52 +196,66 @@
     weighted(out, terms)
 
 
-def solve_kernel(
-    shifts, info, lengths, reg, kv_own, kv_other, q_own, q_other, *rest,
+def prepare_kernel(
+    info, lengths, kv_own, kv_other, q_own, q_other, keys, key_t, value_t, query, same, valid
 ):
-    states, rest = rest[: len(shifts)], rest[len(shifts) :]
-    out_own, out_other, lhs, key_t, same, valid = rest[:6]
-    diagonal, direction, residual, solution, norm = rest[6:]
-    x, core, _, _ = spot(info)
+    x, _, _, _ = spot(info)
     before = doc_of(lengths, (info[1] * NX + x) * BLOCK - 1)
     lane = places_of(info, 1)
     row = places_of(info, 0)
     lane_doc = doc_of(lengths, lane)
     valid[...] = (lane_doc == before).astype(F32)
     same[...] = ((doc_of(lengths, row) == lane_doc) & (row <= lane)).astype(F32).astype(BF)
+
+    def one(pair, carried):
+        for h in (2 * pair, 2 * pair + 1):
+            k = jnp.concatenate([kv_own[0, h], kv_other[0, h]], axis=0)
+            keys[h] = k
+            key_t[h] = k.T
+            value_t[h] = jnp.concatenate([kv_own[1, h], kv_other[1, h]], axis=0).T
+            q = jnp.concatenate([q_own[0, h], q_other[0, h]], axis=0).T.astype(F32)
+            scale = lax.rsqrt(jnp.mean(q * q, axis=0, keepdims=True) + 1e-06)
+            query[h] = q * scale / math.sqrt(HD)
+        return carried
+
+    lax.fori_loop(0, keys.shape[0] // 2, one, 0)
+
+
+def solve_kernel(shifts, info, reg, keys, key_t, value_t, query, same, valid, *rest):
+    states, rest = rest[: len(shifts)], rest[len(shifts) :]
+    out_own, out_other, lhs, held_valid, diagonal, direction, residual, solution, norm = rest
+    x, core, _, _ = spot(info)
+    held_valid[...] = jnp.broadcast_to(valid[...], (HD, BLOCK)).astype(BF)
     eye, beside = diagonals()
     count = len(shifts) * PER
-
-    def head(i):
-        return lax.rem(x - shifts[i // PER] + NX, NX) * PER + i % PER
+    head = [lax.rem(x - shifts[i // PER] + NX, NX) * PER + i % PER for i in range(count)]
 
     def state(i, which):
         return states[i // PER][i % PER, which]
 
     for i in range(count):
-        h = head(i)
-        k = jnp.concatenate([kv_own[0, h], kv_other[0, h]], axis=0)
-        keys = state(i, 0).astype(F32)
-        mirrored = keys.T
-        lhs[i, 0:BLOCK] = k
-        lhs[i, BLOCK:] = jnp.where(eye, 0.0, jnp.where(beside, mirrored, keys)).astype(BF)
-        key_t[i] = k.T
-        middle = jnp.sum(jnp.where(eye | beside, keys, 0.0), axis=1, keepdims=True)
-        diagonal[i] = middle * valid[...] + reg[core * 16 + h]
-        q = jnp.concatenate([q_own[h], q_other[h]], axis=0).T.astype(F32)
-        q = q * lax.rsqrt(jnp.mean(q * q, axis=0, keepdims=True) + 1e-06) / math.sqrt(HD)
+        held = state(i, 0).astype(F32)
+        plain = jnp.where(eye, 0.0, jnp.where(beside, held.T, held)).astype(BF)
+        lhs[i, :, 0:BLOCK] = key_t[head[i]]
+        lhs[i, :, BLOCK:] = plain
+        middle = jnp.sum(jnp.where(eye | beside, held, 0.0), axis=1, keepdims=True)
+        diagonal[i] = middle * valid[...] + reg[core * 16 + head[i]]
+        q = query[head[i]]
         direction[i] = q
         residual[i] = q
         solution[i] = jnp.zeros_like(q)
         norm[i] = jnp.sum(q * q, axis=0, keepdims=True)
 
+    def scores(i, rounded_vector):
+        return dot(keys[head[i]], rounded_vector).astype(BF) * same[...]
+
     def apply(i):
-        full = dot(lhs[i], direction[i].astype(BF))
-        return full[BLOCK:], full[0:BLOCK].astype(BF) * same[...]
-
-    def update(i, from_state, score):
+        p = direction[i].astype(BF)
+        return jnp.concatenate([scores(i, p), p * held_valid[...]], axis=0)
+
+    def update(i, applied):
         p = direction[i]
-        image = from_state * valid[...] + dot(key_t[i], score) + diagonal[i] * p
+        image = dot(lhs[i], applied) + diagonal[i] * p
         old = norm[i]
         step = old / (jnp.sum(p * image, axis=0, keepdims=True) + 1e-06)
         solution[i] = solution[i] + step * p
@@ -236,28 +265,35 @@
         direction[i] = r + (new / (old + 1e-06)) * p
         norm[i] = new
 
+    def staggered(first, second, total, lag):
+        held = {}
+        for t in range(total + lag):
+            if t < total:
+                held[t] = first(t % count)
+            if t >= lag:
+                second((t - lag) % count, held.pop(t - lag))
+
     def iterate(_, carried):
-        held = {}
-        for i in range(count + 2):
-            if i < count:
-                held[i] = apply(i)
-            if i >= 2:
-                update(i - 2, *held.pop(i - 2))
+        staggered(apply, update, UNROLL * count, 3)
         return carried
 
-    lax.fori_loop(0, ITERS, iterate, 0)
-    for i in range(count):
-        h = head(i)
+    def apply_last(i):
         u = solution[i]
         high = u.astype(BF)
         low = (u - high.astype(F32)).astype(BF)
-        score = dot(lhs[i, 0:BLOCK], high).astype(BF) * same[...]
+        return jnp.concatenate(
+            [scores(i, high), high * held_valid[...], low * held_valid[...]], axis=0
+        )
+
+    def finish(i, applied):
         values = state(i, 1)
-        from_state = dot(values, high) + dot(values, low)
-        v = jnp.concatenate([kv_own[1, h], kv_other[1, h]], axis=0)
-        result = (from_state * valid[...] + dot(v.T, score)).T.astype(BF)
+        whole = jnp.concatenate([value_t[head[i]], values, values], axis=1)
+        result = dot(whole, applied).T.astype(BF)
         out_own[i] = result[0 : BLOCK // 2]
         out_other[i] = result[BLOCK // 2 :]
+
+    lax.fori_loop(0, ITERS // UNROLL, iterate, 0)
+    staggered(apply_last, finish, count, 2)
 
 
 def unpack_kernel(info, *rest):
@@ -292,21 +328,46 @@
             a, "head", [(i, (i + 2 * shift) % (2 * NX)) for i in range(2 * NX)]
         )
 
-    kv, q = array((2, half, rows, width)), array((half, rows, width))
-    kv_own, q_own, kv_send, q_send = call(
-        pack_kernel, [kv, q, kv, q], "pack", [pltpu.VMEM((rows * half, width), F32)], scalars=1
-    )(info, qkv.reshape(rows, 3 * heads, width))
-    kv_other = swap(kv_send)
-    q_other = swap(q_send)
+    def relay(a):
+        ring = [(2 * x, 2 * ((x + 1) % NX)) for x in range(NX)]
+        back = [(2 * x + 1, 2 * ((x - 1) % NX) + 1) for x in range(NX)]
+        return lax.ppermute(a, "head", ring + back)
+
+    flat = qkv.reshape(rows, 3 * heads, width)
+    kv_other = swap(pack(info, flat, 1, 2, True))
+    q_other = swap(pack(info, flat, 0, 1, True))
+    kv_own = pack(info, flat, 1, 2, False)
+    q_own = pack(info, flat, 0, 1, False)
 
     states = array((PER, 2, width, width))
     order = (2, 1, 3, 0)
     parts = [None] * NX
+    own = kv_own
     for shift in order:
+        if shift == 0:
+            own, parts[2] = lax.optimization_barrier((own, parts[2]))
+            parts[2] = relay(parts[2])
         part = call(functools.partial(sums_kernel, shift), states, "block_sums")(
-            info, lengths, kv_own, kv_other
+            info, lengths, own, kv_other
         )
-        parts[shift] = along_x(part, shift) if shift else part
+        if shift:
+            part = relay(part) if shift == 2 else along_x(part, shift)
+        parts[shift] = part
+    columns = array((half, width, BLOCK))
+    prepared = call(
+        prepare_kernel,
+        [
+            array((half, BLOCK, width)),
+            columns,
+            columns,
+            array(columns.shape, F32),
+            array((BLOCK, BLOCK)),
+            array((1, BLOCK), F32),
+        ],
+        "prepare",
+        limit=24,
+    )(info, lengths, own, kv_other, q_own, q_other)
+    parts, prepared = lax.optimization_barrier((parts, prepared))
     total = call(totals_kernel, states, "ctx_totals")(info, lengths, *parts)
     places = lax.axis_size("ctx")
     slices = lax.all_to_all(total.reshape(places, -1, width), "ctx", 0, 0, tiled=True)
@@ -329,20 +390,17 @@
             [result, result],
             "solve",
             [
-                pltpu.VMEM((count, BLOCK + width, width), BF),
-                pltpu.VMEM((count, width, BLOCK), BF),
-                pltpu.VMEM((BLOCK, BLOCK), BF),
-                pltpu.VMEM((1, BLOCK), F32),
+                pltpu.VMEM((count, width, BLOCK + width), BF),
+                pltpu.VMEM((width, BLOCK), BF),
                 vectors,
                 vectors,
                 vectors,
                 vectors,
                 pltpu.VMEM((count, 1, BLOCK), F32),
             ],
-            scalars=3,
             flops=10**9 * count,
-            limit=24,
-        )(info, lengths, reg, kv_own, kv_other, q_own, q_other, *(before[s] for s in shifts))
+            limit=28,
+        )(info, reg, *prepared, *(before[s] for s in shifts))
         results += [mine, swap(others)]
     return call(
         unpack_kernel,

time: 119 us -> 111 us (0.933)
  blocking collectives: 15.6 us -> 36.8 us
  waiting for transfers between devices: 20.6 us -> 4.88 us
  starting transfers between devices: 28.6 us -> 17.3 us
  Pallas kernels: 51.4 us -> 49.1 us
    all_to_all x0 -> x1, blocking collectives: none -> 20.9 us  [body(): lax.all_to_all(total.reshape(places, -1, width), 'ctx', 0, 0, tiled=True)]
    all_to_all x1 -> x0, starting transfers between devices: 9.6 us -> none  [body(): lax.all_to_all(total.reshape(places, -1, width), 'ctx', 0, 0, tiled=True)]
    ppermute x6 -> x5, waiting for transfers between devices: 9.43 us -> 0.16 us  [along_x(): lax.ppermute(a, 'head', [(i, (i + 2 * shift) % (2 * NX)) for i in range(2...]
    pallas_call x15, Pallas kernels: 51.4 us -> 43.3 us  [run(): pl.pallas_call(kernel, in_specs=[SMEM] * scalars + [VMEM] * (len(args) -...]
    all_to_all x1 -> x0, waiting for transfers between devices: 7.78 us -> none  [body(): lax.all_to_all(total.reshape(places, -1, width), 'ctx', 0, 0, tiled=True)]
    pallas_call x0 -> x4, Pallas kernels: none -> 5.82 us  [pack(): pl.pallas_call(functools.partial(pack_kernel, first == 1), grid_spec=pltp...]
    ppermute x0 -> x2, waiting for transfers between devices: none -> 3.39 us  [relay(): return lax.ppermute(a, 'head', ring + back)]
    ppermute x6 -> x5, starting transfers between devices: 9.02 us -> 6.06 us  [along_x(): lax.ppermute(a, 'head', [(i, (i + 2 * shift) % (2 * NX)) for i in range(2...]
  transfers between devices with their start and end apart: 12 -> 12, of which waited for: 6 -> 3; matrix products, arithmetic and copies ran while one was open for 0% -> 0% of each run, Pallas kernels for 36% -> 35%
where the time goes in v4:
time: 111 us; the launch traced here: 110 us
  Pallas kernels  49.1 us (44%)
  blocking collectives  36.8 us (33%)
  starting transfers between devices  17.3 us (16%)
  waiting for transfers between devices  4.88 us (4%)
  local copies, waits for them, and re-layouts  1.9 us (2%)
    pallas_call x15, Pallas kernels, run(): pl.pallas_call(kernel, in_specs=[SMEM] * scalars + [VMEM] * (len(args) -...  43.3 us
    all_to_all x1, blocking collectives, body(): lax.all_to_all(total.reshape(places, -1, width), 'ctx', 0, 0, tiled=True)  20.9 us
    all_to_all x1, blocking collectives, body(): lax.all_to_all(entries, 'ctx', 0, 0, tiled=True).reshape(states.shape)  16 us
    ppermute x5, starting transfers between devices, swap(): return lax.ppermute(a, 'head', [(i, i ^ 1) for i in range(2 * NX)])  8.81 us
    ppermute x5, starting transfers between devices, along_x(): lax.ppermute(a, 'head', [(i, (i + 2 * shift) % (2 * NX)) for i in range(2...  6.06 us
    pallas_call x4, Pallas kernels, pack(): pl.pallas_call(functools.partial(pack_kernel, first == 1), grid_spec=pltp...  5.82 us
    ppermute x2, waiting for transfers between devices, relay(): return lax.ppermute(a, 'head', ring + back)  3.39 us
    ppermute x2, starting transfers between devices, relay(): return lax.ppermute(a, 'head', ring + back)  2.42 us
  transfers between devices with their start and end apart: 12, of which 3 were waited for; matrix products, arithmetic and copies ran while one was open for 0% of the time, Pallas kernels for 35%

profile of v4, /device:TPU:1, one launch (start us, length us, event | category | flops | bytes accessed | tf_op | source)
XLA Modules:
  0.0 110.2 jit_solution(17874651694534194950)
XLA Ops:
  0.0 1.9 %copy-done = bf16[128,3,32,128]{3,2,1,0:T(8,128)(2,1)S(1)} copy-done((bf16[128,3,32,128]{3,2,1,0:T(8,128)(2,1)S(1)}, bf16[128,3,32,128]{3,2,1,0:T(8,128)(2,1)}, u32[]{:S(2)}) %copy-start) | copy-done | bytes 3145752
  1.9 1.9 %pack.5 = bf16[2,16,128,128]{3,2,1,0:T(8,128)(2,1)S(1)} custom-call(s32[2]{0:T(128)S(1)} %compare_select_fusion.info, bf16[128,96,128]{2,1,0:T(8,128)(2,1)S(1)} %bitcast.3), custom_call_target="tpu_custom_call" | custom-call | tf_op jit(solution)/shard_map/pack/pallas_call | solution.py:109
  3.9 3.3 %collective-permute-start = (bf16[2,16,128,128]{3,2,1,0:T(8,128)(2,1)S(1)}, bf16[2,16,128,128]{3,2,1,0:T(8,128)(2,1)S(1)}, u32[]{:S(2)}, u32[]{:S(2)}) collective-permute-start(bf16[2,16,128,128]{3,2,1,0:T(8,128)(2,1)S(1)} %pack.5), channel_id=1, source_target_pairs={{0,1},{1,0},{2,3},{3,2},{4,5},{5,4},{6,7},{7,6},{8,9},{9,8},{10,11... | collective-permute-start | bytes 3145736 | tf_op jit(solution)/shard_map/ppermute | solution.py:324
  8.2 1.9 %pack.4.own.kv_own = bf16[2,16,128,128]{3,2,1,0:T(8,128)(2,1)S(1)} custom-call(s32[2]{0:T(128)S(1)} %compare_select_fusion.info, bf16[128,96,128]{2,1,0:T(8,128)(2,1)S(1)} %bitcast.5), custom_call_target="tpu_custom_call" | custom-call | tf_op jit(solution)/shard_map/pack/pallas_call | solution.py:109
  10.2 1.0 block_sums.4
  12.1 1.0 block_sums.6
  13.9 1.0 block_sums.7
  14.9 2.1 %collective-permute-start.4 = (bf16[4,2,128,128]{3,2,1,0:T(8,128)(2,1)S(1)}, bf16[4,2,128,128]{3,2,1,0:T(8,128)(2,1)S(1)}, u32[]{:S(2)}, u32[]{:S(2)}) collective-permute-start(bf16[4,2,128,128]{3,2,1,0:T(8,128)(2,1)S(1)} %block_sums.7), channel_id=1, source_target_pairs={{0,6},{1,7},{2,0},{3,1},{4,2},{5,3},{6,4},{7,5},{8,14},{9,15},{10,... | collective-permute-start | bytes 786440 | tf_op jit(solution)/shard_map/ppermute | solution.py:327
  16.9 1.6 %collective-permute-start.3 = (bf16[4,2,128,128]{3,2,1,0:T(8,128)(2,1)S(1)}, bf16[4,2,128,128]{3,2,1,0:T(8,128)(2,1)S(1)}, u32[]{:S(2)}, u32[]{:S(2)}) collective-permute-start(bf16[4,2,128,128]{3,2,1,0:T(8,128)(2,1)S(1)} %collective-permute-done.1), channel_id=1, source_target_pairs={{0,2},{2,4},{4,6},{6,0},{1,7},{3,1},{5,3},{7,5},{8,10},{10,12},{12... | collective-permute-start | bytes 786440 | tf_op jit(solution)/shard_map/ppermute | solution.py:334
  19.5 1.0 block_sums.5.p0
  20.5 2.0 %prepare.1 = (bf16[16,256,128]{2,1,0:T(8,128)(2,1)S(1)}, bf16[16,128,256]{2,1,0:T(8,128)(2,1)S(1)}, bf16[16,128,256]{2,1,0:T(8,128)(2,1)S(1)}, f32[16,128,256]{2...) custom-call(s32[2]{0:T(128)S(1)} %compare_select_fusion.info, s32[8]{0:T(128)S(1)} %copy-done.2, ...), custom_call_target="tpu_custom_call" | custom-call | bytes 3145768 | tf_op jit(solution)/shard_map/prepare/pallas_call | solution.py:33
  22.7 3.4 %collective-permute-done.3.p2 = bf16[4,2,128,128]{3,2,1,0:T(8,128)(2,1)S(1)} collective-permute-done((bf16[4,2,128,128]{3,2,1,0:T(8,128)(2,1)S(1)}, bf16[4,2,128,128]{3,2,1,0:T(8,128)(2,1)S(1)}, u32[]{:S(2)}, u32[]{:S(2)}) %collective-permute-start.3) | collective-permute-done | bytes 262176 | tf_op jit(solution)/shard_map/ppermute | solution.py:334
  27.0 20.9 %all_to_all.10.parts = bf16[32,32,128]{2,1,0:T(8,128)(2,1)S(1)} all-to-all(bf16[32,32,128]{2,1,0:T(8,128)(2,1)S(1)} %bitcast.11), channel_id=1, replica_groups=mesh['ctx'=32,'head'=8] {'ctx'}, dimensions={0} | all-to-all | bytes 524288 | tf_op jit(solution)/shard_map/all_to_all | solution.py:373
  47.9 1.1 %entries.1 = bf16[32,32,128]{2,1,0:T(8,128)(2,1)S(1)} custom-call(s32[2]{0:T(128)S(1)} %compare_select_fusion.info, s32[8]{0:T(128)S(1)} %copy-done.2, bf16[32,32,128]{2,1,0:T(8,128)(2,1)S(1)} %all_to_all.10.parts), custom_call_target="tpu_custom_call" | custom-call | bytes 262184 | tf_op jit(solution)/shard_map/entries/pallas_call | solution.py:33
  49.0 16.0 %all_to_all.11 = bf16[32,32,128]{2,1,0:T(8,128)(2,1)S(1)} all-to-all(bf16[32,32,128]{2,1,0:T(8,128)(2,1)S(1)} %entries.1), channel_id=1, replica_groups=mesh['ctx'=32,'head'=8] {'ctx'}, dimensions={0} | all-to-all | bytes 524288 | tf_op jit(solution)/shard_map/all_to_all | solution.py:375
  67.9 1.0 block_states.4.rest_0_
  68.9 1.4 %collective-permute-start.10 = (bf16[4,2,128,128]{3,2,1,0:T(8,128)(2,1)S(1)}, bf16[4,2,128,128]{3,2,1,0:T(8,128)(2,1)S(1)}, u32[]{:S(2)}, u32[]{:S(2)}) collective-permute-start(bf16[4,2,128,128]{3,2,1,0:T(8,128)(2,1)S(1)} %block_states.7), channel_id=1, source_target_pairs={{0,4},{1,5},{2,6},{3,7},{4,0},{5,1},{6,2},{7,3},{8,12},{9,13},{10,... | collective-permute-start | bytes 786440 | tf_op jit(solution)/shard_map/ppermute | solution.py:327
  70.3 1.3 %collective-permute-start.8 = (bf16[4,2,128,128]{3,2,1,0:T(8,128)(2,1)S(1)}, bf16[4,2,128,128]{3,2,1,0:T(8,128)(2,1)S(1)}, u32[]{:S(2)}, u32[]{:S(2)}) collective-permute-start(bf16[4,2,128,128]{3,2,1,0:T(8,128)(2,1)S(1)} %block_states.6), channel_id=1, source_target_pairs={{0,6},{1,7},{2,0},{3,1},{4,2},{5,3},{6,4},{7,5},{8,14},{9,15},{10,... | collective-permute-start | bytes 786440 | tf_op jit(solution)/shard_map/ppermute | solution.py:327
  72.1 8.0 %solve.3 = (bf16[4,128,128]{2,1,0:T(8,128)(2,1)S(1)}, bf16[4,128,128]{2,1,0:T(8,128)(2,1)S(1)}) custom-call(s32[2]{0:T(128)S(1)} %compare_select_fusion.info, f32[32]{0:T(128)S(1)} %copy-done.3, bf16[16,256,128]{2,1,0:T(8,128)(2,1)S(1)} %get-tuple-element.37.keys, bf16[16,128,256]{2,1,0:T(8,128)(2,1)S(1)} %get-tuple-element.38.key_t, ...), custom_call_target="tpu_custom_call" | custom-call | flops 4000000000 | bytes 5637256 | tf_op jit(solution)/shard_map/solve/pallas_call | solution.py:33
  80.1 4.4 %collective-permute-start.6 = (bf16[4,128,128]{2,1,0:T(8,128)(2,1)S(1)}, bf16[4,128,128]{2,1,0:T(8,128)(2,1)S(1)}, u32[]{:S(2)}, u32[]{:S(2)}) collective-permute-start(bf16[4,128,128]{2,1,0:T(8,128)(2,1)S(1)} %get-tuple-element.48), channel_id=1, source_target_pairs={{0,1},{1,0},{2,3},{3,2},{4,5},{5,4},{6,7},{7,6},{8,9},{9,8},{10,11... | collective-permute-start | bytes 393224 | tf_op jit(solution)/shard_map/ppermute | solution.py:324
  84.5 13.0 %solve.4 = (bf16[8,128,128]{2,1,0:T(8,128)(2,1)S(1)}, bf16[8,128,128]{2,1,0:T(8,128)(2,1)S(1)}) custom-call(s32[2]{0:T(128)S(1)} %compare_select_fusion.info, f32[32]{0:T(128)S(1)} %copy-done.3, bf16[16,256,128]{2,1,0:T(8,128)(2,1)S(1)} %get-tuple-element.37.keys, bf16[16,128,256]{2,1,0:T(8,128)(2,1)S(1)} %get-tuple-element.38.key_t, ...), custom_call_target="tpu_custom_call" | custom-call | flops 8000000000 | bytes 5899400 | tf_op jit(solution)/shard_map/solve/pallas_call | solution.py:33
  98.4 8.0 %solve.5 = (bf16[4,128,128]{2,1,0:T(8,128)(2,1)S(1)}, bf16[4,128,128]{2,1,0:T(8,128)(2,1)S(1)}) custom-call(s32[2]{0:T(128)S(1)} %compare_select_fusion.info, f32[32]{0:T(128)S(1)} %copy-done.3, bf16[16,256,128]{2,1,0:T(8,128)(2,1)S(1)} %get-tuple-element.37.keys, bf16[16,128,256]{2,1,0:T(8,128)(2,1)S(1)} %get-tuple-element.38.key_t, ...), custom_call_target="tpu_custom_call" | custom-call | flops 4000000000 | bytes 5637256 | tf_op jit(solution)/shard_map/solve/pallas_call | solution.py:33
  106.5 1.3 %collective-permute-done.11.rest_5_ = bf16[4,128,128]{2,1,0:T(8,128)(2,1)S(1)} collective-permute-done((bf16[4,128,128]{2,1,0:T(8,128)(2,1)S(1)}, bf16[4,128,128]{2,1,0:T(8,128)(2,1)S(1)}, u32[]{:S(2)}, u32[]{:S(2)}) %collective-permute-start.11) | collective-permute-done | bytes 131104 | tf_op jit(solution)/shard_map/ppermute | solution.py:324
  107.8 2.4 %unpack.1 = bf16[128,32,128]{2,1,0:T(8,128)(2,1)} custom-call(s32[2]{0:T(128)S(1)} %compare_select_fusion.info, bf16[4,128,128]{2,1,0:T(8,128)(2,1)S(1)} %get-tuple-element.47.rest_0_, bf16[4,128,128]{2,1,0:T(8,128)(2,1)S(1)} %collective-permute-done.6.rest_1_, bf16[8,128,128]{2,1,0:T(8,128)(2,1)S(1)} %get-tuple-element.49.rest_2_, ...), custom_call_target="tpu_custom_call" | custom-call | bytes 1048584 | tf_op jit(solution)/shard_map/unpack/pallas_call | solution.py:33
  (30 shorter events, 9.2 us)
Async XLA Ops:
  0.0 1.9 %copy-start = (bf16[128,3,32,128]{3,2,1,0:T(8,128)(2,1)S(1)}, bf16[128,3,32,128]{3,2,1,0:T(8,128)(2,1)}, u32[]{:S(2)}) copy-start(bf16[128,3,32,128]{3,2,1,0:T(8,128)(2,1)} %param.3) | copy-start | bytes 9437188
  3.8 6.3 %copy-start.2 = (s32[8]{0:T(128)S(1)}, s32[8]{0:T(128)}, u32[]{:S(2)}) copy-start(s32[8]{0:T(128)} %lengths.21) | copy-start | bytes 100
  3.9 6.3 %collective-permute-start = (bf16[2,16,128,128]{3,2,1,0:T(8,128)(2,1)S(1)}, bf16[2,16,128,128]{3,2,1,0:T(8,128)(2,1)S(1)}, u32[]{:S(2)}, u32[]{:S(2)}) collective-permute-start(bf16[2,16,128,128]{3,2,1,0:T(8,128)(2,1)S(1)} %pack.5), channel_id=1, source_target_pairs={{0,1},{1,0},{2,3},{3,2},{4,5},{5,4},{6,7},{7,6},{8,9},{9,8},{10,11... | collective-permute-start | bytes 3145736 | tf_op jit(solution)/shard_map/ppermute | solution.py:324
  8.1 12.4 %collective-permute-start.5 = (bf16[1,16,128,128]{3,2,1,0:T(8,128)(2,1)S(1)}, bf16[1,16,128,128]{3,2,1,0:T(8,128)(2,1)S(1)}, u32[]{:S(2)}, u32[]{:S(2)}) collective-permute-start(bf16[1,16,128,128]{3,2,1,0:T(8,128)(2,1)S(1)} %pack.7), channel_id=1, source_target_pairs={{0,1},{1,0},{2,3},{3,2},{4,5},{5,4},{6,7},{7,6},{8,9},{9,8},{10,11... | collective-permute-start | bytes 1572872 | tf_op jit(solution)/shard_map/ppermute | solution.py:324
  10.2 8.3 %copy-start.1 = (bf16[128,3,32,128]{3,2,1,0:T(8,128)(2,1)S(1)}, bf16[128,3,32,128]{3,2,1,0:T(8,128)(2,1)}, u32[]{:S(2)}) copy-start(bf16[128,3,32,128]{3,2,1,0:T(8,128)(2,1)} %param.3) | copy-start | bytes 9437188
  11.2 5.7 %collective-permute-start.1 = (bf16[4,2,128,128]{3,2,1,0:T(8,128)(2,1)S(1)}, bf16[4,2,128,128]{3,2,1,0:T(8,128)(2,1)S(1)}, u32[]{:S(2)}, u32[]{:S(2)}) collective-permute-start(bf16[4,2,128,128]{3,2,1,0:T(8,128)(2,1)S(1)} %block_sums.4), channel_id=1, source_target_pairs={{0,2},{2,4},{4,6},{6,0},{1,7},{3,1},{5,3},{7,5},{8,10},{10,12},{12... | collective-permute-start | bytes 786440 | tf_op jit(solution)/shard_map/ppermute | solution.py:334
  13.1 9.6 %collective-permute-start.2 = (bf16[4,2,128,128]{3,2,1,0:T(8,128)(2,1)S(1)}, bf16[4,2,128,128]{3,2,1,0:T(8,128)(2,1)S(1)}, u32[]{:S(2)}, u32[]{:S(2)}) collective-permute-start(bf16[4,2,128,128]{3,2,1,0:T(8,128)(2,1)S(1)} %block_sums.6), channel_id=1, source_target_pairs={{0,2},{1,3},{2,4},{3,5},{4,6},{5,7},{6,0},{7,1},{8,10},{9,11},{10,... | collective-permute-start | bytes 786440 | tf_op jit(solution)/shard_map/ppermute | solution.py:327
  14.9 7.8 %collective-permute-start.4 = (bf16[4,2,128,128]{3,2,1,0:T(8,128)(2,1)S(1)}, bf16[4,2,128,128]{3,2,1,0:T(8,128)(2,1)S(1)}, u32[]{:S(2)}, u32[]{:S(2)}) collective-permute-start(bf16[4,2,128,128]{3,2,1,0:T(8,128)(2,1)S(1)} %block_sums.7), channel_id=1, source_target_pairs={{0,6},{1,7},{2,0},{3,1},{4,2},{5,3},{6,4},{7,5},{8,14},{9,15},{10,... | collective-permute-start | bytes 786440 | tf_op jit(solution)/shard_map/ppermute | solution.py:327
  16.9 9.2 %collective-permute-start.3 = (bf16[4,2,128,128]{3,2,1,0:T(8,128)(2,1)S(1)}, bf16[4,2,128,128]{3,2,1,0:T(8,128)(2,1)S(1)}, u32[]{:S(2)}, u32[]{:S(2)}) collective-permute-start(bf16[4,2,128,128]{3,2,1,0:T(8,128)(2,1)S(1)} %collective-permute-done.1), channel_id=1, source_target_pairs={{0,2},{2,4},{4,6},{6,0},{1,7},{3,1},{5,3},{7,5},{8,10},{10,12},{12... | collective-permute-start | bytes 786440 | tf_op jit(solution)/shard_map/ppermute | solution.py:334
  65.0 7.1 %copy-start.3 = (f32[32]{0:T(128)S(1)}, f32[32]{0:T(128)}, u32[]{:S(2)}) copy-start(f32[32]{0:T(128)} %reg.5) | copy-start | bytes 388
  68.9 29.5 %collective-permute-start.10 = (bf16[4,2,128,128]{3,2,1,0:T(8,128)(2,1)S(1)}, bf16[4,2,128,128]{3,2,1,0:T(8,128)(2,1)S(1)}, u32[]{:S(2)}, u32[]{:S(2)}) collective-permute-start(bf16[4,2,128,128]{3,2,1,0:T(8,128)(2,1)S(1)} %block_states.7), channel_id=1, source_target_pairs={{0,4},{1,5},{2,6},{3,7},{4,0},{5,1},{6,2},{7,3},{8,12},{9,13},{10,... | collective-permute-start | bytes 786440 | tf_op jit(solution)/shard_map/ppermute | solution.py:327
  70.3 14.1 %collective-permute-start.8 = (bf16[4,2,128,128]{3,2,1,0:T(8,128)(2,1)S(1)}, bf16[4,2,128,128]{3,2,1,0:T(8,128)(2,1)S(1)}, u32[]{:S(2)}, u32[]{:S(2)}) collective-permute-start(bf16[4,2,128,128]{3,2,1,0:T(8,128)(2,1)S(1)} %block_states.6), channel_id=1, source_target_pairs={{0,6},{1,7},{2,0},{3,1},{4,2},{5,3},{6,4},{7,5},{8,14},{9,15},{10,... | collective-permute-start | bytes 786440 | tf_op jit(solution)/shard_map/ppermute | solution.py:327
  71.6 12.8 %collective-permute-start.7 = (bf16[4,2,128,128]{3,2,1,0:T(8,128)(2,1)S(1)}, bf16[4,2,128,128]{3,2,1,0:T(8,128)(2,1)S(1)}, u32[]{:S(2)}, u32[]{:S(2)}) collective-permute-start(bf16[4,2,128,128]{3,2,1,0:T(8,128)(2,1)S(1)} %block_states.5), channel_id=1, source_target_pairs={{0,2},{1,3},{2,4},{3,5},{4,6},{5,7},{6,0},{7,1},{8,10},{9,11},{10,... | collective-permute-start | bytes 786440 | tf_op jit(solution)/shard_map/ppermute | solution.py:327
  80.1 26.4 %collective-permute-start.6 = (bf16[4,128,128]{2,1,0:T(8,128)(2,1)S(1)}, bf16[4,128,128]{2,1,0:T(8,128)(2,1)S(1)}, u32[]{:S(2)}, u32[]{:S(2)}) collective-permute-start(bf16[4,128,128]{2,1,0:T(8,128)(2,1)S(1)} %get-tuple-element.48), channel_id=1, source_target_pairs={{0,1},{1,0},{2,3},{3,2},{4,5},{5,4},{6,7},{7,6},{8,9},{9,8},{10,11... | collective-permute-start | bytes 393224 | tf_op jit(solution)/shard_map/ppermute | solution.py:324
  97.5 10.3 %collective-permute-start.9 = (bf16[8,128,128]{2,1,0:T(8,128)(2,1)S(1)}, bf16[8,128,128]{2,1,0:T(8,128)(2,1)S(1)}, u32[]{:S(2)}, u32[]{:S(2)}) collective-permute-start(bf16[8,128,128]{2,1,0:T(8,128)(2,1)S(1)} %get-tuple-element.50), channel_id=1, source_target_pairs={{0,1},{1,0},{2,3},{3,2},{4,5},{5,4},{6,7},{7,6},{8,9},{9,8},{10,11... | collective-permute-start | bytes 786440 | tf_op jit(solution)/shard_map/ppermute | solution.py:324
  106.4 1.4 %collective-permute-start.11 = (bf16[4,128,128]{2,1,0:T(8,128)(2,1)S(1)}, bf16[4,128,128]{2,1,0:T(8,128)(2,1)S(1)}, u32[]{:S(2)}, u32[]{:S(2)}) collective-permute-start(bf16[4,128,128]{2,1,0:T(8,128)(2,1)S(1)} %get-tuple-element.52), channel_id=1, source_target_pairs={{0,1},{1,0},{2,3},{3,2},{4,5},{5,4},{6,7},{7,6},{8,9},{9,8},{10,11... | collective-permute-start | bytes 393224 | tf_op jit(solution)/shard_map/ppermute | solution.py:324

commit v5 on v4

--- a/solution.py
+++ b/solution.py
@@ -9,7 +9,7 @@
 from jax.sharding import PartitionSpec as P
 
 ITERS = 10
-UNROLL = 2
+UNROLL = 5
 GROUPS = ((0,), (1, 3), (2,))
 BLOCK = 256
 HD = 128
@@ -184,16 +184,26 @@
         running = same * running + parts[c].astype(F32)
 
 
-def states_kernel(shift, info, lengths, p0, p1, p2, p3, entry, out):
+def states_kernel(shifts, info, lengths, p0, p1, p2, p3, entry, *outs):
     x, _, _, _ = spot(info)
     docs = block_docs(info, lengths)
-    mine = lax.rem(x + shift, NX)
-    wanted = pick(docs[:NX], mine)
-    terms = [((docs[0] == wanted).astype(F32), entry)]
-    for back, part in enumerate((p0, p1, p2, p3)):
-        b = lax.rem(x - back + NX, NX)
-        terms.append((((b < mine) & (pick(docs[1:], b) == wanted)).astype(F32), part))
-    weighted(out, terms)
+    weights = []
+    for shift in shifts:
+        mine = lax.rem(x + shift, NX)
+        wanted = pick(docs[:NX], mine)
+        row = [(docs[0] == wanted).astype(F32)]
+        for back in range(NX):
+            b = lax.rem(x - back + NX, NX)
+            row.append(((b < mine) & (pick(docs[1:], b) == wanted)).astype(F32))
+        weights.append(row)
+    for j in range(PER):
+        for which in range(2):
+            parts = [part[j, which].astype(F32) for part in (entry, p0, p1, p2, p3)]
+            for row, out in zip(weights, outs):
+                total = row[0] * parts[0]
+                for weight, part in zip(row[1:], parts[1:]):
+                    total = total + weight * part
+                out[j, which] = rounded(total) if which == 0 else total.astype(BF)
 
 
 def prepare_kernel(
@@ -254,16 +264,18 @@
         return jnp.concatenate([scores(i, p), p * held_valid[...]], axis=0)
 
     def update(i, applied):
-        p = direction[i]
-        image = dot(lhs[i], applied) + diagonal[i] * p
-        old = norm[i]
-        step = old / (jnp.sum(p * image, axis=0, keepdims=True) + 1e-06)
-        solution[i] = solution[i] + step * p
-        r = residual[i] - step * image
-        residual[i] = r
-        new = jnp.sum(r * r, axis=0, keepdims=True)
-        direction[i] = r + (new / (old + 1e-06)) * p
-        norm[i] = new
+        product = dot(lhs[i], applied)
+        for c in (slice(0, BLOCK // 2), slice(BLOCK // 2, BLOCK)):
+            p = direction[i, :, c]
+            image = product[:, c] + diagonal[i, :, c] * p
+            old = norm[i, :, c]
+            step = old / (jnp.sum(p * image, axis=0, keepdims=True) + 1e-06)
+            solution[i, :, c] = solution[i, :, c] + step * p
+            r = residual[i, :, c] - step * image
+            residual[i, :, c] = r
+            new = jnp.sum(r * r, axis=0, keepdims=True)
+            direction[i, :, c] = r + (new / (old + 1e-06)) * p
+            norm[i, :, c] = new
 
     def staggered(first, second, total, lag):
         held = {}
@@ -274,7 +286,7 @@
                 second((t - lag) % count, held.pop(t - lag))
 
     def iterate(_, carried):
-        staggered(apply, update, UNROLL * count, 3)
+        staggered(apply, update, UNROLL * count, min(count, 4) - (count == 4))
         return carried
 
     def apply_last(i):
@@ -333,7 +345,7 @@
         back = [(2 * x + 1, 2 * ((x - 1) % NX) + 1) for x in range(NX)]
         return lax.ppermute(a, "head", ring + back)
 
-    flat = qkv.reshape(rows, 3 * heads, width)
+    flat = pltpu.with_memory_space_constraint(qkv.reshape(rows, 3 * heads, width), pltpu.HBM)
     kv_other = swap(pack(info, flat, 1, 2, True))
     q_other = swap(pack(info, flat, 0, 1, True))
     kv_own = pack(info, flat, 1, 2, False)
@@ -373,12 +385,11 @@
     slices = lax.all_to_all(total.reshape(places, -1, width), "ctx", 0, 0, tiled=True)
     entries = call(entries_kernel, array(slices.shape), "entries")(info, lengths, slices)
     entry = lax.all_to_all(entries, "ctx", 0, 0, tiled=True).reshape(states.shape)
-    before = [None] * NX
-    for shift in order:
-        part = call(functools.partial(states_kernel, shift), states, "block_states")(
-            info, lengths, *parts, entry
-        )
-        before[shift] = along_x(part, shift) if shift else part
+    near = (1, 3, 0)
+    made = call(functools.partial(states_kernel, near), [states] * 3, "block_states")(
+        info, lengths, *parts, entry
+    )
+    before = {shift: along_x(part, shift) if shift else part for shift, part in zip(near, made)}
 
     results = []
     for shifts in GROUPS:
@@ -401,6 +412,12 @@
             flops=10**9 * count,
             limit=28,
         )(info, reg, *prepared, *(before[s] for s in shifts))
+        if shifts == (0,):
+            entry, mine = lax.optimization_barrier((entry, mine))
+            (part,) = call(functools.partial(states_kernel, (2,)), [states], "block_states")(
+                info, lengths, *parts, entry
+            )
+            before[2] = along_x(part, 2)
         results += [mine, swap(others)]
     return call(
         unpack_kernel,

time: 111 us -> 108 us (0.973)
  local copies, waits for them, and re-layouts: 1.9 us -> 0.01 us
  waiting for transfers between devices: 4.88 us -> 3.5 us
    pallas_call x4, Pallas kernels: 5.82 us -> 9.77 us  [pack(): pl.pallas_call(functools.partial(pack_kernel, first == 1), grid_spec=pltp...]
    pallas_call x15 -> x13, Pallas kernels: 43.3 us -> 39.4 us  [run(): pl.pallas_call(kernel, in_specs=[SMEM] * scalars + [VMEM] * (len(args) -...]
    unnamed x8 -> x4, local copies, waits for them, and re-layouts: 1.9 us -> 0.01 us
  transfers between devices with their start and end apart: 12 -> 12, of which waited for: 3 -> 2; matrix products, arithmetic and copies ran while one was open for 0% -> 0% of each run, Pallas kernels for 35% -> 37%
where the time goes in v5:
time: 108 us; the launch traced here: 107 us
  Pallas kernels  49.2 us (46%)
  blocking collectives  36.8 us (34%)
  starting transfers between devices  17.7 us (16%)
  waiting for transfers between devices  3.5 us (3%)
    pallas_call x13, Pallas kernels, run(): pl.pallas_call(kernel, in_specs=[SMEM] * scalars + [VMEM] * (len(args) -...  39.4 us
    all_to_all x1, blocking collectives, body(): lax.all_to_all(total.reshape(places, -1, width), 'ctx', 0, 0, tiled=True)  20.9 us
    all_to_all x1, blocking collectives, body(): lax.all_to_all(entries, 'ctx', 0, 0, tiled=True).reshape(states.shape)  16 us
    pallas_call x4, Pallas kernels, pack(): pl.pallas_call(functools.partial(pack_kernel, first == 1), grid_spec=pltp...  9.77 us
    ppermute x5, starting transfers between devices, swap(): return lax.ppermute(a, 'head', [(i, i ^ 1) for i in range(2 * NX)])  8.34 us
    ppermute x5, starting transfers between devices, along_x(): lax.ppermute(a, 'head', [(i, (i + 2 * shift) % (2 * NX)) for i in range(2...  6.91 us
    ppermute x2, waiting for transfers between devices, relay(): return lax.ppermute(a, 'head', ring + back)  2.49 us
    ppermute x2, starting transfers between devices, relay(): return lax.ppermute(a, 'head', ring + back)  2.42 us
  transfers between devices with their start and end apart: 12, of which 2 were waited for; matrix products, arithmetic and copies ran while one was open for 0% of the time, Pallas kernels for 37%

profile of v5, /device:TPU:1, one launch (start us, length us, event | category | flops | bytes accessed | tf_op | source)
XLA Modules:
  0.0 107.3 jit_solution(11233661637658947282)
XLA Ops:
  0.0 2.9 %pack.5 = bf16[2,16,128,128]{3,2,1,0:T(8,128)(2,1)S(1)} custom-call(s32[2]{0:T(128)S(1)} %compare_select_fusion.info, bf16[128,96,128]{2,1,0:T(8,128)(2,1)} %bitcast.6), custom_call_target="tpu_custom_call" | custom-call | tf_op jit(solution)/shard_map/pack/pallas_call | solution.py:109
  2.9 3.3 %collective-permute-start = (bf16[2,16,128,128]{3,2,1,0:T(8,128)(2,1)S(1)}, bf16[2,16,128,128]{3,2,1,0:T(8,128)(2,1)S(1)}, u32[]{:S(2)}, u32[]{:S(2)}) collective-permute-start(bf16[2,16,128,128]{3,2,1,0:T(8,128)(2,1)S(1)} %pack.5), channel_id=1, source_target_pairs={{0,1},{1,0},{2,3},{3,2},{4,5},{5,4},{6,7},{7,6},{8,9},{9,8},{10,11... | collective-permute-start | bytes 3145736 | tf_op jit(solution)/shard_map/ppermute | solution.py:336
  6.2 2.0 %pack.7 = bf16[1,16,128,128]{3,2,1,0:T(8,128)(2,1)S(1)} custom-call(s32[2]{0:T(128)S(1)} %compare_select_fusion.info, bf16[128,96,128]{2,1,0:T(8,128)(2,1)} %bitcast.7), custom_call_target="tpu_custom_call" | custom-call | tf_op jit(solution)/shard_map/pack/pallas_call | solution.py:109
  8.3 2.9 %pack.4.own.kv_own = bf16[2,16,128,128]{3,2,1,0:T(8,128)(2,1)S(1)} custom-call(s32[2]{0:T(128)S(1)} %compare_select_fusion.info, bf16[128,96,128]{2,1,0:T(8,128)(2,1)} %bitcast.8), custom_call_target="tpu_custom_call" | custom-call | tf_op jit(solution)/shard_map/pack/pallas_call | solution.py:109
  11.2 1.0 block_sums.4
  13.1 1.0 block_sums.6
  14.9 1.0 block_sums.7
  15.9 2.1 %collective-permute-start.4 = (bf16[4,2,128,128]{3,2,1,0:T(8,128)(2,1)S(1)}, bf16[4,2,128,128]{3,2,1,0:T(8,128)(2,1)S(1)}, u32[]{:S(2)}, u32[]{:S(2)}) collective-permute-start(bf16[4,2,128,128]{3,2,1,0:T(8,128)(2,1)S(1)} %block_sums.7), channel_id=1, source_target_pairs={{0,6},{1,7},{2,0},{3,1},{4,2},{5,3},{6,4},{7,5},{8,14},{9,15},{10,... | collective-permute-start | bytes 786440 | tf_op jit(solution)/shard_map/ppermute | solution.py:339
  18.0 1.6 %collective-permute-start.3 = (bf16[4,2,128,128]{3,2,1,0:T(8,128)(2,1)S(1)}, bf16[4,2,128,128]{3,2,1,0:T(8,128)(2,1)S(1)}, u32[]{:S(2)}, u32[]{:S(2)}) collective-permute-start(bf16[4,2,128,128]{3,2,1,0:T(8,128)(2,1)S(1)} %collective-permute-done.1), channel_id=1, source_target_pairs={{0,2},{2,4},{4,6},{6,0},{1,7},{3,1},{5,3},{7,5},{8,10},{10,12},{12... | collective-permute-start | bytes 786440 | tf_op jit(solution)/shard_map/ppermute | solution.py:346
  19.5 2.0 %pack.6.q_own = bf16[1,16,128,128]{3,2,1,0:T(8,128)(2,1)S(1)} custom-call(s32[2]{0:T(128)S(1)} %compare_select_fusion.info, bf16[128,96,128]{2,1,0:T(8,128)(2,1)} %bitcast.9), custom_call_target="tpu_custom_call" | custom-call | tf_op jit(solution)/shard_map/pack/pallas_call | solution.py:109
  21.5 1.0 block_sums.5.p0
  22.6 2.0 %prepare.1 = (bf16[16,256,128]{2,1,0:T(8,128)(2,1)S(1)}, bf16[16,128,256]{2,1,0:T(8,128)(2,1)S(1)}, bf16[16,128,256]{2,1,0:T(8,128)(2,1)S(1)}, f32[16,128,256]{2...) custom-call(s32[2]{0:T(128)S(1)} %compare_select_fusion.info, s32[8]{0:T(128)S(1)} %copy-done, ...), custom_call_target="tpu_custom_call" | custom-call | bytes 3145768 | tf_op jit(solution)/shard_map/prepare/pallas_call | solution.py:33
  24.6 2.5 %collective-permute-done.3.p2 = bf16[4,2,128,128]{3,2,1,0:T(8,128)(2,1)S(1)} collective-permute-done((bf16[4,2,128,128]{3,2,1,0:T(8,128)(2,1)S(1)}, bf16[4,2,128,128]{3,2,1,0:T(8,128)(2,1)S(1)}, u32[]{:S(2)}, u32[]{:S(2)}) %collective-permute-start.3) | collective-permute-done | bytes 262176 | tf_op jit(solution)/shard_map/ppermute | solution.py:346
  28.0 20.9 %all_to_all.10.parts = bf16[32,32,128]{2,1,0:T(8,128)(2,1)S(1)} all-to-all(bf16[32,32,128]{2,1,0:T(8,128)(2,1)S(1)} %bitcast.5), channel_id=1, replica_groups=mesh['ctx'=32,'head'=8] {'ctx'}, dimensions={0} | all-to-all | bytes 524288 | tf_op jit(solution)/shard_map/all_to_all | solution.py:385
  48.9 1.1 %entries.1 = bf16[32,32,128]{2,1,0:T(8,128)(2,1)S(1)} custom-call(s32[2]{0:T(128)S(1)} %compare_select_fusion.info, s32[8]{0:T(128)S(1)} %copy-done, bf16[32,32,128]{2,1,0:T(8,128)(2,1)S(1)} %all_to_all.10.parts), custom_call_target="tpu_custom_call" | custom-call | bytes 262184 | tf_op jit(solution)/shard_map/entries/pallas_call | solution.py:33
  50.0 16.0 %all_to_all.11 = bf16[32,32,128]{2,1,0:T(8,128)(2,1)S(1)} all-to-all(bf16[32,32,128]{2,1,0:T(8,128)(2,1)S(1)} %entries.1), channel_id=1, replica_groups=mesh['ctx'=32,'head'=8] {'ctx'}, dimensions={0} | all-to-all | bytes 524288 | tf_op jit(solution)/shard_map/all_to_all | solution.py:387
  66.0 1.8 %block_states.2 = (bf16[4,2,128,128]{3,2,1,0:T(8,128)(2,1)S(1)}, bf16[4,2,128,128]{3,2,1,0:T(8,128)(2,1)S(1)}, bf16[4,2,128,128]{3,2,1,0:T(8,128)(2,1)S(1)}) custom-call(s32[2]{0:T(128)S(1)} %compare_select_fusion.info, s32[8]{0:T(128)S(1)} %copy-done, bf16[4,2,128,128]{3,2,1,0:T(8,128)(2,1)S(1)} %block_sums.5.p0, ...), custom_call_target="tpu_custom_call" | custom-call | bytes 1310760 | tf_op jit(solution)/shard_map/block_states/pallas_call | solution.py:33
  68.1 2.7 %collective-permute-start.8 = (bf16[4,2,128,128]{3,2,1,0:T(8,128)(2,1)S(1)}, bf16[4,2,128,128]{3,2,1,0:T(8,128)(2,1)S(1)}, u32[]{:S(2)}, u32[]{:S(2)}) collective-permute-start(bf16[4,2,128,128]{3,2,1,0:T(8,128)(2,1)S(1)} %get-tuple-element.57), channel_id=1, source_target_pairs={{0,6},{1,7},{2,0},{3,1},{4,2},{5,3},{6,4},{7,5},{8,14},{9,15},{10,... | collective-permute-start | bytes 786440 | tf_op jit(solution)/shard_map/ppermute | solution.py:339
  70.7 7.2 %solve.3 = (bf16[4,128,128]{2,1,0:T(8,128)(2,1)S(1)}, bf16[4,128,128]{2,1,0:T(8,128)(2,1)S(1)}) custom-call(s32[2]{0:T(128)S(1)} %compare_select_fusion.info, f32[32]{0:T(128)S(1)} %copy-done.1, bf16[16,256,128]{2,1,0:T(8,128)(2,1)S(1)} %get-tuple-element.46.keys, bf16[16,128,256]{2,1,0:T(8,128)(2,1)S(1)} %get-tuple-element.47.key_t, ...), custom_call_target="tpu_custom_call" | custom-call | flops 4000000000 | bytes 5637256 | tf_op jit(solution)/shard_map/solve/pallas_call | solution.py:33
  78.9 1.2 %collective-permute-start.10 = (bf16[4,2,128,128]{3,2,1,0:T(8,128)(2,1)S(1)}, bf16[4,2,128,128]{3,2,1,0:T(8,128)(2,1)S(1)}, u32[]{:S(2)}, u32[]{:S(2)}) collective-permute-start(bf16[4,2,128,128]{3,2,1,0:T(8,128)(2,1)S(1)} %block_states.3), channel_id=1, source_target_pairs={{0,4},{1,5},{2,6},{3,7},{4,0},{5,1},{6,2},{7,3},{8,12},{9,13},{10,... | collective-permute-start | bytes 786440 | tf_op jit(solution)/shard_map/ppermute | solution.py:339
  80.0 4.3 %collective-permute-start.6 = (bf16[4,128,128]{2,1,0:T(8,128)(2,1)S(1)}, bf16[4,128,128]{2,1,0:T(8,128)(2,1)S(1)}, u32[]{:S(2)}, u32[]{:S(2)}) collective-permute-start(bf16[4,128,128]{2,1,0:T(8,128)(2,1)S(1)} %get-tuple-element.55), channel_id=1, source_target_pairs={{0,1},{1,0},{2,3},{3,2},{4,5},{5,4},{6,7},{7,6},{8,9},{9,8},{10,11... | collective-permute-start | bytes 393224 | tf_op jit(solution)/shard_map/ppermute | solution.py:336
  84.3 11.8 %solve.4 = (bf16[8,128,128]{2,1,0:T(8,128)(2,1)S(1)}, bf16[8,128,128]{2,1,0:T(8,128)(2,1)S(1)}) custom-call(s32[2]{0:T(128)S(1)} %compare_select_fusion.info, f32[32]{0:T(128)S(1)} %copy-done.1, bf16[16,256,128]{2,1,0:T(8,128)(2,1)S(1)} %get-tuple-element.46.keys, bf16[16,128,256]{2,1,0:T(8,128)(2,1)S(1)} %get-tuple-element.47.key_t, ...), custom_call_target="tpu_custom_call" | custom-call | flops 8000000000 | bytes 5899400 | tf_op jit(solution)/shard_map/solve/pallas_call | solution.py:33
  96.2 7.2 %solve.5 = (bf16[4,128,128]{2,1,0:T(8,128)(2,1)S(1)}, bf16[4,128,128]{2,1,0:T(8,128)(2,1)S(1)}) custom-call(s32[2]{0:T(128)S(1)} %compare_select_fusion.info, f32[32]{0:T(128)S(1)} %copy-done.1, bf16[16,256,128]{2,1,0:T(8,128)(2,1)S(1)} %get-tuple-element.46.keys, bf16[16,128,256]{2,1,0:T(8,128)(2,1)S(1)} %get-tuple-element.47.key_t, ...), custom_call_target="tpu_custom_call" | custom-call | flops 4000000000 | bytes 5637256 | tf_op jit(solution)/shard_map/solve/pallas_call | solution.py:33
  105.0 2.4 %unpack.1 = bf16[128,32,128]{2,1,0:T(8,128)(2,1)} custom-call(s32[2]{0:T(128)S(1)} %compare_select_fusion.info, bf16[4,128,128]{2,1,0:T(8,128)(2,1)S(1)} %get-tuple-element.54.rest_0_, bf16[4,128,128]{2,1,0:T(8,128)(2,1)S(1)} %collective-permute-done.6.rest_1_, bf16[8,128,128]{2,1,0:T(8,128)(2,1)S(1)} %get-tuple-element.58.rest_2_, ...), custom_call_target="tpu_custom_call" | custom-call | bytes 1048584 | tf_op jit(solution)/shard_map/unpack/pallas_call | solution.py:33
  (24 shorter events, 5.6 us)
Async XLA Ops:
  2.9 8.3 %copy-start = (s32[8]{0:T(128)S(1)}, s32[8]{0:T(128)}, u32[]{:S(2)}) copy-start(s32[8]{0:T(128)} %lengths.17) | copy-start | bytes 100
  2.9 8.3 %collective-permute-start = (bf16[2,16,128,128]{3,2,1,0:T(8,128)(2,1)S(1)}, bf16[2,16,128,128]{3,2,1,0:T(8,128)(2,1)S(1)}, u32[]{:S(2)}, u32[]{:S(2)}) collective-permute-start(bf16[2,16,128,128]{3,2,1,0:T(8,128)(2,1)S(1)} %pack.5), channel_id=1, source_target_pairs={{0,1},{1,0},{2,3},{3,2},{4,5},{5,4},{6,7},{7,6},{8,9},{9,8},{10,11... | collective-permute-start | bytes 3145736 | tf_op jit(solution)/shard_map/ppermute | solution.py:336
  8.2 14.4 %collective-permute-start.5 = (bf16[1,16,128,128]{3,2,1,0:T(8,128)(2,1)S(1)}, bf16[1,16,128,128]{3,2,1,0:T(8,128)(2,1)S(1)}, u32[]{:S(2)}, u32[]{:S(2)}) collective-permute-start(bf16[1,16,128,128]{3,2,1,0:T(8,128)(2,1)S(1)} %pack.7), channel_id=1, source_target_pairs={{0,1},{1,0},{2,3},{3,2},{4,5},{5,4},{6,7},{7,6},{8,9},{9,8},{10,11... | collective-permute-start | bytes 1572872 | tf_op jit(solution)/shard_map/ppermute | solution.py:336
  12.2 5.7 %collective-permute-start.1 = (bf16[4,2,128,128]{3,2,1,0:T(8,128)(2,1)S(1)}, bf16[4,2,128,128]{3,2,1,0:T(8,128)(2,1)S(1)}, u32[]{:S(2)}, u32[]{:S(2)}) collective-permute-start(bf16[4,2,128,128]{3,2,1,0:T(8,128)(2,1)S(1)} %block_sums.4), channel_id=1, source_target_pairs={{0,2},{2,4},{4,6},{6,0},{1,7},{3,1},{5,3},{7,5},{8,10},{10,12},{12... | collective-permute-start | bytes 786440 | tf_op jit(solution)/shard_map/ppermute | solution.py:346
  14.1 10.5 %collective-permute-start.2 = (bf16[4,2,128,128]{3,2,1,0:T(8,128)(2,1)S(1)}, bf16[4,2,128,128]{3,2,1,0:T(8,128)(2,1)S(1)}, u32[]{:S(2)}, u32[]{:S(2)}) collective-permute-start(bf16[4,2,128,128]{3,2,1,0:T(8,128)(2,1)S(1)} %block_sums.6), channel_id=1, source_target_pairs={{0,2},{1,3},{2,4},{3,5},{4,6},{5,7},{6,0},{7,1},{8,10},{9,11},{10,... | collective-permute-start | bytes 786440 | tf_op jit(solution)/shard_map/ppermute | solution.py:339
  15.9 8.7 %collective-permute-start.4 = (bf16[4,2,128,128]{3,2,1,0:T(8,128)(2,1)S(1)}, bf16[4,2,128,128]{3,2,1,0:T(8,128)(2,1)S(1)}, u32[]{:S(2)}, u32[]{:S(2)}) collective-permute-start(bf16[4,2,128,128]{3,2,1,0:T(8,128)(2,1)S(1)} %block_sums.7), channel_id=1, source_target_pairs={{0,6},{1,7},{2,0},{3,1},{4,2},{5,3},{6,4},{7,5},{8,14},{9,15},{10,... | collective-permute-start | bytes 786440 | tf_op jit(solution)/shard_map/ppermute | solution.py:339
  18.0 9.2 %collective-permute-start.3 = (bf16[4,2,128,128]{3,2,1,0:T(8,128)(2,1)S(1)}, bf16[4,2,128,128]{3,2,1,0:T(8,128)(2,1)S(1)}, u32[]{:S(2)}, u32[]{:S(2)}) collective-permute-start(bf16[4,2,128,128]{3,2,1,0:T(8,128)(2,1)S(1)} %collective-permute-done.1), channel_id=1, source_target_pairs={{0,2},{2,4},{4,6},{6,0},{1,7},{3,1},{5,3},{7,5},{8,10},{10,12},{12... | collective-permute-start | bytes 786440 | tf_op jit(solution)/shard_map/ppermute | solution.py:346
  22.5 48.2 %copy-start.1 = (f32[32]{0:T(128)S(1)}, f32[32]{0:T(128)}, u32[]{:S(2)}) copy-start(f32[32]{0:T(128)} %reg.5) | copy-start | bytes 388
  67.8 16.5 %collective-permute-start.7 = (bf16[4,2,128,128]{3,2,1,0:T(8,128)(2,1)S(1)}, bf16[4,2,128,128]{3,2,1,0:T(8,128)(2,1)S(1)}, u32[]{:S(2)}, u32[]{:S(2)}) collective-permute-start(bf16[4,2,128,128]{3,2,1,0:T(8,128)(2,1)S(1)} %get-tuple-element.56), channel_id=1, source_target_pairs={{0,2},{1,3},{2,4},{3,5},{4,6},{5,7},{6,0},{7,1},{8,10},{9,11},{10,... | collective-permute-start | bytes 786440 | tf_op jit(solution)/shard_map/ppermute | solution.py:339
  68.1 16.2 %collective-permute-start.8 = (bf16[4,2,128,128]{3,2,1,0:T(8,128)(2,1)S(1)}, bf16[4,2,128,128]{3,2,1,0:T(8,128)(2,1)S(1)}, u32[]{:S(2)}, u32[]{:S(2)}) collective-permute-start(bf16[4,2,128,128]{3,2,1,0:T(8,128)(2,1)S(1)} %get-tuple-element.57), channel_id=1, source_target_pairs={{0,6},{1,7},{2,0},{3,1},{4,2},{5,3},{6,4},{7,5},{8,14},{9,15},{10,... | collective-permute-start | bytes 786440 | tf_op jit(solution)/shard_map/ppermute | solution.py:339
  78.9 17.3 %collective-permute-start.10 = (bf16[4,2,128,128]{3,2,1,0:T(8,128)(2,1)S(1)}, bf16[4,2,128,128]{3,2,1,0:T(8,128)(2,1)S(1)}, u32[]{:S(2)}, u32[]{:S(2)}) collective-permute-start(bf16[4,2,128,128]{3,2,1,0:T(8,128)(2,1)S(1)} %block_states.3), channel_id=1, source_target_pairs={{0,4},{1,5},{2,6},{3,7},{4,0},{5,1},{6,2},{7,3},{8,12},{9,13},{10,... | collective-permute-start | bytes 786440 | tf_op jit(solution)/shard_map/ppermute | solution.py:339
  80.0 23.9 %collective-permute-start.6 = (bf16[4,128,128]{2,1,0:T(8,128)(2,1)S(1)}, bf16[4,128,128]{2,1,0:T(8,128)(2,1)S(1)}, u32[]{:S(2)}, u32[]{:S(2)}) collective-permute-start(bf16[4,128,128]{2,1,0:T(8,128)(2,1)S(1)} %get-tuple-element.55), channel_id=1, source_target_pairs={{0,1},{1,0},{2,3},{3,2},{4,5},{5,4},{6,7},{7,6},{8,9},{9,8},{10,11... | collective-permute-start | bytes 393224 | tf_op jit(solution)/shard_map/ppermute | solution.py:336
  96.1 8.8 %collective-permute-start.9 = (bf16[8,128,128]{2,1,0:T(8,128)(2,1)S(1)}, bf16[8,128,128]{2,1,0:T(8,128)(2,1)S(1)}, u32[]{:S(2)}, u32[]{:S(2)}) collective-permute-start(bf16[8,128,128]{2,1,0:T(8,128)(2,1)S(1)} %get-tuple-element.59), channel_id=1, source_target_pairs={{0,1},{1,0},{2,3},{3,2},{4,5},{5,4},{6,7},{7,6},{8,9},{9,8},{10,11... | collective-permute-start | bytes 786440 | tf_op jit(solution)/shard_map/ppermute | solution.py:336
  103.4 1.6 %collective-permute-start.11 = (bf16[4,128,128]{2,1,0:T(8,128)(2,1)S(1)}, bf16[4,128,128]{2,1,0:T(8,128)(2,1)S(1)}, u32[]{:S(2)}, u32[]{:S(2)}) collective-permute-start(bf16[4,128,128]{2,1,0:T(8,128)(2,1)S(1)} %get-tuple-element.62), channel_id=1, source_target_pairs={{0,1},{1,0},{2,3},{3,2},{4,5},{5,4},{6,7},{7,6},{8,9},{9,8},{10,11... | collective-permute-start | bytes 393224 | tf_op jit(solution)/shard_map/ppermute | solution.py:336

commit v6 on v5

--- a/solution.py
+++ b/solution.py
@@ -8,13 +8,13 @@
 from jax.experimental.pallas import tpu as pltpu
 from jax.sharding import PartitionSpec as P
 
+
 ITERS = 10
 UNROLL = 5
 GROUPS = ((0,), (1, 3), (2,))
 BLOCK = 256
 HD = 128
 NX = 4
-NY = 4
 NZ = 8
 PER = 4
 F32 = jnp.float32
@@ -27,18 +27,16 @@
     return lax.dot_general(a, b, (((1,), (0,)), ((), ())), preferred_element_type=F32)
 
 
-def call(kernel, outs, name, scratch=(), scalars=2, flops=0, limit=16):
+def call(kernel, outs, scratch=(), scalars=2, flops=0, limit=16):
     def run(*args):
-        moved = sum(math.prod(s) * d.dtype.itemsize for s, d in ((a.shape, a) for a in args))
         return pl.pallas_call(
             kernel,
             in_specs=[SMEM] * scalars + [VMEM] * (len(args) - scalars),
             out_specs=jax.tree.map(lambda _: VMEM, outs),
             out_shape=outs,
             scratch_shapes=list(scratch),
-            cost_estimate=pl.CostEstimate(flops=flops, bytes_accessed=moved, transcendentals=0),
+            cost_estimate=pl.CostEstimate(flops=flops, bytes_accessed=1 << 10, transcendentals=0),
             compiler_params=pltpu.CompilerParams(vmem_limit_bytes=limit << 20),
-            name=name,
         )(*args)
 
     return run
@@ -85,38 +83,44 @@
 
 
 def pack_kernel(keys_first, info, x_ref, out_ref, stage):
-    rows = x_ref.shape[0]
+    rows, count, _ = x_ref.shape
     part = x_ref[...].astype(F32)
-    stage[...] = part.reshape(rows * 16, HD)
+    stage[...] = part.reshape(rows * count, HD)
     if keys_first:
 
         @pl.when(pl.program_id(0) == 0)
         def _():
             scale = lax.rsqrt(jnp.mean(part * part, axis=-1, keepdims=True) + 1e-06)
-            stage[...] = (part * scale / math.sqrt(HD)).reshape(rows * 16, HD)
-
-    for h in range(16):
-        out_ref[0, h] = stage[pl.ds(h, rows, stride=16), :].astype(BF)
-
-
-def pack(info, qkv, first, count, other):
+            stage[...] = (part * scale / math.sqrt(HD)).reshape(rows * count, HD)
+
+    for h in range(count):
+        out_ref[0, h] = stage[pl.ds(h, rows, stride=count), :].astype(BF)
+
+
+def pack(info, qkv, kinds, count, other, far=False):
     rows = qkv.shape[0]
 
     def place(g, info):
         core = info[0] % 2
-        return 0, 2 * (first + g) + (1 - core if other else core), 0
+        core = 1 - core if other else core
+        if count == 16:
+            return 0, 2 * kinds[0] + core, 0
+        pair = info[0] // 4
+        pair = 1 - pair if far else pair
+        return 0, 4 * (kinds[0] + g) + 2 * core + pair, 0
 
     return pl.pallas_call(
-        functools.partial(pack_kernel, first == 1),
+        functools.partial(pack_kernel, kinds[0] == 1),
         grid_spec=pltpu.PrefetchScalarGridSpec(
             num_scalar_prefetch=1,
-            grid=(count,),
-            in_specs=[pl.BlockSpec((rows, 16, HD), place)],
-            out_specs=pl.BlockSpec((1, 16, rows, HD), lambda g, info: (g, 0, 0, 0)),
-            scratch_shapes=[pltpu.VMEM((rows * 16, HD), F32)],
+            grid=(len(kinds),),
+            in_specs=[pl.BlockSpec((rows, count, HD), place)],
+            out_specs=pl.BlockSpec((1, count, rows, HD), lambda g, info: (g, 0, 0, 0)),
+            scratch_shapes=[pltpu.VMEM((rows * count, HD), F32)],
         ),
-        out_shape=jax.ShapeDtypeStruct((count, 16, rows, HD), BF),
+        out_shape=jax.ShapeDtypeStruct((len(kinds), count, rows, HD), BF),
         compiler_params=pltpu.CompilerParams(vmem_limit_bytes=12 << 20),
+        cost_estimate=pl.CostEstimate(flops=0, bytes_accessed=1 << 10, transcendentals=0),
         name="pack",
     )(info, qkv)
 
@@ -127,7 +131,7 @@
     last = (info[1] * NX + x + 1) * BLOCK - 1
     tail = (doc_of(lengths, place) == doc_of(lengths, last)).astype(F32).astype(BF)
     for j in range(PER):
-        h = lax.rem(x + shift, NX) * PER + j
+        h = ((x ^ shift) % 2) * PER + j
         k = jnp.concatenate([own[0, h], other[0, h]], axis=0)
         v = jnp.concatenate([own[1, h], other[1, h]], axis=0)
         out[j, 0] = rounded(started(dot(k.T * tail, k)))
@@ -160,7 +164,7 @@
     docs = block_docs(info, lengths)
     terms = []
     for shift, part in enumerate((p0, p1, p2, p3)):
-        doc = pick(docs[1:], lax.rem(x - shift + NX, NX))
+        doc = pick(docs[1:], (x ^ shift))
         terms.append(((doc == docs[NX]).astype(F32), part))
     weighted(out, terms)
 
@@ -189,11 +193,11 @@
     docs = block_docs(info, lengths)
     weights = []
     for shift in shifts:
-        mine = lax.rem(x + shift, NX)
+        mine = x ^ shift
         wanted = pick(docs[:NX], mine)
         row = [(docs[0] == wanted).astype(F32)]
         for back in range(NX):
-            b = lax.rem(x - back + NX, NX)
+            b = x ^ back
             row.append(((b < mine) & (pick(docs[1:], b) == wanted)).astype(F32))
         weights.append(row)
     for j in range(PER):
@@ -207,7 +211,8 @@
 
 
 def prepare_kernel(
-    info, lengths, kv_own, kv_other, q_own, q_other, keys, key_t, value_t, query, same, valid
+    info, lengths, far_own, far_other, near_own, near_other, q_own, q_other,
+    keys, key_t, value_t, query, same, valid,
 ):
     x, _, _, _ = spot(info)
     before = doc_of(lengths, (info[1] * NX + x) * BLOCK - 1)
@@ -217,18 +222,23 @@
     valid[...] = (lane_doc == before).astype(F32)
     same[...] = ((doc_of(lengths, row) == lane_doc) & (row <= lane)).astype(F32).astype(BF)
 
-    def one(pair, carried):
-        for h in (2 * pair, 2 * pair + 1):
-            k = jnp.concatenate([kv_own[0, h], kv_other[0, h]], axis=0)
-            keys[h] = k
-            key_t[h] = k.T
-            value_t[h] = jnp.concatenate([kv_own[1, h], kv_other[1, h]], axis=0).T
-            q = jnp.concatenate([q_own[0, h], q_other[0, h]], axis=0).T.astype(F32)
-            scale = lax.rsqrt(jnp.mean(q * q, axis=0, keepdims=True) + 1e-06)
-            query[h] = q * scale / math.sqrt(HD)
-        return carried
-
-    lax.fori_loop(0, keys.shape[0] // 2, one, 0)
+    for far in range(2):
+        own, other = ((near_own, near_other), (far_own, far_other))[far]
+        base = 2 * PER * ((x // 2) ^ far)
+
+        def one(pair, carried):
+            for i in (2 * pair, 2 * pair + 1):
+                h = base + i
+                k = jnp.concatenate([own[0, i], other[0, i]], axis=0)
+                keys[h] = k
+                key_t[h] = k.T
+                value_t[h] = jnp.concatenate([own[1, i], other[1, i]], axis=0).T
+                q = jnp.concatenate([q_own[0, h], q_other[0, h]], axis=0).T.astype(F32)
+                scale = lax.rsqrt(jnp.mean(q * q, axis=0, keepdims=True) + 1e-06)
+                query[h] = q * scale / math.sqrt(HD)
+            return carried
+
+        lax.fori_loop(0, PER, one, 0)
 
 
 def solve_kernel(shifts, info, reg, keys, key_t, value_t, query, same, valid, *rest):
@@ -238,7 +248,8 @@
     held_valid[...] = jnp.broadcast_to(valid[...], (HD, BLOCK)).astype(BF)
     eye, beside = diagonals()
     count = len(shifts) * PER
-    head = [lax.rem(x - shifts[i // PER] + NX, NX) * PER + i % PER for i in range(count)]
+    unroll = UNROLL if count > PER else ITERS
+    head = [(x ^ shifts[i // PER]) * PER + i % PER for i in range(count)]
 
     def state(i, which):
         return states[i // PER][i % PER, which]
@@ -286,7 +297,7 @@
                 second((t - lag) % count, held.pop(t - lag))
 
     def iterate(_, carried):
-        staggered(apply, update, UNROLL * count, min(count, 4) - (count == 4))
+        staggered(apply, update, unroll * count, 3 if count > PER else 2)
         return carried
 
     def apply_last(i):
@@ -304,7 +315,7 @@
         out_own[i] = result[0 : BLOCK // 2]
         out_other[i] = result[BLOCK // 2 :]
 
-    lax.fori_loop(0, ITERS // UNROLL, iterate, 0)
+    lax.fori_loop(0, ITERS // unroll, iterate, 0)
     staggered(apply_last, finish, count, 2)
 
 
@@ -316,7 +327,7 @@
         for g, shifts in enumerate(GROUPS):
             part = parts[2 * g + other]
             for i in range(len(shifts) * PER):
-                h = lax.rem(x - shifts[i // PER] + NX, NX) * PER + i % PER
+                h = (x ^ shifts[i // PER]) * PER + i % PER
                 stage[pl.ds(h, rows, stride=16), :] = part[i].astype(F32)
         half = core if other == 0 else 1 - core
         first = pl.multiple_of(half * 16, 16)
@@ -337,7 +348,7 @@
 
     def along_x(a, shift):
         return lax.ppermute(
-            a, "head", [(i, (i + 2 * shift) % (2 * NX)) for i in range(2 * NX)]
+            a, "head", [(i, 2 * ((i // 2) ^ shift) + i % 2) for i in range(2 * NX)]
         )
 
     def relay(a):
@@ -345,26 +356,37 @@
         back = [(2 * x + 1, 2 * ((x - 1) % NX) + 1) for x in range(NX)]
         return lax.ppermute(a, "head", ring + back)
 
-    flat = pltpu.with_memory_space_constraint(qkv.reshape(rows, 3 * heads, width), pltpu.HBM)
-    kv_other = swap(pack(info, flat, 1, 2, True))
-    q_other = swap(pack(info, flat, 0, 1, True))
-    kv_own = pack(info, flat, 1, 2, False)
-    q_own = pack(info, flat, 0, 1, False)
+    def after(a, *others):
+        return lax.optimization_barrier((a, *others))[0]
+
+    flat = qkv.reshape(rows, 3 * heads, width)
+    first = pltpu.with_memory_space_constraint(flat, pltpu.HBM)
+    key_value, query = (1, 2), (0,)
+    far_send = pack(info, first, key_value, 8, True, True)
+    far_other = swap(far_send)
+    far_own = pack(after(info, far_send), flat, key_value, 8, False, True)
+    near_send = pack(after(info, far_own), flat, key_value, 8, True)
+    near_other = swap(near_send)
 
     states = array((PER, 2, width, width))
-    order = (2, 1, 3, 0)
+
+    def sums(shift, own, other):
+        return call(functools.partial(sums_kernel, shift), states)(info, lengths, own, other)
+
     parts = [None] * NX
-    own = kv_own
-    for shift in order:
-        if shift == 0:
-            own, parts[2] = lax.optimization_barrier((own, parts[2]))
-            parts[2] = relay(parts[2])
-        part = call(functools.partial(sums_kernel, shift), states, "block_sums")(
-            info, lengths, own, kv_other
-        )
-        if shift:
-            part = relay(part) if shift == 2 else along_x(part, shift)
-        parts[shift] = part
+    hop = sums(2, after(far_own, near_send), far_other)
+    parts[2] = relay(hop)
+    third = sums(3, after(far_own, hop), far_other)
+    parts[3] = along_x(third, 3)
+    near_own = pack(after(info, third), flat, key_value, 8, False)
+    second = sums(1, near_own, near_other)
+    parts[1] = along_x(second, 1)
+    parts[2] = relay(parts[2])
+    late = after(info, second)
+    q_send = pack(late, flat, query, 16, True)
+    q_other = swap(q_send)
+    q_own = pack(after(info, q_send), flat, query, 16, False)
+    parts[0] = sums(0, after(near_own, second), near_other)
     columns = array((half, width, BLOCK))
     prepared = call(
         prepare_kernel,
@@ -376,19 +398,16 @@
             array((BLOCK, BLOCK)),
             array((1, BLOCK), F32),
         ],
-        "prepare",
         limit=24,
-    )(info, lengths, own, kv_other, q_own, q_other)
+    )(info, lengths, far_own, far_other, near_own, near_other, q_own, q_other)
     parts, prepared = lax.optimization_barrier((parts, prepared))
-    total = call(totals_kernel, states, "ctx_totals")(info, lengths, *parts)
+    total = call(totals_kernel, states)(info, lengths, *parts)
     places = lax.axis_size("ctx")
     slices = lax.all_to_all(total.reshape(places, -1, width), "ctx", 0, 0, tiled=True)
-    entries = call(entries_kernel, array(slices.shape), "entries")(info, lengths, slices)
+    entries = call(entries_kernel, array(slices.shape))(info, lengths, slices)
     entry = lax.all_to_all(entries, "ctx", 0, 0, tiled=True).reshape(states.shape)
     near = (1, 3, 0)
-    made = call(functools.partial(states_kernel, near), [states] * 3, "block_states")(
-        info, lengths, *parts, entry
-    )
+    made = call(functools.partial(states_kernel, near), [states] * 3)(info, lengths, *parts, entry)
     before = {shift: along_x(part, shift) if shift else part for shift, part in zip(near, made)}
 
     results = []
@@ -399,7 +418,6 @@
         mine, others = call(
             functools.partial(solve_kernel, shifts),
             [result, result],
-            "solve",
             [
                 pltpu.VMEM((count, width, BLOCK + width), BF),
                 pltpu.VMEM((width, BLOCK), BF),
@@ -414,7 +432,7 @@
         )(info, reg, *prepared, *(before[s] for s in shifts))
         if shifts == (0,):
             entry, mine = lax.optimization_barrier((entry, mine))
-            (part,) = call(functools.partial(states_kernel, (2,)), [states], "block_states")(
+            (part,) = call(functools.partial(states_kernel, (2,)), [states])(
                 info, lengths, *parts, entry
             )
             before[2] = along_x(part, 2)
@@ -422,7 +440,6 @@
     return call(
         unpack_kernel,
         array((rows, heads, width)),
-        "unpack",
         [pltpu.VMEM((rows * half, width), F32)],
         scalars=1,
     )(info, *results)
@@ -431,4 +448,5 @@
 def solution(mesh):
     in_specs = (P(("ctx", "head"), None, None, None), P(), P())
     out_specs = P(("ctx", "head"), None, None)
+
     return jax.shard_map(body, mesh=mesh, in_specs=in_specs, out_specs=out_specs, check_vma=False)

time: 108 us -> 105 us (0.972)
  waiting for transfers between devices: 3.5 us -> 9.29 us
  Pallas kernels: 49.2 us -> 45.5 us
  blocking collectives: 36.8 us -> 33.5 us
  starting transfers between devices: 17.7 us -> 16.3 us
    ppermute x2, waiting for transfers between devices: 2.49 us -> 8.29 us  [relay(): return lax.ppermute(a, 'head', ring + back)]
    pallas_call x13, Pallas kernels: 39.4 us -> 37.5 us  [run(): pl.pallas_call(kernel, in_specs=[SMEM] * scalars + [VMEM] * (len(args) -...]
    pallas_call x4 -> x6, Pallas kernels: 9.77 us -> 8 us  [pack(): pl.pallas_call(functools.partial(pack_kernel, kinds[0] == 1), grid_spec=p...]
    all_to_all x1, blocking collectives: 16 us -> 14.2 us  [body(): lax.all_to_all(entries, 'ctx', 0, 0, tiled=True).reshape(states.shape)]
    ppermute x2, starting transfers between devices: 2.42 us -> 0.78 us  [relay(): return lax.ppermute(a, 'head', ring + back)]
    all_to_all x1, blocking collectives: 20.9 us -> 19.2 us  [body(): lax.all_to_all(total.reshape(places, -1, width), 'ctx', 0, 0, tiled=True)]
    ppermute x5 -> x6, starting transfers between devices: 8.34 us -> 8.85 us  [swap(): return lax.ppermute(a, 'head', [(i, i ^ 1) for i in range(2 * NX)])]
  transfers between devices with their start and end apart: 12 -> 13, of which waited for: 2 -> 3; matrix products, arithmetic and copies ran while one was open for 0% -> 0% of each run, Pallas kernels for 37% -> 33%
where the time goes in v6:
time: 105 us
  Pallas kernels  45.5 us (43%)
  blocking collectives  33.5 us (32%)
  starting transfers between devices  16.3 us (16%)
  waiting for transfers between devices  9.29 us (9%)
    pallas_call x13, Pallas kernels, run(): pl.pallas_call(kernel, in_specs=[SMEM] * scalars + [VMEM] * (len(args) -...  37.5 us
    all_to_all x1, blocking collectives, body(): lax.all_to_all(total.reshape(places, -1, width), 'ctx', 0, 0, tiled=True)  19.2 us
    all_to_all x1, blocking collectives, body(): lax.all_to_all(entries, 'ctx', 0, 0, tiled=True).reshape(states.shape)  14.2 us
    ppermute x6, starting transfers between devices, swap(): return lax.ppermute(a, 'head', [(i, i ^ 1) for i in range(2 * NX)])  8.85 us
    ppermute x2, waiting for transfers between devices, relay(): return lax.ppermute(a, 'head', ring + back)  8.29 us
    pallas_call x6, Pallas kernels, pack(): pl.pallas_call(functools.partial(pack_kernel, kinds[0] == 1), grid_spec=p...  8 us
    ppermute x5, starting transfers between devices, along_x(): lax.ppermute(a, 'head', [(i, 2 * (i // 2 ^ shift) + i % 2) for i in range...  6.71 us
  transfers between devices with their start and end apart: 13, of which 3 were waited for; matrix products, arithmetic and copies ran while one was open for 0% of the time, Pallas kernels for 33%

profile of v6, /device:TPU:1, one launch (start us, length us, event | category | flops | bytes accessed | tf_op | source)
XLA Modules:
  0.0 104.8 jit_solution(6939679398179777045)
XLA Ops:
  0.0 2.3 %pack.6 = bf16[2,8,128,128]{3,2,1,0:T(8,128)(2,1)S(1)} custom-call(s32[2]{0:T(128)S(1)} %compare_select_fusion.info, bf16[128,96,128]{2,1,0:T(8,128)(2,1)} %bitcast.3), custom_call_target="tpu_custom_call" | custom-call | bytes 1024 | tf_op jit(solution)/shard_map/pack/pallas_call | solution.py:112
  2.4 3.3 %collective-permute-start = (bf16[2,8,128,128]{3,2,1,0:T(8,128)(2,1)S(1)}, bf16[2,8,128,128]{3,2,1,0:T(8,128)(2,1)S(1)}, u32[]{:S(2)}, u32[]{:S(2)}) collective-permute-start(bf16[2,8,128,128]{3,2,1,0:T(8,128)(2,1)S(1)} %pack.6), channel_id=1, source_target_pairs={{0,1},{1,0},{2,3},{3,2},{4,5},{5,4},{6,7},{7,6},{8,9},{9,8},{10,11... | collective-permute-start | bytes 1572872 | tf_op jit(solution)/shard_map/ppermute | solution.py:347
  5.6 1.2 %pack.7.own.far_own = bf16[2,8,128,128]{3,2,1,0:T(8,128)(2,1)S(1)} custom-call(s32[2]{0:T(128)S(1)} %compare_select_fusion.info, bf16[128,96,128]{2,1,0:T(8,128)(2,1)S(1)} %bitcast.4), custom_call_target="tpu_custom_call" | custom-call | bytes 1024 | tf_op jit(solution)/shard_map/pack/pallas_call | solution.py:112
  6.9 1.2 %pack.8 = bf16[2,8,128,128]{3,2,1,0:T(8,128)(2,1)S(1)} custom-call(s32[2]{0:T(128)S(1)} %compare_select_fusion.info, bf16[128,96,128]{2,1,0:T(8,128)(2,1)S(1)} %bitcast.5), custom_call_target="tpu_custom_call" | custom-call | bytes 1024 | tf_op jit(solution)/shard_map/pack/pallas_call | solution.py:112
  8.3 1.0 shard_map.37
  9.3 1.0 shard_map.38
  10.3 1.2 %pack.9.own.near_own = bf16[2,8,128,128]{3,2,1,0:T(8,128)(2,1)S(1)} custom-call(s32[2]{0:T(128)S(1)} %compare_select_fusion.info, bf16[128,96,128]{2,1,0:T(8,128)(2,1)S(1)} %bitcast.6), custom_call_target="tpu_custom_call" | custom-call | bytes 1024 | tf_op jit(solution)/shard_map/pack/pallas_call | solution.py:112
  11.6 1.0 shard_map.39
  15.7 6.1 %collective-permute-done.3 = bf16[4,2,128,128]{3,2,1,0:T(8,128)(2,1)S(1)} collective-permute-done((bf16[4,2,128,128]{3,2,1,0:T(8,128)(2,1)S(1)}, bf16[4,2,128,128]{3,2,1,0:T(8,128)(2,1)S(1)}, u32[]{:S(2)}, u32[]{:S(2)}) %collective-permute-start.3) | collective-permute-done | bytes 262176 | tf_op jit(solution)/shard_map/ppermute | solution.py:357
  22.8 1.0 shard_map.40.p0
  23.8 2.0 %shard_map.41 = (bf16[16,256,128]{2,1,0:T(8,128)(2,1)S(1)}, bf16[16,128,256]{2,1,0:T(8,128)(2,1)S(1)}, bf16[16,128,256]{2,1,0:T(8,128)(2,1)S(1)}, f32[16,128,256...) custom-call(s32[2]{0:T(128)S(1)} %compare_select_fusion.info, s32[8]{0:T(128)S(1)} %copy-done.1, ...), custom_call_target="tpu_custom_call" | custom-call | bytes 1024 | tf_op jit(solution)/shard_map/pallas_call | solution.py:32
  25.9 2.2 %collective-permute-done.4.p2 = bf16[4,2,128,128]{3,2,1,0:T(8,128)(2,1)S(1)} collective-permute-done((bf16[4,2,128,128]{3,2,1,0:T(8,128)(2,1)S(1)}, bf16[4,2,128,128]{3,2,1,0:T(8,128)(2,1)S(1)}, u32[]{:S(2)}, u32[]{:S(2)}) %collective-permute-start.4) | collective-permute-done | bytes 262176 | tf_op jit(solution)/shard_map/ppermute | solution.py:357
  29.0 19.2 %all_to_all.10.parts = bf16[32,32,128]{2,1,0:T(8,128)(2,1)S(1)} all-to-all(bf16[32,32,128]{2,1,0:T(8,128)(2,1)S(1)} %bitcast.11), channel_id=1, replica_groups=mesh['ctx'=32,'head'=8] {'ctx'}, dimensions={0} | all-to-all | bytes 524288 | tf_op jit(solution)/shard_map/all_to_all | solution.py:406
  48.2 1.1 %shard_map.43 = bf16[32,32,128]{2,1,0:T(8,128)(2,1)S(1)} custom-call(s32[2]{0:T(128)S(1)} %compare_select_fusion.info, s32[8]{0:T(128)S(1)} %copy-done.1, bf16[32,32,128]{2,1,0:T(8,128)(2,1)S(1)} %all_to_all.10.parts), custom_call_target="tpu_custom_call" | custom-call | bytes 1024 | tf_op jit(solution)/shard_map/pallas_call | solution.py:32
  49.4 14.2 %all_to_all.11 = bf16[32,32,128]{2,1,0:T(8,128)(2,1)S(1)} all-to-all(bf16[32,32,128]{2,1,0:T(8,128)(2,1)S(1)} %shard_map.43), channel_id=1, replica_groups=mesh['ctx'=32,'head'=8] {'ctx'}, dimensions={0} | all-to-all | bytes 524288 | tf_op jit(solution)/shard_map/all_to_all | solution.py:408
  63.6 1.8 %shard_map.44 = (bf16[4,2,128,128]{3,2,1,0:T(8,128)(2,1)S(1)}, bf16[4,2,128,128]{3,2,1,0:T(8,128)(2,1)S(1)}, bf16[4,2,128,128]{3,2,1,0:T(8,128)(2,1)S(1)}) custom-call(s32[2]{0:T(128)S(1)} %compare_select_fusion.info, s32[8]{0:T(128)S(1)} %copy-done.1, bf16[4,2,128,128]{3,2,1,0:T(8,128)(2,1)S(1)} %shard_map.40.p0, ...), custom_call_target="tpu_custom_call" | custom-call | bytes 1024 | tf_op jit(solution)/shard_map/pallas_call | solution.py:32
  65.4 2.4 %collective-permute-start.8 = (bf16[4,2,128,128]{3,2,1,0:T(8,128)(2,1)S(1)}, bf16[4,2,128,128]{3,2,1,0:T(8,128)(2,1)S(1)}, u32[]{:S(2)}, u32[]{:S(2)}) collective-permute-start(bf16[4,2,128,128]{3,2,1,0:T(8,128)(2,1)S(1)} %get-tuple-element.68), channel_id=1, source_target_pairs={{0,2},{1,3},{2,0},{3,1},{4,6},{5,7},{6,4},{7,5},{8,10},{9,11},{10,... | collective-permute-start | bytes 786440 | tf_op jit(solution)/shard_map/ppermute | solution.py:350
  67.8 2.3 %collective-permute-start.9 = (bf16[4,2,128,128]{3,2,1,0:T(8,128)(2,1)S(1)}, bf16[4,2,128,128]{3,2,1,0:T(8,128)(2,1)S(1)}, u32[]{:S(2)}, u32[]{:S(2)}) collective-permute-start(bf16[4,2,128,128]{3,2,1,0:T(8,128)(2,1)S(1)} %get-tuple-element.69), channel_id=1, source_target_pairs={{0,6},{1,7},{2,4},{3,5},{4,2},{5,3},{6,0},{7,1},{8,14},{9,15},{10,... | collective-permute-start | bytes 786440 | tf_op jit(solution)/shard_map/ppermute | solution.py:350
  70.1 6.1 %shard_map.45 = (bf16[4,128,128]{2,1,0:T(8,128)(2,1)S(1)}, bf16[4,128,128]{2,1,0:T(8,128)(2,1)S(1)}) custom-call(s32[2]{0:T(128)S(1)} %compare_select_fusion.info, f32[32]{0:T(128)S(1)} %copy-done.2, bf16[16,256,128]{2,1,0:T(8,128)(2,1)S(1)} %get-tuple-element.58.keys, bf16[16,128,256]{2,1,0:T(8,128)(2,1)S(1)} %get-tuple-element.59.key_t, ...), custom_call_target="tpu_custom_call" | custom-call | flops 4000000000 | bytes 1024 | tf_op jit(solution)/shard_map/pallas_call | solution.py:32
  77.3 1.2 %collective-permute-start.11 = (bf16[4,2,128,128]{3,2,1,0:T(8,128)(2,1)S(1)}, bf16[4,2,128,128]{3,2,1,0:T(8,128)(2,1)S(1)}, u32[]{:S(2)}, u32[]{:S(2)}) collective-permute-start(bf16[4,2,128,128]{3,2,1,0:T(8,128)(2,1)S(1)} %shard_map.47), channel_id=1, source_target_pairs={{0,4},{1,5},{2,6},{3,7},{4,0},{5,1},{6,2},{7,3},{8,12},{9,13},{10,... | collective-permute-start | bytes 786440 | tf_op jit(solution)/shard_map/ppermute | solution.py:350
  78.4 4.2 %collective-permute-start.7 = (bf16[4,128,128]{2,1,0:T(8,128)(2,1)S(1)}, bf16[4,128,128]{2,1,0:T(8,128)(2,1)S(1)}, u32[]{:S(2)}, u32[]{:S(2)}) collective-permute-start(bf16[4,128,128]{2,1,0:T(8,128)(2,1)S(1)} %get-tuple-element.67), channel_id=1, source_target_pairs={{0,1},{1,0},{2,3},{3,2},{4,5},{5,4},{6,7},{7,6},{8,9},{9,8},{10,11... | collective-permute-start | bytes 393224 | tf_op jit(solution)/shard_map/ppermute | solution.py:347
  82.7 11.6 %shard_map.46 = (bf16[8,128,128]{2,1,0:T(8,128)(2,1)S(1)}, bf16[8,128,128]{2,1,0:T(8,128)(2,1)S(1)}) custom-call(s32[2]{0:T(128)S(1)} %compare_select_fusion.info, f32[32]{0:T(128)S(1)} %copy-done.2, bf16[16,256,128]{2,1,0:T(8,128)(2,1)S(1)} %get-tuple-element.58.keys, bf16[16,128,256]{2,1,0:T(8,128)(2,1)S(1)} %get-tuple-element.59.key_t, ...), custom_call_target="tpu_custom_call" | custom-call | flops 8000000000 | bytes 1024 | tf_op jit(solution)/shard_map/pallas_call | solution.py:32
  94.4 6.1 %shard_map.48 = (bf16[4,128,128]{2,1,0:T(8,128)(2,1)S(1)}, bf16[4,128,128]{2,1,0:T(8,128)(2,1)S(1)}) custom-call(s32[2]{0:T(128)S(1)} %compare_select_fusion.info, f32[32]{0:T(128)S(1)} %copy-done.2, bf16[16,256,128]{2,1,0:T(8,128)(2,1)S(1)} %get-tuple-element.58.keys, bf16[16,128,256]{2,1,0:T(8,128)(2,1)S(1)} %get-tuple-element.59.key_t, ...), custom_call_target="tpu_custom_call" | custom-call | flops 4000000000 | bytes 1024 | tf_op jit(solution)/shard_map/pallas_call | solution.py:32
  102.1 2.7 %shard_map.49 = bf16[128,32,128]{2,1,0:T(8,128)(2,1)} custom-call(s32[2]{0:T(128)S(1)} %compare_select_fusion.info, bf16[4,128,128]{2,1,0:T(8,128)(2,1)S(1)} %get-tuple-element.66.rest_0_, bf16[4,128,128]{2,1,0:T(8,128)(2,1)S(1)} %collective-permute-done.7.rest_1_, bf16[8,128,128]{2,1,0:T(8,128)(2,1)S(1)} %get-tuple-element.70.rest_2_, ...), custom_call_target="tpu_custom_call" | custom-call | bytes 1024 | tf_op jit(solution)/shard_map/pallas_call | solution.py:32
  (30 shorter events, 7.8 us)
Async XLA Ops:
  0.0 5.6 %copy-start = (bf16[128,3,32,128]{3,2,1,0:T(8,128)(2,1)S(1)}, bf16[128,3,32,128]{3,2,1,0:T(8,128)(2,1)}, u32[]{:S(2)}) copy-start(bf16[128,3,32,128]{3,2,1,0:T(8,128)(2,1)} %param.3) | copy-start | bytes 9437188
  2.4 5.9 %copy-start.1 = (s32[8]{0:T(128)S(1)}, s32[8]{0:T(128)}, u32[]{:S(2)}) copy-start(s32[8]{0:T(128)} %lengths.17) | copy-start | bytes 100
  2.4 5.9 %collective-permute-start = (bf16[2,8,128,128]{3,2,1,0:T(8,128)(2,1)S(1)}, bf16[2,8,128,128]{3,2,1,0:T(8,128)(2,1)S(1)}, u32[]{:S(2)}, u32[]{:S(2)}) collective-permute-start(bf16[2,8,128,128]{3,2,1,0:T(8,128)(2,1)S(1)} %pack.6), channel_id=1, source_target_pairs={{0,1},{1,0},{2,3},{3,2},{4,5},{5,4},{6,7},{7,6},{8,9},{9,8},{10,11... | collective-permute-start | bytes 1572872 | tf_op jit(solution)/shard_map/ppermute | solution.py:347
  8.2 3.4 %collective-permute-start.1 = (bf16[2,8,128,128]{3,2,1,0:T(8,128)(2,1)S(1)}, bf16[2,8,128,128]{3,2,1,0:T(8,128)(2,1)S(1)}, u32[]{:S(2)}, u32[]{:S(2)}) collective-permute-start(bf16[2,8,128,128]{3,2,1,0:T(8,128)(2,1)S(1)} %pack.8), channel_id=1, source_target_pairs={{0,1},{1,0},{2,3},{3,2},{4,5},{5,4},{6,7},{7,6},{8,9},{9,8},{10,11... | collective-permute-start | bytes 1572872 | tf_op jit(solution)/shard_map/ppermute | solution.py:347
  13.6 10.2 %collective-permute-start.6 = (bf16[1,16,128,128]{3,2,1,0:T(8,128)(2,1)S(1)}, bf16[1,16,128,128]{3,2,1,0:T(8,128)(2,1)S(1)}, u32[]{:S(2)}, u32[]{:S(2)}) collective-permute-start(bf16[1,16,128,128]{3,2,1,0:T(8,128)(2,1)S(1)} %pack.10), channel_id=1, source_target_pairs={{0,1},{1,0},{2,3},{3,2},{4,5},{5,4},{6,7},{7,6},{8,9},{9,8},{10,11... | collective-permute-start | bytes 1572872 | tf_op jit(solution)/shard_map/ppermute | solution.py:347
  14.1 7.7 %collective-permute-start.3 = (bf16[4,2,128,128]{3,2,1,0:T(8,128)(2,1)S(1)}, bf16[4,2,128,128]{3,2,1,0:T(8,128)(2,1)S(1)}, u32[]{:S(2)}, u32[]{:S(2)}) collective-permute-start(bf16[4,2,128,128]{3,2,1,0:T(8,128)(2,1)S(1)} %shard_map.37), channel_id=1, source_target_pairs={{0,2},{2,4},{4,6},{6,0},{1,7},{3,1},{5,3},{7,5},{8,10},{10,12},{12... | collective-permute-start | bytes 786440 | tf_op jit(solution)/shard_map/ppermute | solution.py:357
  14.9 10.9 %collective-permute-start.2 = (bf16[4,2,128,128]{3,2,1,0:T(8,128)(2,1)S(1)}, bf16[4,2,128,128]{3,2,1,0:T(8,128)(2,1)S(1)}, u32[]{:S(2)}, u32[]{:S(2)}) collective-permute-start(bf16[4,2,128,128]{3,2,1,0:T(8,128)(2,1)S(1)} %shard_map.39), channel_id=1, source_target_pairs={{0,2},{1,3},{2,0},{3,1},{4,6},{5,7},{6,4},{7,5},{8,10},{9,11},{10,... | collective-permute-start | bytes 786440 | tf_op jit(solution)/shard_map/ppermute | solution.py:350
  15.6 10.3 %collective-permute-start.5 = (bf16[4,2,128,128]{3,2,1,0:T(8,128)(2,1)S(1)}, bf16[4,2,128,128]{3,2,1,0:T(8,128)(2,1)S(1)}, u32[]{:S(2)}, u32[]{:S(2)}) collective-permute-start(bf16[4,2,128,128]{3,2,1,0:T(8,128)(2,1)S(1)} %shard_map.38), channel_id=1, source_target_pairs={{0,6},{1,7},{2,4},{3,5},{4,2},{5,3},{6,0},{7,1},{8,14},{9,15},{10,... | collective-permute-start | bytes 786440 | tf_op jit(solution)/shard_map/ppermute | solution.py:350
  21.8 6.3 %collective-permute-start.4 = (bf16[4,2,128,128]{3,2,1,0:T(8,128)(2,1)S(1)}, bf16[4,2,128,128]{3,2,1,0:T(8,128)(2,1)S(1)}, u32[]{:S(2)}, u32[]{:S(2)}) collective-permute-start(bf16[4,2,128,128]{3,2,1,0:T(8,128)(2,1)S(1)} %collective-permute-done.3), channel_id=1, source_target_pairs={{0,2},{2,4},{4,6},{6,0},{1,7},{3,1},{5,3},{7,5},{8,10},{10,12},{12... | collective-permute-start | bytes 786440 | tf_op jit(solution)/shard_map/ppermute | solution.py:357
  23.8 46.3 %copy-start.2 = (f32[32]{0:T(128)S(1)}, f32[32]{0:T(128)}, u32[]{:S(2)}) copy-start(f32[32]{0:T(128)} %reg.5) | copy-start | bytes 388
  65.4 17.3 %collective-permute-start.8 = (bf16[4,2,128,128]{3,2,1,0:T(8,128)(2,1)S(1)}, bf16[4,2,128,128]{3,2,1,0:T(8,128)(2,1)S(1)}, u32[]{:S(2)}, u32[]{:S(2)}) collective-permute-start(bf16[4,2,128,128]{3,2,1,0:T(8,128)(2,1)S(1)} %get-tuple-element.68), channel_id=1, source_target_pairs={{0,2},{1,3},{2,0},{3,1},{4,6},{5,7},{6,4},{7,5},{8,10},{9,11},{10,... | collective-permute-start | bytes 786440 | tf_op jit(solution)/shard_map/ppermute | solution.py:350
  67.8 14.8 %collective-permute-start.9 = (bf16[4,2,128,128]{3,2,1,0:T(8,128)(2,1)S(1)}, bf16[4,2,128,128]{3,2,1,0:T(8,128)(2,1)S(1)}, u32[]{:S(2)}, u32[]{:S(2)}) collective-permute-start(bf16[4,2,128,128]{3,2,1,0:T(8,128)(2,1)S(1)} %get-tuple-element.69), channel_id=1, source_target_pairs={{0,6},{1,7},{2,4},{3,5},{4,2},{5,3},{6,0},{7,1},{8,14},{9,15},{10,... | collective-permute-start | bytes 786440 | tf_op jit(solution)/shard_map/ppermute | solution.py:350
  77.3 17.1 %collective-permute-start.11 = (bf16[4,2,128,128]{3,2,1,0:T(8,128)(2,1)S(1)}, bf16[4,2,128,128]{3,2,1,0:T(8,128)(2,1)S(1)}, u32[]{:S(2)}, u32[]{:S(2)}) collective-permute-start(bf16[4,2,128,128]{3,2,1,0:T(8,128)(2,1)S(1)} %shard_map.47), channel_id=1, source_target_pairs={{0,4},{1,5},{2,6},{3,7},{4,0},{5,1},{6,2},{7,3},{8,12},{9,13},{10,... | collective-permute-start | bytes 786440 | tf_op jit(solution)/shard_map/ppermute | solution.py:350
  78.4 22.7 %collective-permute-start.7 = (bf16[4,128,128]{2,1,0:T(8,128)(2,1)S(1)}, bf16[4,128,128]{2,1,0:T(8,128)(2,1)S(1)}, u32[]{:S(2)}, u32[]{:S(2)}) collective-permute-start(bf16[4,128,128]{2,1,0:T(8,128)(2,1)S(1)} %get-tuple-element.67), channel_id=1, source_target_pairs={{0,1},{1,0},{2,3},{3,2},{4,5},{5,4},{6,7},{7,6},{8,9},{9,8},{10,11... | collective-permute-start | bytes 393224 | tf_op jit(solution)/shard_map/ppermute | solution.py:347
  94.3 7.8 %collective-permute-start.10 = (bf16[8,128,128]{2,1,0:T(8,128)(2,1)S(1)}, bf16[8,128,128]{2,1,0:T(8,128)(2,1)S(1)}, u32[]{:S(2)}, u32[]{:S(2)}) collective-permute-start(bf16[8,128,128]{2,1,0:T(8,128)(2,1)S(1)} %get-tuple-element.71), channel_id=1, source_target_pairs={{0,1},{1,0},{2,3},{3,2},{4,5},{5,4},{6,7},{7,6},{8,9},{9,8},{10,11... | collective-permute-start | bytes 786440 | tf_op jit(solution)/shard_map/ppermute | solution.py:347
  100.5 1.6 %collective-permute-start.12 = (bf16[4,128,128]{2,1,0:T(8,128)(2,1)S(1)}, bf16[4,128,128]{2,1,0:T(8,128)(2,1)S(1)}, u32[]{:S(2)}, u32[]{:S(2)}) collective-permute-start(bf16[4,128,128]{2,1,0:T(8,128)(2,1)S(1)} %get-tuple-element.74), channel_id=1, source_target_pairs={{0,1},{1,0},{2,3},{3,2},{4,5},{5,4},{6,7},{7,6},{8,9},{9,8},{10,11... | collective-permute-start | bytes 393224 | tf_op jit(solution)/shard_map/ppermute | solution.py:347

commit v7 on v6

--- a/solution.py
+++ b/solution.py
@@ -320,18 +320,37 @@
 
 
 def unpack_kernel(info, *rest):
-    parts, (out_ref, stage) = rest[:-2], rest[-2:]
-    x, core, _, _ = spot(info)
+    x, _, _, _ = spot(info)
+    parts, (out_ref, stage) = rest[: len(GROUPS)], rest[-2:]
     rows = out_ref.shape[0]
-    for other in range(2):
-        for g, shifts in enumerate(GROUPS):
-            part = parts[2 * g + other]
-            for i in range(len(shifts) * PER):
-                h = (x ^ shifts[i // PER]) * PER + i % PER
-                stage[pl.ds(h, rows, stride=16), :] = part[i].astype(F32)
-        half = core if other == 0 else 1 - core
-        first = pl.multiple_of(half * 16, 16)
-        out_ref[:, pl.ds(first, 16), :] = stage[...].reshape(rows, 16, HD).astype(BF)
+    for shifts, part in zip(GROUPS, parts):
+        for i in range(len(shifts) * PER):
+            h = (x ^ shifts[i // PER]) * PER + i % PER
+            stage[pl.ds(h, rows, stride=16), :] = part[i].astype(F32)
+    out_ref[...] = stage[...].reshape(rows, 16, HD).astype(BF)
+
+
+def unpack(info, parts, other, shape, base=()):
+    rows = shape[0]
+
+    def place(g, info):
+        core = info[0] % 2
+        return 0, 1 - core if other else core, 0
+
+    return pl.pallas_call(
+        unpack_kernel,
+        grid_spec=pltpu.PrefetchScalarGridSpec(
+            num_scalar_prefetch=1,
+            grid=(1,),
+            in_specs=[VMEM] * len(parts) + [pl.BlockSpec(memory_space=pl.ANY)] * len(base),
+            out_specs=pl.BlockSpec((rows, 16, HD), place),
+            scratch_shapes=[pltpu.VMEM((rows * 16, HD), F32)],
+        ),
+        out_shape=jax.ShapeDtypeStruct(shape, BF),
+        input_output_aliases={1 + len(parts): 0} if base else {},
+        compiler_params=pltpu.CompilerParams(vmem_limit_bytes=12 << 20),
+        name="unpack",
+    )(info, *parts, *base)
 
 
 def body(qkv, lengths, reg):
@@ -406,16 +425,20 @@
     slices = lax.all_to_all(total.reshape(places, -1, width), "ctx", 0, 0, tiled=True)
     entries = call(entries_kernel, array(slices.shape))(info, lengths, slices)
     entry = lax.all_to_all(entries, "ctx", 0, 0, tiled=True).reshape(states.shape)
-    near = (1, 3, 0)
-    made = call(functools.partial(states_kernel, near), [states] * 3)(info, lengths, *parts, entry)
-    before = {shift: along_x(part, shift) if shift else part for shift, part in zip(near, made)}
-
-    results = []
+    masks = (1, 3, 0, 2)
+    made = call(functools.partial(states_kernel, masks), [states] * NX)(
+        info, lengths, *parts, entry
+    )
+    before = dict(zip(masks, made))
+    for shift in (1, 3):
+        before[shift] = along_x(before[shift], shift)
+
+    mine, theirs = [], []
     for shifts in GROUPS:
         count = len(shifts) * PER
         vectors = pltpu.VMEM((count, width, BLOCK), F32)
         result = array((count, rows, width))
-        mine, others = call(
+        kept, others = call(
             functools.partial(solve_kernel, shifts),
             [result, result],
             [
@@ -431,18 +454,12 @@
             limit=28,
         )(info, reg, *prepared, *(before[s] for s in shifts))
         if shifts == (0,):
-            entry, mine = lax.optimization_barrier((entry, mine))
-            (part,) = call(functools.partial(states_kernel, (2,)), [states])(
-                info, lengths, *parts, entry
-            )
-            before[2] = along_x(part, 2)
-        results += [mine, swap(others)]
-    return call(
-        unpack_kernel,
-        array((rows, heads, width)),
-        [pltpu.VMEM((rows * half, width), F32)],
-        scalars=1,
-    )(info, *results)
+            before[2] = along_x(after(before[2], kept), 2)
+        mine.append(kept)
+        theirs.append(swap(others))
+    shape = (rows, heads, width)
+    out = unpack(info, mine, False, shape)
+    return unpack(info, theirs, True, shape, (out,))
 
 
 def solution(mesh):

time: 105 us -> 105 us (level)
    pallas_call x0 -> x2, Pallas kernels: none -> 3.86 us  [unpack(): pl.pallas_call(unpack_kernel, grid_spec=pltpu.PrefetchScalarGridSpec(num_...]
    pallas_call x13 -> x11, Pallas kernels: 37.5 us -> 34.3 us  [run(): pl.pallas_call(kernel, in_specs=[SMEM] * scalars + [VMEM] * (len(args) -...]
  transfers between devices with their start and end apart: 13 -> 13, of which waited for: 3 -> 2; matrix products, arithmetic and copies ran while one was open for 0% -> 0% of each run, Pallas kernels for 33% -> 34%
where the time goes in v7:
time: 105 us; the launch traced here: 104 us
  Pallas kernels  46.1 us (44%)
  blocking collectives  33.5 us (32%)
  starting transfers between devices  16.3 us (16%)
  waiting for transfers between devices  8.31 us (8%)
    pallas_call x11, Pallas kernels, run(): pl.pallas_call(kernel, in_specs=[SMEM] * scalars + [VMEM] * (len(args) -...  34.3 us
    all_to_all x1, blocking collectives, body(): lax.all_to_all(total.reshape(places, -1, width), 'ctx', 0, 0, tiled=True)  19.2 us
    all_to_all x1, blocking collectives, body(): lax.all_to_all(entries, 'ctx', 0, 0, tiled=True).reshape(states.shape)  14.2 us
    ppermute x6, starting transfers between devices, swap(): return lax.ppermute(a, 'head', [(i, i ^ 1) for i in range(2 * NX)])  8.86 us
    ppermute x2, waiting for transfers between devices, relay(): return lax.ppermute(a, 'head', ring + back)  8.29 us
    pallas_call x6, Pallas kernels, pack(): pl.pallas_call(functools.partial(pack_kernel, kinds[0] == 1), grid_spec=p...  8 us
    ppermute x5, starting transfers between devices, along_x(): lax.ppermute(a, 'head', [(i, 2 * (i // 2 ^ shift) + i % 2) for i in range...  6.7 us
    pallas_call x2, Pallas kernels, unpack(): pl.pallas_call(unpack_kernel, grid_spec=pltpu.PrefetchScalarGridSpec(num_...  3.86 us
  transfers between devices with their start and end apart: 13, of which 2 were waited for; matrix products, arithmetic and copies ran while one was open for 0% of the time, Pallas kernels for 34%

profile of v7, /device:TPU:1, one launch (start us, length us, event | category | flops | bytes accessed | tf_op | source)
XLA Modules:
  0.0 104.5 jit_solution(8326286844241763083)
XLA Ops:
  0.0 2.3 %pack.6 = bf16[2,8,128,128]{3,2,1,0:T(8,128)(2,1)S(1)} custom-call(s32[2]{0:T(128)S(1)} %compare_select_fusion.info, bf16[128,96,128]{2,1,0:T(8,128)(2,1)} %bitcast.3), custom_call_target="tpu_custom_call" | custom-call | bytes 1024 | tf_op jit(solution)/shard_map/pack/pallas_call | solution.py:112
  2.4 3.3 %collective-permute-start = (bf16[2,8,128,128]{3,2,1,0:T(8,128)(2,1)S(1)}, bf16[2,8,128,128]{3,2,1,0:T(8,128)(2,1)S(1)}, u32[]{:S(2)}, u32[]{:S(2)}) collective-permute-start(bf16[2,8,128,128]{3,2,1,0:T(8,128)(2,1)S(1)} %pack.6), channel_id=1, source_target_pairs={{0,1},{1,0},{2,3},{3,2},{4,5},{5,4},{6,7},{7,6},{8,9},{9,8},{10,11... | collective-permute-start | bytes 1572872 | tf_op jit(solution)/shard_map/ppermute | solution.py:366
  5.6 1.2 %pack.7.own.far_own = bf16[2,8,128,128]{3,2,1,0:T(8,128)(2,1)S(1)} custom-call(s32[2]{0:T(128)S(1)} %compare_select_fusion.info, bf16[128,96,128]{2,1,0:T(8,128)(2,1)S(1)} %bitcast.4), custom_call_target="tpu_custom_call" | custom-call | bytes 1024 | tf_op jit(solution)/shard_map/pack/pallas_call | solution.py:112
  6.9 1.2 %pack.8 = bf16[2,8,128,128]{3,2,1,0:T(8,128)(2,1)S(1)} custom-call(s32[2]{0:T(128)S(1)} %compare_select_fusion.info, bf16[128,96,128]{2,1,0:T(8,128)(2,1)S(1)} %bitcast.5), custom_call_target="tpu_custom_call" | custom-call | bytes 1024 | tf_op jit(solution)/shard_map/pack/pallas_call | solution.py:112
  9.3 1.0 shard_map.38
  10.3 1.2 %pack.9.own.near_own = bf16[2,8,128,128]{3,2,1,0:T(8,128)(2,1)S(1)} custom-call(s32[2]{0:T(128)S(1)} %compare_select_fusion.info, bf16[128,96,128]{2,1,0:T(8,128)(2,1)S(1)} %bitcast.6), custom_call_target="tpu_custom_call" | custom-call | bytes 1024 | tf_op jit(solution)/shard_map/pack/pallas_call | solution.py:112
  11.6 1.0 shard_map.39
  15.7 6.1 %collective-permute-done.3 = bf16[4,2,128,128]{3,2,1,0:T(8,128)(2,1)S(1)} collective-permute-done((bf16[4,2,128,128]{3,2,1,0:T(8,128)(2,1)S(1)}, bf16[4,2,128,128]{3,2,1,0:T(8,128)(2,1)S(1)}, u32[]{:S(2)}, u32[]{:S(2)}) %collective-permute-start.3) | collective-permute-done | bytes 262176 | tf_op jit(solution)/shard_map/ppermute | solution.py:376
  22.8 1.0 shard_map.40.p0
  23.8 2.0 %shard_map.41 = (bf16[16,256,128]{2,1,0:T(8,128)(2,1)S(1)}, bf16[16,128,256]{2,1,0:T(8,128)(2,1)S(1)}, bf16[16,128,256]{2,1,0:T(8,128)(2,1)S(1)}, f32[16,128,256...) custom-call(s32[2]{0:T(128)S(1)} %compare_select_fusion.info, s32[8]{0:T(128)S(1)} %copy-done.1, ...), custom_call_target="tpu_custom_call" | custom-call | bytes 1024 | tf_op jit(solution)/shard_map/pallas_call | solution.py:32
  25.9 2.2 %collective-permute-done.4.p2 = bf16[4,2,128,128]{3,2,1,0:T(8,128)(2,1)S(1)} collective-permute-done((bf16[4,2,128,128]{3,2,1,0:T(8,128)(2,1)S(1)}, bf16[4,2,128,128]{3,2,1,0:T(8,128)(2,1)S(1)}, u32[]{:S(2)}, u32[]{:S(2)}) %collective-permute-start.4) | collective-permute-done | bytes 262176 | tf_op jit(solution)/shard_map/ppermute | solution.py:376
  29.0 19.2 %all_to_all.10.parts = bf16[32,32,128]{2,1,0:T(8,128)(2,1)S(1)} all-to-all(bf16[32,32,128]{2,1,0:T(8,128)(2,1)S(1)} %bitcast.10), channel_id=1, replica_groups=mesh['ctx'=32,'head'=8] {'ctx'}, dimensions={0} | all-to-all | bytes 524288 | tf_op jit(solution)/shard_map/all_to_all | solution.py:425
  48.2 1.1 %shard_map.43 = bf16[32,32,128]{2,1,0:T(8,128)(2,1)S(1)} custom-call(s32[2]{0:T(128)S(1)} %compare_select_fusion.info, s32[8]{0:T(128)S(1)} %copy-done.1, bf16[32,32,128]{2,1,0:T(8,128)(2,1)S(1)} %all_to_all.10.parts), custom_call_target="tpu_custom_call" | custom-call | bytes 1024 | tf_op jit(solution)/shard_map/pallas_call | solution.py:32
  49.4 14.2 %all_to_all.11 = bf16[32,32,128]{2,1,0:T(8,128)(2,1)S(1)} all-to-all(bf16[32,32,128]{2,1,0:T(8,128)(2,1)S(1)} %shard_map.43), channel_id=1, replica_groups=mesh['ctx'=32,'head'=8] {'ctx'}, dimensions={0} | all-to-all | bytes 524288 | tf_op jit(solution)/shard_map/all_to_all | solution.py:427
  63.6 2.2 %shard_map.44 = (bf16[4,2,128,128]{3,2,1,0:T(8,128)(2,1)S(1)}, bf16[4,2,128,128]{3,2,1,0:T(8,128)(2,1)S(1)}, bf16[4,2,128,128]{3,2,1,0:T(8,128)(2,1)S(1)}, bf16[4,2,128,128]{3,2,1,0:T(8,128)(2,1)S(1)}) custom-call(s32[2]{0:T(128)S(1)} %compare_select_fusion.info, s32[8]{0:T(128)S(1)} %copy-done.1, bf16[4,2,128,128]{3,2,1,0:T(8,128)(2,1)S(1)} %shard_map.40.p0, ...), custom_call_target="tpu_custom_call" | custom-call | bytes 1024 | tf_op jit(solution)/shard_map/pallas_call | solution.py:32
  65.8 2.4 %collective-permute-start.8 = (bf16[4,2,128,128]{3,2,1,0:T(8,128)(2,1)S(1)}, bf16[4,2,128,128]{3,2,1,0:T(8,128)(2,1)S(1)}, u32[]{:S(2)}, u32[]{:S(2)}) collective-permute-start(bf16[4,2,128,128]{3,2,1,0:T(8,128)(2,1)S(1)} %get-tuple-element.66), channel_id=1, source_target_pairs={{0,2},{1,3},{2,0},{3,1},{4,6},{5,7},{6,4},{7,5},{8,10},{9,11},{10,... | collective-permute-start | bytes 786440 | tf_op jit(solution)/shard_map/ppermute | solution.py:369
  68.3 2.3 %collective-permute-start.9 = (bf16[4,2,128,128]{3,2,1,0:T(8,128)(2,1)S(1)}, bf16[4,2,128,128]{3,2,1,0:T(8,128)(2,1)S(1)}, u32[]{:S(2)}, u32[]{:S(2)}) collective-permute-start(bf16[4,2,128,128]{3,2,1,0:T(8,128)(2,1)S(1)} %get-tuple-element.67), channel_id=1, source_target_pairs={{0,6},{1,7},{2,4},{3,5},{4,2},{5,3},{6,0},{7,1},{8,14},{9,15},{10,... | collective-permute-start | bytes 786440 | tf_op jit(solution)/shard_map/ppermute | solution.py:369
  70.6 6.1 %shard_map.45 = (bf16[4,128,128]{2,1,0:T(8,128)(2,1)S(1)}, bf16[4,128,128]{2,1,0:T(8,128)(2,1)S(1)}) custom-call(s32[2]{0:T(128)S(1)} %compare_select_fusion.info, f32[32]{0:T(128)S(1)} %copy-done.2, bf16[16,256,128]{2,1,0:T(8,128)(2,1)S(1)} %get-tuple-element.54.keys, bf16[16,128,256]{2,1,0:T(8,128)(2,1)S(1)} %get-tuple-element.55.key_t, ...), custom_call_target="tpu_custom_call" | custom-call | flops 4000000000 | bytes 1024 | tf_op jit(solution)/shard_map/pallas_call | solution.py:32
  76.7 1.2 %collective-permute-start.11 = (bf16[4,2,128,128]{3,2,1,0:T(8,128)(2,1)S(1)}, bf16[4,2,128,128]{3,2,1,0:T(8,128)(2,1)S(1)}, u32[]{:S(2)}, u32[]{:S(2)}) collective-permute-start(bf16[4,2,128,128]{3,2,1,0:T(8,128)(2,1)S(1)} %get-tuple-element.71), channel_id=1, source_target_pairs={{0,4},{1,5},{2,6},{3,7},{4,0},{5,1},{6,2},{7,3},{8,12},{9,13},{10,... | collective-permute-start | bytes 786440 | tf_op jit(solution)/shard_map/ppermute | solution.py:369
  77.9 4.2 %collective-permute-start.7 = (bf16[4,128,128]{2,1,0:T(8,128)(2,1)S(1)}, bf16[4,128,128]{2,1,0:T(8,128)(2,1)S(1)}, u32[]{:S(2)}, u32[]{:S(2)}) collective-permute-start(bf16[4,128,128]{2,1,0:T(8,128)(2,1)S(1)} %get-tuple-element.65), channel_id=1, source_target_pairs={{0,1},{1,0},{2,3},{3,2},{4,5},{5,4},{6,7},{7,6},{8,9},{9,8},{10,11... | collective-permute-start | bytes 393224 | tf_op jit(solution)/shard_map/ppermute | solution.py:366
  82.1 11.6 %shard_map.46 = (bf16[8,128,128]{2,1,0:T(8,128)(2,1)S(1)}, bf16[8,128,128]{2,1,0:T(8,128)(2,1)S(1)}) custom-call(s32[2]{0:T(128)S(1)} %compare_select_fusion.info, f32[32]{0:T(128)S(1)} %copy-done.2, bf16[16,256,128]{2,1,0:T(8,128)(2,1)S(1)} %get-tuple-element.54.keys, bf16[16,128,256]{2,1,0:T(8,128)(2,1)S(1)} %get-tuple-element.55.key_t, ...), custom_call_target="tpu_custom_call" | custom-call | flops 8000000000 | bytes 1024 | tf_op jit(solution)/shard_map/pallas_call | solution.py:32
  93.9 6.1 %shard_map.47 = (bf16[4,128,128]{2,1,0:T(8,128)(2,1)S(1)}, bf16[4,128,128]{2,1,0:T(8,128)(2,1)S(1)}) custom-call(s32[2]{0:T(128)S(1)} %compare_select_fusion.info, f32[32]{0:T(128)S(1)} %copy-done.2, bf16[16,256,128]{2,1,0:T(8,128)(2,1)S(1)} %get-tuple-element.54.keys, bf16[16,128,256]{2,1,0:T(8,128)(2,1)S(1)} %get-tuple-element.55.key_t, ...), custom_call_target="tpu_custom_call" | custom-call | flops 4000000000 | bytes 1024 | tf_op jit(solution)/shard_map/pallas_call | solution.py:32
  100.6 1.9 %unpack.2.rest_3_ = bf16[128,32,128]{2,1,0:T(8,128)(2,1)} custom-call(s32[2]{0:T(128)S(1)} %compare_select_fusion.info, bf16[4,128,128]{2,1,0:T(8,128)(2,1)S(1)} %get-tuple-element.70.rest_0_, bf16[8,128,128]{2,1,0:T(8,128)(2,1)S(1)} %get-tuple-element.73.rest_1_, bf16[4,128,128]{2,1,0:T(8,128)(2,1)S(1)} %get-tuple-element.74.rest_2_), custom_call_target="tpu_custom_call" | custom-call | tf_op jit(solution)/shard_map/unpack/pallas_call | solution.py:340
  102.5 1.9 %unpack.3 = bf16[128,32,128]{2,1,0:T(8,128)(2,1)} custom-call(s32[2]{0:T(128)S(1)} %compare_select_fusion.info, bf16[4,128,128]{2,1,0:T(8,128)(2,1)S(1)} %collective-permute-done.7.rest_0_, bf16[8,128,128]{2,1,0:T(8,128)(2,1)S(1)} %collective-permute-done.10.rest_1_, ...), custom_call_target="tpu_custom_call", output_to_operand_aliasing={{}: (4, {})} | custom-call | tf_op jit(solution)/shard_map/unpack/pallas_call | solution.py:340
  (30 shorter events, 6.8 us)
Async XLA Ops:
  0.0 5.6 %copy-start = (bf16[128,3,32,128]{3,2,1,0:T(8,128)(2,1)S(1)}, bf16[128,3,32,128]{3,2,1,0:T(8,128)(2,1)}, u32[]{:S(2)}) copy-start(bf16[128,3,32,128]{3,2,1,0:T(8,128)(2,1)} %param.3) | copy-start | bytes 9437188
  2.4 5.9 %copy-start.1 = (s32[8]{0:T(128)S(1)}, s32[8]{0:T(128)}, u32[]{:S(2)}) copy-start(s32[8]{0:T(128)} %lengths.15) | copy-start | bytes 100
  2.4 5.9 %collective-permute-start = (bf16[2,8,128,128]{3,2,1,0:T(8,128)(2,1)S(1)}, bf16[2,8,128,128]{3,2,1,0:T(8,128)(2,1)S(1)}, u32[]{:S(2)}, u32[]{:S(2)}) collective-permute-start(bf16[2,8,128,128]{3,2,1,0:T(8,128)(2,1)S(1)} %pack.6), channel_id=1, source_target_pairs={{0,1},{1,0},{2,3},{3,2},{4,5},{5,4},{6,7},{7,6},{8,9},{9,8},{10,11... | collective-permute-start | bytes 1572872 | tf_op jit(solution)/shard_map/ppermute | solution.py:366
  8.2 3.4 %collective-permute-start.1 = (bf16[2,8,128,128]{3,2,1,0:T(8,128)(2,1)S(1)}, bf16[2,8,128,128]{3,2,1,0:T(8,128)(2,1)S(1)}, u32[]{:S(2)}, u32[]{:S(2)}) collective-permute-start(bf16[2,8,128,128]{3,2,1,0:T(8,128)(2,1)S(1)} %pack.8), channel_id=1, source_target_pairs={{0,1},{1,0},{2,3},{3,2},{4,5},{5,4},{6,7},{7,6},{8,9},{9,8},{10,11... | collective-permute-start | bytes 1572872 | tf_op jit(solution)/shard_map/ppermute | solution.py:366
  13.6 10.2 %collective-permute-start.6 = (bf16[1,16,128,128]{3,2,1,0:T(8,128)(2,1)S(1)}, bf16[1,16,128,128]{3,2,1,0:T(8,128)(2,1)S(1)}, u32[]{:S(2)}, u32[]{:S(2)}) collective-permute-start(bf16[1,16,128,128]{3,2,1,0:T(8,128)(2,1)S(1)} %pack.10), channel_id=1, source_target_pairs={{0,1},{1,0},{2,3},{3,2},{4,5},{5,4},{6,7},{7,6},{8,9},{9,8},{10,11... | collective-permute-start | bytes 1572872 | tf_op jit(solution)/shard_map/ppermute | solution.py:366
  14.1 7.7 %collective-permute-start.3 = (bf16[4,2,128,128]{3,2,1,0:T(8,128)(2,1)S(1)}, bf16[4,2,128,128]{3,2,1,0:T(8,128)(2,1)S(1)}, u32[]{:S(2)}, u32[]{:S(2)}) collective-permute-start(bf16[4,2,128,128]{3,2,1,0:T(8,128)(2,1)S(1)} %shard_map.37), channel_id=1, source_target_pairs={{0,2},{2,4},{4,6},{6,0},{1,7},{3,1},{5,3},{7,5},{8,10},{10,12},{12... | collective-permute-start | bytes 786440 | tf_op jit(solution)/shard_map/ppermute | solution.py:376
  14.9 10.9 %collective-permute-start.2 = (bf16[4,2,128,128]{3,2,1,0:T(8,128)(2,1)S(1)}, bf16[4,2,128,128]{3,2,1,0:T(8,128)(2,1)S(1)}, u32[]{:S(2)}, u32[]{:S(2)}) collective-permute-start(bf16[4,2,128,128]{3,2,1,0:T(8,128)(2,1)S(1)} %shard_map.39), channel_id=1, source_target_pairs={{0,2},{1,3},{2,0},{3,1},{4,6},{5,7},{6,4},{7,5},{8,10},{9,11},{10,... | collective-permute-start | bytes 786440 | tf_op jit(solution)/shard_map/ppermute | solution.py:369
  15.6 10.3 %collective-permute-start.5 = (bf16[4,2,128,128]{3,2,1,0:T(8,128)(2,1)S(1)}, bf16[4,2,128,128]{3,2,1,0:T(8,128)(2,1)S(1)}, u32[]{:S(2)}, u32[]{:S(2)}) collective-permute-start(bf16[4,2,128,128]{3,2,1,0:T(8,128)(2,1)S(1)} %shard_map.38), channel_id=1, source_target_pairs={{0,6},{1,7},{2,4},{3,5},{4,2},{5,3},{6,0},{7,1},{8,14},{9,15},{10,... | collective-permute-start | bytes 786440 | tf_op jit(solution)/shard_map/ppermute | solution.py:369
  21.8 6.3 %collective-permute-start.4 = (bf16[4,2,128,128]{3,2,1,0:T(8,128)(2,1)S(1)}, bf16[4,2,128,128]{3,2,1,0:T(8,128)(2,1)S(1)}, u32[]{:S(2)}, u32[]{:S(2)}) collective-permute-start(bf16[4,2,128,128]{3,2,1,0:T(8,128)(2,1)S(1)} %collective-permute-done.3), channel_id=1, source_target_pairs={{0,2},{2,4},{4,6},{6,0},{1,7},{3,1},{5,3},{7,5},{8,10},{10,12},{12... | collective-permute-start | bytes 786440 | tf_op jit(solution)/shard_map/ppermute | solution.py:376
  23.8 46.8 %copy-start.2 = (f32[32]{0:T(128)S(1)}, f32[32]{0:T(128)}, u32[]{:S(2)}) copy-start(f32[32]{0:T(128)} %reg.5) | copy-start | bytes 388
  65.8 16.3 %collective-permute-start.8 = (bf16[4,2,128,128]{3,2,1,0:T(8,128)(2,1)S(1)}, bf16[4,2,128,128]{3,2,1,0:T(8,128)(2,1)S(1)}, u32[]{:S(2)}, u32[]{:S(2)}) collective-permute-start(bf16[4,2,128,128]{3,2,1,0:T(8,128)(2,1)S(1)} %get-tuple-element.66), channel_id=1, source_target_pairs={{0,2},{1,3},{2,0},{3,1},{4,6},{5,7},{6,4},{7,5},{8,10},{9,11},{10,... | collective-permute-start | bytes 786440 | tf_op jit(solution)/shard_map/ppermute | solution.py:369
  68.3 13.9 %collective-permute-start.9 = (bf16[4,2,128,128]{3,2,1,0:T(8,128)(2,1)S(1)}, bf16[4,2,128,128]{3,2,1,0:T(8,128)(2,1)S(1)}, u32[]{:S(2)}, u32[]{:S(2)}) collective-permute-start(bf16[4,2,128,128]{3,2,1,0:T(8,128)(2,1)S(1)} %get-tuple-element.67), channel_id=1, source_target_pairs={{0,6},{1,7},{2,4},{3,5},{4,2},{5,3},{6,0},{7,1},{8,14},{9,15},{10,... | collective-permute-start | bytes 786440 | tf_op jit(solution)/shard_map/ppermute | solution.py:369
  76.7 17.1 %collective-permute-start.11 = (bf16[4,2,128,128]{3,2,1,0:T(8,128)(2,1)S(1)}, bf16[4,2,128,128]{3,2,1,0:T(8,128)(2,1)S(1)}, u32[]{:S(2)}, u32[]{:S(2)}) collective-permute-start(bf16[4,2,128,128]{3,2,1,0:T(8,128)(2,1)S(1)} %get-tuple-element.71), channel_id=1, source_target_pairs={{0,4},{1,5},{2,6},{3,7},{4,0},{5,1},{6,2},{7,3},{8,12},{9,13},{10,... | collective-permute-start | bytes 786440 | tf_op jit(solution)/shard_map/ppermute | solution.py:369
  77.9 24.6 %collective-permute-start.7 = (bf16[4,128,128]{2,1,0:T(8,128)(2,1)S(1)}, bf16[4,128,128]{2,1,0:T(8,128)(2,1)S(1)}, u32[]{:S(2)}, u32[]{:S(2)}) collective-permute-start(bf16[4,128,128]{2,1,0:T(8,128)(2,1)S(1)} %get-tuple-element.65), channel_id=1, source_target_pairs={{0,1},{1,0},{2,3},{3,2},{4,5},{5,4},{6,7},{7,6},{8,9},{9,8},{10,11... | collective-permute-start | bytes 393224 | tf_op jit(solution)/shard_map/ppermute | solution.py:366
  93.8 8.8 %collective-permute-start.10 = (bf16[8,128,128]{2,1,0:T(8,128)(2,1)S(1)}, bf16[8,128,128]{2,1,0:T(8,128)(2,1)S(1)}, u32[]{:S(2)}, u32[]{:S(2)}) collective-permute-start(bf16[8,128,128]{2,1,0:T(8,128)(2,1)S(1)} %get-tuple-element.68), channel_id=1, source_target_pairs={{0,1},{1,0},{2,3},{3,2},{4,5},{5,4},{6,7},{7,6},{8,9},{9,8},{10,11... | collective-permute-start | bytes 786440 | tf_op jit(solution)/shard_map/ppermute | solution.py:366
  100.0 2.5 %collective-permute-start.12 = (bf16[4,128,128]{2,1,0:T(8,128)(2,1)S(1)}, bf16[4,128,128]{2,1,0:T(8,128)(2,1)S(1)}, u32[]{:S(2)}, u32[]{:S(2)}) collective-permute-start(bf16[4,128,128]{2,1,0:T(8,128)(2,1)S(1)} %get-tuple-element.72), channel_id=1, source_target_pairs={{0,1},{1,0},{2,3},{3,2},{4,5},{5,4},{6,7},{7,6},{8,9},{9,8},{10,11... | collective-permute-start | bytes 393224 | tf_op jit(solution)/shard_map/ppermute | solution.py:366

commit v8 on v7

--- a/solution.py
+++ b/solution.py
@@ -456,7 +456,10 @@
         if shifts == (0,):
             before[2] = along_x(after(before[2], kept), 2)
         mine.append(kept)
-        theirs.append(swap(others))
+        theirs.append(others)
+    theirs[0] = swap(after(theirs[0], mine[1]))
+    theirs[1] = swap(theirs[1])
+    theirs[2] = swap(theirs[2])
     shape = (rows, heads, width)
     out = unpack(info, mine, False, shape)
     return unpack(info, theirs, True, shape, (out,))

time: 105 us -> 105 us (level)
  no operation moved by 1% of the time
where the time goes in v8:
time: 105 us
  Pallas kernels  46.1 us (44%)
  blocking collectives  33.5 us (32%)
  starting transfers between devices  16.6 us (16%)
  waiting for transfers between devices  8.31 us (8%)
    pallas_call x11, Pallas kernels, run(): pl.pallas_call(kernel, in_specs=[SMEM] * scalars + [VMEM] * (len(args) -...  34.3 us
    all_to_all x1, blocking collectives, body(): lax.all_to_all(total.reshape(places, -1, width), 'ctx', 0, 0, tiled=True)  19.2 us
    all_to_all x1, blocking collectives, body(): lax.all_to_all(entries, 'ctx', 0, 0, tiled=True).reshape(states.shape)  14.2 us
    ppermute x6, starting transfers between devices, swap(): return lax.ppermute(a, 'head', [(i, i ^ 1) for i in range(2 * NX)])  8.87 us
    ppermute x2, waiting for transfers between devices, relay(): return lax.ppermute(a, 'head', ring + back)  8.29 us
    pallas_call x6, Pallas kernels, pack(): pl.pallas_call(functools.partial(pack_kernel, kinds[0] == 1), grid_spec=p...  8 us
    ppermute x5, starting transfers between devices, along_x(): lax.ppermute(a, 'head', [(i, 2 * (i // 2 ^ shift) + i % 2) for i in range...  6.92 us
    pallas_call x2, Pallas kernels, unpack(): pl.pallas_call(unpack_kernel, grid_spec=pltpu.PrefetchScalarGridSpec(num_...  3.86 us
  transfers between devices with their start and end apart: 13, of which 2 were waited for; matrix products, arithmetic and copies ran while one was open for 0% of the time, Pallas kernels for 34%

profile of v8, /device:TPU:1, one launch (start us, length us, event | category | flops | bytes accessed | tf_op | source)
XLA Modules:
  0.0 104.7 jit_solution(2548870602617474213)
XLA Ops:
  0.0 2.3 %pack.6 = bf16[2,8,128,128]{3,2,1,0:T(8,128)(2,1)S(1)} custom-call(s32[2]{0:T(128)S(1)} %compare_select_fusion.info, bf16[128,96,128]{2,1,0:T(8,128)(2,1)} %bitcast.3), custom_call_target="tpu_custom_call" | custom-call | bytes 1024 | tf_op jit(solution)/shard_map/pack/pallas_call | solution.py:112
  2.4 3.3 %collective-permute-start = (bf16[2,8,128,128]{3,2,1,0:T(8,128)(2,1)S(1)}, bf16[2,8,128,128]{3,2,1,0:T(8,128)(2,1)S(1)}, u32[]{:S(2)}, u32[]{:S(2)}) collective-permute-start(bf16[2,8,128,128]{3,2,1,0:T(8,128)(2,1)S(1)} %pack.6), channel_id=1, source_target_pairs={{0,1},{1,0},{2,3},{3,2},{4,5},{5,4},{6,7},{7,6},{8,9},{9,8},{10,11... | collective-permute-start | bytes 1572872 | tf_op jit(solution)/shard_map/ppermute | solution.py:366
  5.6 1.2 %pack.7.own.far_own = bf16[2,8,128,128]{3,2,1,0:T(8,128)(2,1)S(1)} custom-call(s32[2]{0:T(128)S(1)} %compare_select_fusion.info, bf16[128,96,128]{2,1,0:T(8,128)(2,1)S(1)} %bitcast.4), custom_call_target="tpu_custom_call" | custom-call | bytes 1024 | tf_op jit(solution)/shard_map/pack/pallas_call | solution.py:112
  6.9 1.2 %pack.8 = bf16[2,8,128,128]{3,2,1,0:T(8,128)(2,1)S(1)} custom-call(s32[2]{0:T(128)S(1)} %compare_select_fusion.info, bf16[128,96,128]{2,1,0:T(8,128)(2,1)S(1)} %bitcast.5), custom_call_target="tpu_custom_call" | custom-call | bytes 1024 | tf_op jit(solution)/shard_map/pack/pallas_call | solution.py:112
  9.3 1.0 shard_map.38
  10.3 1.2 %pack.9.own.near_own = bf16[2,8,128,128]{3,2,1,0:T(8,128)(2,1)S(1)} custom-call(s32[2]{0:T(128)S(1)} %compare_select_fusion.info, bf16[128,96,128]{2,1,0:T(8,128)(2,1)S(1)} %bitcast.6), custom_call_target="tpu_custom_call" | custom-call | bytes 1024 | tf_op jit(solution)/shard_map/pack/pallas_call | solution.py:112
  11.6 1.0 shard_map.39
  15.7 6.1 %collective-permute-done.3 = bf16[4,2,128,128]{3,2,1,0:T(8,128)(2,1)S(1)} collective-permute-done((bf16[4,2,128,128]{3,2,1,0:T(8,128)(2,1)S(1)}, bf16[4,2,128,128]{3,2,1,0:T(8,128)(2,1)S(1)}, u32[]{:S(2)}, u32[]{:S(2)}) %collective-permute-start.3) | collective-permute-done | bytes 262176 | tf_op jit(solution)/shard_map/ppermute | solution.py:376
  22.8 1.0 shard_map.40.p0
  23.8 2.0 %shard_map.41 = (bf16[16,256,128]{2,1,0:T(8,128)(2,1)S(1)}, bf16[16,128,256]{2,1,0:T(8,128)(2,1)S(1)}, bf16[16,128,256]{2,1,0:T(8,128)(2,1)S(1)}, f32[16,128,256...) custom-call(s32[2]{0:T(128)S(1)} %compare_select_fusion.info, s32[8]{0:T(128)S(1)} %copy-done.1, ...), custom_call_target="tpu_custom_call" | custom-call | bytes 1024 | tf_op jit(solution)/shard_map/pallas_call | solution.py:32
  25.9 2.2 %collective-permute-done.4.p2 = bf16[4,2,128,128]{3,2,1,0:T(8,128)(2,1)S(1)} collective-permute-done((bf16[4,2,128,128]{3,2,1,0:T(8,128)(2,1)S(1)}, bf16[4,2,128,128]{3,2,1,0:T(8,128)(2,1)S(1)}, u32[]{:S(2)}, u32[]{:S(2)}) %collective-permute-start.4) | collective-permute-done | bytes 262176 | tf_op jit(solution)/shard_map/ppermute | solution.py:376
  29.0 19.2 %all_to_all.10.parts = bf16[32,32,128]{2,1,0:T(8,128)(2,1)S(1)} all-to-all(bf16[32,32,128]{2,1,0:T(8,128)(2,1)S(1)} %bitcast.10), channel_id=1, replica_groups=mesh['ctx'=32,'head'=8] {'ctx'}, dimensions={0} | all-to-all | bytes 524288 | tf_op jit(solution)/shard_map/all_to_all | solution.py:425
  48.2 1.1 %shard_map.43 = bf16[32,32,128]{2,1,0:T(8,128)(2,1)S(1)} custom-call(s32[2]{0:T(128)S(1)} %compare_select_fusion.info, s32[8]{0:T(128)S(1)} %copy-done.1, bf16[32,32,128]{2,1,0:T(8,128)(2,1)S(1)} %all_to_all.10.parts), custom_call_target="tpu_custom_call" | custom-call | bytes 1024 | tf_op jit(solution)/shard_map/pallas_call | solution.py:32
  49.4 14.2 %all_to_all.11 = bf16[32,32,128]{2,1,0:T(8,128)(2,1)S(1)} all-to-all(bf16[32,32,128]{2,1,0:T(8,128)(2,1)S(1)} %shard_map.43), channel_id=1, replica_groups=mesh['ctx'=32,'head'=8] {'ctx'}, dimensions={0} | all-to-all | bytes 524288 | tf_op jit(solution)/shard_map/all_to_all | solution.py:427
  63.6 2.2 %shard_map.44 = (bf16[4,2,128,128]{3,2,1,0:T(8,128)(2,1)S(1)}, bf16[4,2,128,128]{3,2,1,0:T(8,128)(2,1)S(1)}, bf16[4,2,128,128]{3,2,1,0:T(8,128)(2,1)S(1)}, bf16[4,2,128,128]{3,2,1,0:T(8,128)(2,1)S(1)}) custom-call(s32[2]{0:T(128)S(1)} %compare_select_fusion.info, s32[8]{0:T(128)S(1)} %copy-done.1, bf16[4,2,128,128]{3,2,1,0:T(8,128)(2,1)S(1)} %shard_map.40.p0, ...), custom_call_target="tpu_custom_call" | custom-call | bytes 1024 | tf_op jit(solution)/shard_map/pallas_call | solution.py:32
  65.8 2.4 %collective-permute-start.7 = (bf16[4,2,128,128]{3,2,1,0:T(8,128)(2,1)S(1)}, bf16[4,2,128,128]{3,2,1,0:T(8,128)(2,1)S(1)}, u32[]{:S(2)}, u32[]{:S(2)}) collective-permute-start(bf16[4,2,128,128]{3,2,1,0:T(8,128)(2,1)S(1)} %get-tuple-element.67), channel_id=1, source_target_pairs={{0,2},{1,3},{2,0},{3,1},{4,6},{5,7},{6,4},{7,5},{8,10},{9,11},{10,... | collective-permute-start | bytes 786440 | tf_op jit(solution)/shard_map/ppermute | solution.py:369
  68.3 2.3 %collective-permute-start.8 = (bf16[4,2,128,128]{3,2,1,0:T(8,128)(2,1)S(1)}, bf16[4,2,128,128]{3,2,1,0:T(8,128)(2,1)S(1)}, u32[]{:S(2)}, u32[]{:S(2)}) collective-permute-start(bf16[4,2,128,128]{3,2,1,0:T(8,128)(2,1)S(1)} %get-tuple-element.68), channel_id=1, source_target_pairs={{0,6},{1,7},{2,4},{3,5},{4,2},{5,3},{6,0},{7,1},{8,14},{9,15},{10,... | collective-permute-start | bytes 786440 | tf_op jit(solution)/shard_map/ppermute | solution.py:369
  70.6 6.1 %shard_map.45 = (bf16[4,128,128]{2,1,0:T(8,128)(2,1)S(1)}, bf16[4,128,128]{2,1,0:T(8,128)(2,1)S(1)}) custom-call(s32[2]{0:T(128)S(1)} %compare_select_fusion.info, f32[32]{0:T(128)S(1)} %copy-done.2, bf16[16,256,128]{2,1,0:T(8,128)(2,1)S(1)} %get-tuple-element.55.keys, bf16[16,128,256]{2,1,0:T(8,128)(2,1)S(1)} %get-tuple-element.56.key_t, ...), custom_call_target="tpu_custom_call" | custom-call | flops 4000000000 | bytes 1024 | tf_op jit(solution)/shard_map/pallas_call | solution.py:32
  76.7 1.4 %collective-permute-start.11 = (bf16[4,2,128,128]{3,2,1,0:T(8,128)(2,1)S(1)}, bf16[4,2,128,128]{3,2,1,0:T(8,128)(2,1)S(1)}, u32[]{:S(2)}, u32[]{:S(2)}) collective-permute-start(bf16[4,2,128,128]{3,2,1,0:T(8,128)(2,1)S(1)} %get-tuple-element.74), channel_id=1, source_target_pairs={{0,4},{1,5},{2,6},{3,7},{4,0},{5,1},{6,2},{7,3},{8,12},{9,13},{10,... | collective-permute-start | bytes 786440 | tf_op jit(solution)/shard_map/ppermute | solution.py:369
  78.1 11.6 %shard_map.46 = (bf16[8,128,128]{2,1,0:T(8,128)(2,1)S(1)}, bf16[8,128,128]{2,1,0:T(8,128)(2,1)S(1)}) custom-call(s32[2]{0:T(128)S(1)} %compare_select_fusion.info, f32[32]{0:T(128)S(1)} %copy-done.2, bf16[16,256,128]{2,1,0:T(8,128)(2,1)S(1)} %get-tuple-element.55.keys, bf16[16,128,256]{2,1,0:T(8,128)(2,1)S(1)} %get-tuple-element.56.key_t, ...), custom_call_target="tpu_custom_call" | custom-call | flops 8000000000 | bytes 1024 | tf_op jit(solution)/shard_map/pallas_call | solution.py:32
  89.7 4.3 %collective-permute-start.10 = (bf16[8,128,128]{2,1,0:T(8,128)(2,1)S(1)}, bf16[8,128,128]{2,1,0:T(8,128)(2,1)S(1)}, u32[]{:S(2)}, u32[]{:S(2)}) collective-permute-start(bf16[8,128,128]{2,1,0:T(8,128)(2,1)S(1)} %get-tuple-element.71), channel_id=1, source_target_pairs={{0,1},{1,0},{2,3},{3,2},{4,5},{5,4},{6,7},{7,6},{8,9},{9,8},{10,11... | collective-permute-start | bytes 786440 | tf_op jit(solution)/shard_map/ppermute | solution.py:366
  94.1 6.1 %shard_map.47 = (bf16[4,128,128]{2,1,0:T(8,128)(2,1)S(1)}, bf16[4,128,128]{2,1,0:T(8,128)(2,1)S(1)}) custom-call(s32[2]{0:T(128)S(1)} %compare_select_fusion.info, f32[32]{0:T(128)S(1)} %copy-done.2, bf16[16,256,128]{2,1,0:T(8,128)(2,1)S(1)} %get-tuple-element.55.keys, bf16[16,128,256]{2,1,0:T(8,128)(2,1)S(1)} %get-tuple-element.56.key_t, ...), custom_call_target="tpu_custom_call" | custom-call | flops 4000000000 | bytes 1024 | tf_op jit(solution)/shard_map/pallas_call | solution.py:32
  100.8 1.9 %unpack.2.rest_3_ = bf16[128,32,128]{2,1,0:T(8,128)(2,1)} custom-call(s32[2]{0:T(128)S(1)} %compare_select_fusion.info, bf16[4,128,128]{2,1,0:T(8,128)(2,1)S(1)} %get-tuple-element.73.rest_0_, bf16[8,128,128]{2,1,0:T(8,128)(2,1)S(1)} %get-tuple-element.69.rest_1_, bf16[4,128,128]{2,1,0:T(8,128)(2,1)S(1)} %get-tuple-element.76.rest_2_), custom_call_target="tpu_custom_call" | custom-call | tf_op jit(solution)/shard_map/unpack/pallas_call | solution.py:340
  102.7 1.9 %unpack.3 = bf16[128,32,128]{2,1,0:T(8,128)(2,1)} custom-call(s32[2]{0:T(128)S(1)} %compare_select_fusion.info, bf16[4,128,128]{2,1,0:T(8,128)(2,1)S(1)} %collective-permute-done.9.rest_0_, bf16[8,128,128]{2,1,0:T(8,128)(2,1)S(1)} %collective-permute-done.10.rest_1_, ...), custom_call_target="tpu_custom_call", output_to_operand_aliasing={{}: (4, {})} | custom-call | tf_op jit(solution)/shard_map/unpack/pallas_call | solution.py:340
  (30 shorter events, 6.8 us)
Async XLA Ops:
  0.0 5.6 %copy-start = (bf16[128,3,32,128]{3,2,1,0:T(8,128)(2,1)S(1)}, bf16[128,3,32,128]{3,2,1,0:T(8,128)(2,1)}, u32[]{:S(2)}) copy-start(bf16[128,3,32,128]{3,2,1,0:T(8,128)(2,1)} %param.3) | copy-start | bytes 9437188
  2.4 5.9 %copy-start.1 = (s32[8]{0:T(128)S(1)}, s32[8]{0:T(128)}, u32[]{:S(2)}) copy-start(s32[8]{0:T(128)} %lengths.15) | copy-start | bytes 100
  2.4 5.9 %collective-permute-start = (bf16[2,8,128,128]{3,2,1,0:T(8,128)(2,1)S(1)}, bf16[2,8,128,128]{3,2,1,0:T(8,128)(2,1)S(1)}, u32[]{:S(2)}, u32[]{:S(2)}) collective-permute-start(bf16[2,8,128,128]{3,2,1,0:T(8,128)(2,1)S(1)} %pack.6), channel_id=1, source_target_pairs={{0,1},{1,0},{2,3},{3,2},{4,5},{5,4},{6,7},{7,6},{8,9},{9,8},{10,11... | collective-permute-start | bytes 1572872 | tf_op jit(solution)/shard_map/ppermute | solution.py:366
  8.2 3.4 %collective-permute-start.1 = (bf16[2,8,128,128]{3,2,1,0:T(8,128)(2,1)S(1)}, bf16[2,8,128,128]{3,2,1,0:T(8,128)(2,1)S(1)}, u32[]{:S(2)}, u32[]{:S(2)}) collective-permute-start(bf16[2,8,128,128]{3,2,1,0:T(8,128)(2,1)S(1)} %pack.8), channel_id=1, source_target_pairs={{0,1},{1,0},{2,3},{3,2},{4,5},{5,4},{6,7},{7,6},{8,9},{9,8},{10,11... | collective-permute-start | bytes 1572872 | tf_op jit(solution)/shard_map/ppermute | solution.py:366
  13.6 10.2 %collective-permute-start.6 = (bf16[1,16,128,128]{3,2,1,0:T(8,128)(2,1)S(1)}, bf16[1,16,128,128]{3,2,1,0:T(8,128)(2,1)S(1)}, u32[]{:S(2)}, u32[]{:S(2)}) collective-permute-start(bf16[1,16,128,128]{3,2,1,0:T(8,128)(2,1)S(1)} %pack.10), channel_id=1, source_target_pairs={{0,1},{1,0},{2,3},{3,2},{4,5},{5,4},{6,7},{7,6},{8,9},{9,8},{10,11... | collective-permute-start | bytes 1572872 | tf_op jit(solution)/shard_map/ppermute | solution.py:366
  14.1 7.7 %collective-permute-start.3 = (bf16[4,2,128,128]{3,2,1,0:T(8,128)(2,1)S(1)}, bf16[4,2,128,128]{3,2,1,0:T(8,128)(2,1)S(1)}, u32[]{:S(2)}, u32[]{:S(2)}) collective-permute-start(bf16[4,2,128,128]{3,2,1,0:T(8,128)(2,1)S(1)} %shard_map.37), channel_id=1, source_target_pairs={{0,2},{2,4},{4,6},{6,0},{1,7},{3,1},{5,3},{7,5},{8,10},{10,12},{12... | collective-permute-start | bytes 786440 | tf_op jit(solution)/shard_map/ppermute | solution.py:376
  14.9 10.9 %collective-permute-start.2 = (bf16[4,2,128,128]{3,2,1,0:T(8,128)(2,1)S(1)}, bf16[4,2,128,128]{3,2,1,0:T(8,128)(2,1)S(1)}, u32[]{:S(2)}, u32[]{:S(2)}) collective-permute-start(bf16[4,2,128,128]{3,2,1,0:T(8,128)(2,1)S(1)} %shard_map.39), channel_id=1, source_target_pairs={{0,2},{1,3},{2,0},{3,1},{4,6},{5,7},{6,4},{7,5},{8,10},{9,11},{10,... | collective-permute-start | bytes 786440 | tf_op jit(solution)/shard_map/ppermute | solution.py:369
  15.6 10.3 %collective-permute-start.5 = (bf16[4,2,128,128]{3,2,1,0:T(8,128)(2,1)S(1)}, bf16[4,2,128,128]{3,2,1,0:T(8,128)(2,1)S(1)}, u32[]{:S(2)}, u32[]{:S(2)}) collective-permute-start(bf16[4,2,128,128]{3,2,1,0:T(8,128)(2,1)S(1)} %shard_map.38), channel_id=1, source_target_pairs={{0,6},{1,7},{2,4},{3,5},{4,2},{5,3},{6,0},{7,1},{8,14},{9,15},{10,... | collective-permute-start | bytes 786440 | tf_op jit(solution)/shard_map/ppermute | solution.py:369
  21.8 6.3 %collective-permute-start.4 = (bf16[4,2,128,128]{3,2,1,0:T(8,128)(2,1)S(1)}, bf16[4,2,128,128]{3,2,1,0:T(8,128)(2,1)S(1)}, u32[]{:S(2)}, u32[]{:S(2)}) collective-permute-start(bf16[4,2,128,128]{3,2,1,0:T(8,128)(2,1)S(1)} %collective-permute-done.3), channel_id=1, source_target_pairs={{0,2},{2,4},{4,6},{6,0},{1,7},{3,1},{5,3},{7,5},{8,10},{10,12},{12... | collective-permute-start | bytes 786440 | tf_op jit(solution)/shard_map/ppermute | solution.py:376
  23.8 46.8 %copy-start.2 = (f32[32]{0:T(128)S(1)}, f32[32]{0:T(128)}, u32[]{:S(2)}) copy-start(f32[32]{0:T(128)} %reg.5) | copy-start | bytes 388
  65.8 12.3 %collective-permute-start.7 = (bf16[4,2,128,128]{3,2,1,0:T(8,128)(2,1)S(1)}, bf16[4,2,128,128]{3,2,1,0:T(8,128)(2,1)S(1)}, u32[]{:S(2)}, u32[]{:S(2)}) collective-permute-start(bf16[4,2,128,128]{3,2,1,0:T(8,128)(2,1)S(1)} %get-tuple-element.67), channel_id=1, source_target_pairs={{0,2},{1,3},{2,0},{3,1},{4,6},{5,7},{6,4},{7,5},{8,10},{9,11},{10,... | collective-permute-start | bytes 786440 | tf_op jit(solution)/shard_map/ppermute | solution.py:369
  68.3 9.8 %collective-permute-start.8 = (bf16[4,2,128,128]{3,2,1,0:T(8,128)(2,1)S(1)}, bf16[4,2,128,128]{3,2,1,0:T(8,128)(2,1)S(1)}, u32[]{:S(2)}, u32[]{:S(2)}) collective-permute-start(bf16[4,2,128,128]{3,2,1,0:T(8,128)(2,1)S(1)} %get-tuple-element.68), channel_id=1, source_target_pairs={{0,6},{1,7},{2,4},{3,5},{4,2},{5,3},{6,0},{7,1},{8,14},{9,15},{10,... | collective-permute-start | bytes 786440 | tf_op jit(solution)/shard_map/ppermute | solution.py:369
  76.7 17.3 %collective-permute-start.11 = (bf16[4,2,128,128]{3,2,1,0:T(8,128)(2,1)S(1)}, bf16[4,2,128,128]{3,2,1,0:T(8,128)(2,1)S(1)}, u32[]{:S(2)}, u32[]{:S(2)}) collective-permute-start(bf16[4,2,128,128]{3,2,1,0:T(8,128)(2,1)S(1)} %get-tuple-element.74), channel_id=1, source_target_pairs={{0,4},{1,5},{2,6},{3,7},{4,0},{5,1},{6,2},{7,3},{8,12},{9,13},{10,... | collective-permute-start | bytes 786440 | tf_op jit(solution)/shard_map/ppermute | solution.py:369
  89.7 13.0 %collective-permute-start.10 = (bf16[8,128,128]{2,1,0:T(8,128)(2,1)S(1)}, bf16[8,128,128]{2,1,0:T(8,128)(2,1)S(1)}, u32[]{:S(2)}, u32[]{:S(2)}) collective-permute-start(bf16[8,128,128]{2,1,0:T(8,128)(2,1)S(1)} %get-tuple-element.71), channel_id=1, source_target_pairs={{0,1},{1,0},{2,3},{3,2},{4,5},{5,4},{6,7},{7,6},{8,9},{9,8},{10,11... | collective-permute-start | bytes 786440 | tf_op jit(solution)/shard_map/ppermute | solution.py:366
  100.2 2.5 %collective-permute-start.12 = (bf16[4,128,128]{2,1,0:T(8,128)(2,1)S(1)}, bf16[4,128,128]{2,1,0:T(8,128)(2,1)S(1)}, u32[]{:S(2)}, u32[]{:S(2)}) collective-permute-start(bf16[4,128,128]{2,1,0:T(8,128)(2,1)S(1)} %get-tuple-element.75), channel_id=1, source_target_pairs={{0,1},{1,0},{2,3},{3,2},{4,5},{5,4},{6,7},{7,6},{8,9},{9,8},{10,11... | collective-permute-start | bytes 393224 | tf_op jit(solution)/shard_map/ppermute | solution.py:366
  100.3 2.4 %collective-permute-start.9 = (bf16[4,128,128]{2,1,0:T(8,128)(2,1)S(1)}, bf16[4,128,128]{2,1,0:T(8,128)(2,1)S(1)}, u32[]{:S(2)}, u32[]{:S(2)}) collective-permute-start(bf16[4,128,128]{2,1,0:T(8,128)(2,1)S(1)} %get-tuple-element.70), channel_id=1, source_target_pairs={{0,1},{1,0},{2,3},{3,2},{4,5},{5,4},{6,7},{7,6},{8,9},{9,8},{10,11... | collective-permute-start | bytes 393224 | tf_op jit(solution)/shard_map/ppermute | solution.py:366

commit v9 on v8

--- a/solution.py
+++ b/solution.py
@@ -82,19 +82,20 @@
     return jnp.where(beside, 0.0, state)
 
 
-def pack_kernel(keys_first, info, x_ref, out_ref, stage):
-    rows, count, _ = x_ref.shape
-    part = x_ref[...].astype(F32)
-    stage[...] = part.reshape(rows * count, HD)
-    if keys_first:
-
-        @pl.when(pl.program_id(0) == 0)
-        def _():
-            scale = lax.rsqrt(jnp.mean(part * part, axis=-1, keepdims=True) + 1e-06)
-            stage[...] = (part * scale / math.sqrt(HD)).reshape(rows * count, HD)
-
-    for h in range(count):
-        out_ref[0, h] = stage[pl.ds(h, rows, stride=count), :].astype(BF)
+def pack_kernel(keys_first, info, x_ref, out_ref):
+    if not keys_first:
+        out_ref[0] = jnp.swapaxes(x_ref[...], 0, 1)
+        return
+
+    @pl.when(pl.program_id(0) == 0)
+    def _():
+        part = x_ref[...].astype(F32)
+        scale = lax.rsqrt(jnp.mean(part * part, axis=-1, keepdims=True) + 1e-06)
+        out_ref[0] = jnp.swapaxes((part * scale / math.sqrt(HD)).astype(BF), 0, 1)
+
+    @pl.when(pl.program_id(0) > 0)
+    def _():
+        out_ref[0] = jnp.swapaxes(x_ref[...], 0, 1)
 
 
 def pack(info, qkv, kinds, count, other, far=False):
@@ -116,7 +117,6 @@
             grid=(len(kinds),),
             in_specs=[pl.BlockSpec((rows, count, HD), place)],
             out_specs=pl.BlockSpec((1, count, rows, HD), lambda g, info: (g, 0, 0, 0)),
-            scratch_shapes=[pltpu.VMEM((rows * count, HD), F32)],
         ),
         out_shape=jax.ShapeDtypeStruct((len(kinds), count, rows, HD), BF),
         compiler_params=pltpu.CompilerParams(vmem_limit_bytes=12 << 20),
@@ -322,12 +322,11 @@
 def unpack_kernel(info, *rest):
     x, _, _, _ = spot(info)
     parts, (out_ref, stage) = rest[: len(GROUPS)], rest[-2:]
-    rows = out_ref.shape[0]
     for shifts, part in zip(GROUPS, parts):
         for i in range(len(shifts) * PER):
             h = (x ^ shifts[i // PER]) * PER + i % PER
-            stage[pl.ds(h, rows, stride=16), :] = part[i].astype(F32)
-    out_ref[...] = stage[...].reshape(rows, 16, HD).astype(BF)
+            stage[h] = part[i]
+    out_ref[...] = jnp.swapaxes(stage[...], 0, 1)
 
 
 def unpack(info, parts, other, shape, base=()):
@@ -344,7 +343,7 @@
             grid=(1,),
             in_specs=[VMEM] * len(parts) + [pl.BlockSpec(memory_space=pl.ANY)] * len(base),
             out_specs=pl.BlockSpec((rows, 16, HD), place),
-            scratch_shapes=[pltpu.VMEM((rows * 16, HD), F32)],
+            scratch_shapes=[pltpu.VMEM((16, rows, HD), BF)],
         ),
         out_shape=jax.ShapeDtypeStruct(shape, BF),
         input_output_aliases={1 + len(parts): 0} if base else {},

time: 105 us -> 103 us (0.981)
  Pallas kernels: 46.1 us -> 44.3 us
    pallas_call x6, Pallas kernels: 8 us -> 6.93 us  [pack(): pl.pallas_call(functools.partial(pack_kernel, kinds[0] == 1), grid_spec=p...]
where the time goes in v9:
time: 103 us
  Pallas kernels  44.3 us (43%)
  blocking collectives  33.5 us (33%)
  starting transfers between devices  16.5 us (16%)
  waiting for transfers between devices  8.56 us (8%)
    pallas_call x11, Pallas kernels, run(): pl.pallas_call(kernel, in_specs=[SMEM] * scalars + [VMEM] * (len(args) -...  34.3 us
    all_to_all x1, blocking collectives, body(): lax.all_to_all(total.reshape(places, -1, width), 'ctx', 0, 0, tiled=True)  19.2 us
    all_to_all x1, blocking collectives, body(): lax.all_to_all(entries, 'ctx', 0, 0, tiled=True).reshape(states.shape)  14.2 us
    ppermute x6, starting transfers between devices, swap(): return lax.ppermute(a, 'head', [(i, i ^ 1) for i in range(2 * NX)])  8.87 us
    ppermute x2, waiting for transfers between devices, relay(): return lax.ppermute(a, 'head', ring + back)  8.53 us
    pallas_call x6, Pallas kernels, pack(): pl.pallas_call(functools.partial(pack_kernel, kinds[0] == 1), grid_spec=p...  6.93 us
    ppermute x5, starting transfers between devices, along_x(): lax.ppermute(a, 'head', [(i, 2 * (i // 2 ^ shift) + i % 2) for i in range...  6.88 us
    pallas_call x2, Pallas kernels, unpack(): pl.pallas_call(unpack_kernel, grid_spec=pltpu.PrefetchScalarGridSpec(num_...  3.15 us
  transfers between devices with their start and end apart: 13, of which 2 were waited for; matrix products, arithmetic and copies ran while one was open for 0% of the time, Pallas kernels for 34%

profile of v9, /device:TPU:1, one launch (start us, length us, event | category | flops | bytes accessed | tf_op | source)
XLA Modules:
  0.0 103.1 jit_solution(14939682942349172656)
XLA Ops:
  0.0 2.2 %pack.6 = bf16[2,8,128,128]{3,2,1,0:T(8,128)(2,1)S(1)} custom-call(s32[2]{0:T(128)S(1)} %compare_select_fusion.info, bf16[128,96,128]{2,1,0:T(8,128)(2,1)} %bitcast.3), custom_call_target="tpu_custom_call" | custom-call | bytes 1024 | tf_op jit(solution)/shard_map/pack/pallas_call | solution.py:113
  2.2 3.3 %collective-permute-start = (bf16[2,8,128,128]{3,2,1,0:T(8,128)(2,1)S(1)}, bf16[2,8,128,128]{3,2,1,0:T(8,128)(2,1)S(1)}, u32[]{:S(2)}, u32[]{:S(2)}) collective-permute-start(bf16[2,8,128,128]{3,2,1,0:T(8,128)(2,1)S(1)} %pack.6), channel_id=1, source_target_pairs={{0,1},{1,0},{2,3},{3,2},{4,5},{5,4},{6,7},{7,6},{8,9},{9,8},{10,11... | collective-permute-start | bytes 1572872 | tf_op jit(solution)/shard_map/ppermute | solution.py:365
  5.5 1.1 %pack.7.own.far_own = bf16[2,8,128,128]{3,2,1,0:T(8,128)(2,1)S(1)} custom-call(s32[2]{0:T(128)S(1)} %compare_select_fusion.info, bf16[128,96,128]{2,1,0:T(8,128)(2,1)S(1)} %bitcast.4), custom_call_target="tpu_custom_call" | custom-call | bytes 1024 | tf_op jit(solution)/shard_map/pack/pallas_call | solution.py:113
  6.6 1.1 %pack.8 = bf16[2,8,128,128]{3,2,1,0:T(8,128)(2,1)S(1)} custom-call(s32[2]{0:T(128)S(1)} %compare_select_fusion.info, bf16[128,96,128]{2,1,0:T(8,128)(2,1)S(1)} %bitcast.5), custom_call_target="tpu_custom_call" | custom-call | bytes 1024 | tf_op jit(solution)/shard_map/pack/pallas_call | solution.py:113
  7.8 1.0 shard_map.37
  8.9 1.0 shard_map.38
  9.9 1.1 %pack.9.own.near_own = bf16[2,8,128,128]{3,2,1,0:T(8,128)(2,1)S(1)} custom-call(s32[2]{0:T(128)S(1)} %compare_select_fusion.info, bf16[128,96,128]{2,1,0:T(8,128)(2,1)S(1)} %bitcast.6), custom_call_target="tpu_custom_call" | custom-call | bytes 1024 | tf_op jit(solution)/shard_map/pack/pallas_call | solution.py:113
  14.9 6.1 %collective-permute-done.3 = bf16[4,2,128,128]{3,2,1,0:T(8,128)(2,1)S(1)} collective-permute-done((bf16[4,2,128,128]{3,2,1,0:T(8,128)(2,1)S(1)}, bf16[4,2,128,128]{3,2,1,0:T(8,128)(2,1)S(1)}, u32[]{:S(2)}, u32[]{:S(2)}) %collective-permute-start.3) | collective-permute-done | bytes 262176 | tf_op jit(solution)/shard_map/ppermute | solution.py:375
  21.7 1.0 shard_map.40.p0
  22.8 2.0 %shard_map.41 = (bf16[16,256,128]{2,1,0:T(8,128)(2,1)S(1)}, bf16[16,128,256]{2,1,0:T(8,128)(2,1)S(1)}, bf16[16,128,256]{2,1,0:T(8,128)(2,1)S(1)}, f32[16,128,256...) custom-call(s32[2]{0:T(128)S(1)} %compare_select_fusion.info, s32[8]{0:T(128)S(1)} %copy-done.1, ...), custom_call_target="tpu_custom_call" | custom-call | bytes 1024 | tf_op jit(solution)/shard_map/pallas_call | solution.py:32
  24.8 2.4 %collective-permute-done.4.p2 = bf16[4,2,128,128]{3,2,1,0:T(8,128)(2,1)S(1)} collective-permute-done((bf16[4,2,128,128]{3,2,1,0:T(8,128)(2,1)S(1)}, bf16[4,2,128,128]{3,2,1,0:T(8,128)(2,1)S(1)}, u32[]{:S(2)}, u32[]{:S(2)}) %collective-permute-start.4) | collective-permute-done | bytes 262176 | tf_op jit(solution)/shard_map/ppermute | solution.py:375
  28.2 19.2 %all_to_all.10.parts = bf16[32,32,128]{2,1,0:T(8,128)(2,1)S(1)} all-to-all(bf16[32,32,128]{2,1,0:T(8,128)(2,1)S(1)} %bitcast.10), channel_id=1, replica_groups=mesh['ctx'=32,'head'=8] {'ctx'}, dimensions={0} | all-to-all | bytes 524288 | tf_op jit(solution)/shard_map/all_to_all | solution.py:424
  47.4 1.1 %shard_map.43 = bf16[32,32,128]{2,1,0:T(8,128)(2,1)S(1)} custom-call(s32[2]{0:T(128)S(1)} %compare_select_fusion.info, s32[8]{0:T(128)S(1)} %copy-done.1, bf16[32,32,128]{2,1,0:T(8,128)(2,1)S(1)} %all_to_all.10.parts), custom_call_target="tpu_custom_call" | custom-call | bytes 1024 | tf_op jit(solution)/shard_map/pallas_call | solution.py:32
  48.6 14.2 %all_to_all.11 = bf16[32,32,128]{2,1,0:T(8,128)(2,1)S(1)} all-to-all(bf16[32,32,128]{2,1,0:T(8,128)(2,1)S(1)} %shard_map.43), channel_id=1, replica_groups=mesh['ctx'=32,'head'=8] {'ctx'}, dimensions={0} | all-to-all | bytes 524288 | tf_op jit(solution)/shard_map/all_to_all | solution.py:426
  62.8 2.2 %shard_map.44 = (bf16[4,2,128,128]{3,2,1,0:T(8,128)(2,1)S(1)}, bf16[4,2,128,128]{3,2,1,0:T(8,128)(2,1)S(1)}, bf16[4,2,128,128]{3,2,1,0:T(8,128)(2,1)S(1)}, bf16[4,2,128,128]{3,2,1,0:T(8,128)(2,1)S(1)}) custom-call(s32[2]{0:T(128)S(1)} %compare_select_fusion.info, s32[8]{0:T(128)S(1)} %copy-done.1, bf16[4,2,128,128]{3,2,1,0:T(8,128)(2,1)S(1)} %shard_map.40.p0, ...), custom_call_target="tpu_custom_call" | custom-call | bytes 1024 | tf_op jit(solution)/shard_map/pallas_call | solution.py:32
  65.0 2.6 %collective-permute-start.7 = (bf16[4,2,128,128]{3,2,1,0:T(8,128)(2,1)S(1)}, bf16[4,2,128,128]{3,2,1,0:T(8,128)(2,1)S(1)}, u32[]{:S(2)}, u32[]{:S(2)}) collective-permute-start(bf16[4,2,128,128]{3,2,1,0:T(8,128)(2,1)S(1)} %get-tuple-element.67), channel_id=1, source_target_pairs={{0,2},{1,3},{2,0},{3,1},{4,6},{5,7},{6,4},{7,5},{8,10},{9,11},{10,... | collective-permute-start | bytes 786440 | tf_op jit(solution)/shard_map/ppermute | solution.py:368
  67.6 2.3 %collective-permute-start.8 = (bf16[4,2,128,128]{3,2,1,0:T(8,128)(2,1)S(1)}, bf16[4,2,128,128]{3,2,1,0:T(8,128)(2,1)S(1)}, u32[]{:S(2)}, u32[]{:S(2)}) collective-permute-start(bf16[4,2,128,128]{3,2,1,0:T(8,128)(2,1)S(1)} %get-tuple-element.68), channel_id=1, source_target_pairs={{0,6},{1,7},{2,4},{3,5},{4,2},{5,3},{6,0},{7,1},{8,14},{9,15},{10,... | collective-permute-start | bytes 786440 | tf_op jit(solution)/shard_map/ppermute | solution.py:368
  69.9 6.1 %shard_map.45 = (bf16[4,128,128]{2,1,0:T(8,128)(2,1)S(1)}, bf16[4,128,128]{2,1,0:T(8,128)(2,1)S(1)}) custom-call(s32[2]{0:T(128)S(1)} %compare_select_fusion.info, f32[32]{0:T(128)S(1)} %copy-done.2, bf16[16,256,128]{2,1,0:T(8,128)(2,1)S(1)} %get-tuple-element.55.keys, bf16[16,128,256]{2,1,0:T(8,128)(2,1)S(1)} %get-tuple-element.56.key_t, ...), custom_call_target="tpu_custom_call" | custom-call | flops 4000000000 | bytes 1024 | tf_op jit(solution)/shard_map/pallas_call | solution.py:32
  76.1 1.2 %collective-permute-start.11 = (bf16[4,2,128,128]{3,2,1,0:T(8,128)(2,1)S(1)}, bf16[4,2,128,128]{3,2,1,0:T(8,128)(2,1)S(1)}, u32[]{:S(2)}, u32[]{:S(2)}) collective-permute-start(bf16[4,2,128,128]{3,2,1,0:T(8,128)(2,1)S(1)} %get-tuple-element.74), channel_id=1, source_target_pairs={{0,4},{1,5},{2,6},{3,7},{4,0},{5,1},{6,2},{7,3},{8,12},{9,13},{10,... | collective-permute-start | bytes 786440 | tf_op jit(solution)/shard_map/ppermute | solution.py:368
  77.3 11.6 %shard_map.46 = (bf16[8,128,128]{2,1,0:T(8,128)(2,1)S(1)}, bf16[8,128,128]{2,1,0:T(8,128)(2,1)S(1)}) custom-call(s32[2]{0:T(128)S(1)} %compare_select_fusion.info, f32[32]{0:T(128)S(1)} %copy-done.2, bf16[16,256,128]{2,1,0:T(8,128)(2,1)S(1)} %get-tuple-element.55.keys, bf16[16,128,256]{2,1,0:T(8,128)(2,1)S(1)} %get-tuple-element.56.key_t, ...), custom_call_target="tpu_custom_call" | custom-call | flops 8000000000 | bytes 1024 | tf_op jit(solution)/shard_map/pallas_call | solution.py:32
  88.9 4.3 %collective-permute-start.10 = (bf16[8,128,128]{2,1,0:T(8,128)(2,1)S(1)}, bf16[8,128,128]{2,1,0:T(8,128)(2,1)S(1)}, u32[]{:S(2)}, u32[]{:S(2)}) collective-permute-start(bf16[8,128,128]{2,1,0:T(8,128)(2,1)S(1)} %get-tuple-element.71), channel_id=1, source_target_pairs={{0,1},{1,0},{2,3},{3,2},{4,5},{5,4},{6,7},{7,6},{8,9},{9,8},{10,11... | collective-permute-start | bytes 786440 | tf_op jit(solution)/shard_map/ppermute | solution.py:365
  93.2 6.1 %shard_map.47 = (bf16[4,128,128]{2,1,0:T(8,128)(2,1)S(1)}, bf16[4,128,128]{2,1,0:T(8,128)(2,1)S(1)}) custom-call(s32[2]{0:T(128)S(1)} %compare_select_fusion.info, f32[32]{0:T(128)S(1)} %copy-done.2, bf16[16,256,128]{2,1,0:T(8,128)(2,1)S(1)} %get-tuple-element.55.keys, bf16[16,128,256]{2,1,0:T(8,128)(2,1)S(1)} %get-tuple-element.56.key_t, ...), custom_call_target="tpu_custom_call" | custom-call | flops 4000000000 | bytes 1024 | tf_op jit(solution)/shard_map/pallas_call | solution.py:32
  99.9 1.6 %unpack.2.rest_3_ = bf16[128,32,128]{2,1,0:T(8,128)(2,1)} custom-call(s32[2]{0:T(128)S(1)} %compare_select_fusion.info, bf16[4,128,128]{2,1,0:T(8,128)(2,1)S(1)} %get-tuple-element.73.rest_0_, bf16[8,128,128]{2,1,0:T(8,128)(2,1)S(1)} %get-tuple-element.69.rest_1_, bf16[4,128,128]{2,1,0:T(8,128)(2,1)S(1)} %get-tuple-element.76.rest_2_), custom_call_target="tpu_custom_call" | custom-call | tf_op jit(solution)/shard_map/unpack/pallas_call | solution.py:339
  101.5 1.6 %unpack.3 = bf16[128,32,128]{2,1,0:T(8,128)(2,1)} custom-call(s32[2]{0:T(128)S(1)} %compare_select_fusion.info, bf16[4,128,128]{2,1,0:T(8,128)(2,1)S(1)} %collective-permute-done.9.rest_0_, bf16[8,128,128]{2,1,0:T(8,128)(2,1)S(1)} %collective-permute-done.10.rest_1_, ...), custom_call_target="tpu_custom_call", output_to_operand_aliasing={{}: (4, {})} | custom-call | tf_op jit(solution)/shard_map/unpack/pallas_call | solution.py:339
  (30 shorter events, 6.3 us)
Async XLA Ops:
  0.0 5.5 %copy-start = (bf16[128,3,32,128]{3,2,1,0:T(8,128)(2,1)S(1)}, bf16[128,3,32,128]{3,2,1,0:T(8,128)(2,1)}, u32[]{:S(2)}) copy-start(bf16[128,3,32,128]{3,2,1,0:T(8,128)(2,1)} %param.3) | copy-start | bytes 9437188
  2.2 5.6 %copy-start.1 = (s32[8]{0:T(128)S(1)}, s32[8]{0:T(128)}, u32[]{:S(2)}) copy-start(s32[8]{0:T(128)} %lengths.15) | copy-start | bytes 100
  2.2 5.6 %collective-permute-start = (bf16[2,8,128,128]{3,2,1,0:T(8,128)(2,1)S(1)}, bf16[2,8,128,128]{3,2,1,0:T(8,128)(2,1)S(1)}, u32[]{:S(2)}, u32[]{:S(2)}) collective-permute-start(bf16[2,8,128,128]{3,2,1,0:T(8,128)(2,1)S(1)} %pack.6), channel_id=1, source_target_pairs={{0,1},{1,0},{2,3},{3,2},{4,5},{5,4},{6,7},{7,6},{8,9},{9,8},{10,11... | collective-permute-start | bytes 1572872 | tf_op jit(solution)/shard_map/ppermute | solution.py:365
  7.7 3.3 %collective-permute-start.1 = (bf16[2,8,128,128]{3,2,1,0:T(8,128)(2,1)S(1)}, bf16[2,8,128,128]{3,2,1,0:T(8,128)(2,1)S(1)}, u32[]{:S(2)}, u32[]{:S(2)}) collective-permute-start(bf16[2,8,128,128]{3,2,1,0:T(8,128)(2,1)S(1)} %pack.8), channel_id=1, source_target_pairs={{0,1},{1,0},{2,3},{3,2},{4,5},{5,4},{6,7},{7,6},{8,9},{9,8},{10,11... | collective-permute-start | bytes 1572872 | tf_op jit(solution)/shard_map/ppermute | solution.py:365
  12.7 10.0 %collective-permute-start.6 = (bf16[1,16,128,128]{3,2,1,0:T(8,128)(2,1)S(1)}, bf16[1,16,128,128]{3,2,1,0:T(8,128)(2,1)S(1)}, u32[]{:S(2)}, u32[]{:S(2)}) collective-permute-start(bf16[1,16,128,128]{3,2,1,0:T(8,128)(2,1)S(1)} %pack.10), channel_id=1, source_target_pairs={{0,1},{1,0},{2,3},{3,2},{4,5},{5,4},{6,7},{7,6},{8,9},{9,8},{10,11... | collective-permute-start | bytes 1572872 | tf_op jit(solution)/shard_map/ppermute | solution.py:365
  13.3 7.7 %collective-permute-start.3 = (bf16[4,2,128,128]{3,2,1,0:T(8,128)(2,1)S(1)}, bf16[4,2,128,128]{3,2,1,0:T(8,128)(2,1)S(1)}, u32[]{:S(2)}, u32[]{:S(2)}) collective-permute-start(bf16[4,2,128,128]{3,2,1,0:T(8,128)(2,1)S(1)} %shard_map.37), channel_id=1, source_target_pairs={{0,2},{2,4},{4,6},{6,0},{1,7},{3,1},{5,3},{7,5},{8,10},{10,12},{12... | collective-permute-start | bytes 786440 | tf_op jit(solution)/shard_map/ppermute | solution.py:375
  14.1 10.7 %collective-permute-start.2 = (bf16[4,2,128,128]{3,2,1,0:T(8,128)(2,1)S(1)}, bf16[4,2,128,128]{3,2,1,0:T(8,128)(2,1)S(1)}, u32[]{:S(2)}, u32[]{:S(2)}) collective-permute-start(bf16[4,2,128,128]{3,2,1,0:T(8,128)(2,1)S(1)} %shard_map.39), channel_id=1, source_target_pairs={{0,2},{1,3},{2,0},{3,1},{4,6},{5,7},{6,4},{7,5},{8,10},{9,11},{10,... | collective-permute-start | bytes 786440 | tf_op jit(solution)/shard_map/ppermute | solution.py:368
  14.8 10.0 %collective-permute-start.5 = (bf16[4,2,128,128]{3,2,1,0:T(8,128)(2,1)S(1)}, bf16[4,2,128,128]{3,2,1,0:T(8,128)(2,1)S(1)}, u32[]{:S(2)}, u32[]{:S(2)}) collective-permute-start(bf16[4,2,128,128]{3,2,1,0:T(8,128)(2,1)S(1)} %shard_map.38), channel_id=1, source_target_pairs={{0,6},{1,7},{2,4},{3,5},{4,2},{5,3},{6,0},{7,1},{8,14},{9,15},{10,... | collective-permute-start | bytes 786440 | tf_op jit(solution)/shard_map/ppermute | solution.py:368
  21.0 6.3 %collective-permute-start.4 = (bf16[4,2,128,128]{3,2,1,0:T(8,128)(2,1)S(1)}, bf16[4,2,128,128]{3,2,1,0:T(8,128)(2,1)S(1)}, u32[]{:S(2)}, u32[]{:S(2)}) collective-permute-start(bf16[4,2,128,128]{3,2,1,0:T(8,128)(2,1)S(1)} %collective-permute-done.3), channel_id=1, source_target_pairs={{0,2},{2,4},{4,6},{6,0},{1,7},{3,1},{5,3},{7,5},{8,10},{10,12},{12... | collective-permute-start | bytes 786440 | tf_op jit(solution)/shard_map/ppermute | solution.py:375
  22.7 47.2 %copy-start.2 = (f32[32]{0:T(128)S(1)}, f32[32]{0:T(128)}, u32[]{:S(2)}) copy-start(f32[32]{0:T(128)} %reg.5) | copy-start | bytes 388
  65.0 12.2 %collective-permute-start.7 = (bf16[4,2,128,128]{3,2,1,0:T(8,128)(2,1)S(1)}, bf16[4,2,128,128]{3,2,1,0:T(8,128)(2,1)S(1)}, u32[]{:S(2)}, u32[]{:S(2)}) collective-permute-start(bf16[4,2,128,128]{3,2,1,0:T(8,128)(2,1)S(1)} %get-tuple-element.67), channel_id=1, source_target_pairs={{0,2},{1,3},{2,0},{3,1},{4,6},{5,7},{6,4},{7,5},{8,10},{9,11},{10,... | collective-permute-start | bytes 786440 | tf_op jit(solution)/shard_map/ppermute | solution.py:368
  67.6 9.6 %collective-permute-start.8 = (bf16[4,2,128,128]{3,2,1,0:T(8,128)(2,1)S(1)}, bf16[4,2,128,128]{3,2,1,0:T(8,128)(2,1)S(1)}, u32[]{:S(2)}, u32[]{:S(2)}) collective-permute-start(bf16[4,2,128,128]{3,2,1,0:T(8,128)(2,1)S(1)} %get-tuple-element.68), channel_id=1, source_target_pairs={{0,6},{1,7},{2,4},{3,5},{4,2},{5,3},{6,0},{7,1},{8,14},{9,15},{10,... | collective-permute-start | bytes 786440 | tf_op jit(solution)/shard_map/ppermute | solution.py:368
  76.1 17.1 %collective-permute-start.11 = (bf16[4,2,128,128]{3,2,1,0:T(8,128)(2,1)S(1)}, bf16[4,2,128,128]{3,2,1,0:T(8,128)(2,1)S(1)}, u32[]{:S(2)}, u32[]{:S(2)}) collective-permute-start(bf16[4,2,128,128]{3,2,1,0:T(8,128)(2,1)S(1)} %get-tuple-element.74), channel_id=1, source_target_pairs={{0,4},{1,5},{2,6},{3,7},{4,0},{5,1},{6,2},{7,3},{8,12},{9,13},{10,... | collective-permute-start | bytes 786440 | tf_op jit(solution)/shard_map/ppermute | solution.py:368
  88.9 12.7 %collective-permute-start.10 = (bf16[8,128,128]{2,1,0:T(8,128)(2,1)S(1)}, bf16[8,128,128]{2,1,0:T(8,128)(2,1)S(1)}, u32[]{:S(2)}, u32[]{:S(2)}) collective-permute-start(bf16[8,128,128]{2,1,0:T(8,128)(2,1)S(1)} %get-tuple-element.71), channel_id=1, source_target_pairs={{0,1},{1,0},{2,3},{3,2},{4,5},{5,4},{6,7},{7,6},{8,9},{9,8},{10,11... | collective-permute-start | bytes 786440 | tf_op jit(solution)/shard_map/ppermute | solution.py:365
  99.3 2.2 %collective-permute-start.12 = (bf16[4,128,128]{2,1,0:T(8,128)(2,1)S(1)}, bf16[4,128,128]{2,1,0:T(8,128)(2,1)S(1)}, u32[]{:S(2)}, u32[]{:S(2)}) collective-permute-start(bf16[4,128,128]{2,1,0:T(8,128)(2,1)S(1)} %get-tuple-element.75), channel_id=1, source_target_pairs={{0,1},{1,0},{2,3},{3,2},{4,5},{5,4},{6,7},{7,6},{8,9},{9,8},{10,11... | collective-permute-start | bytes 393224 | tf_op jit(solution)/shard_map/ppermute | solution.py:365
  99.5 2.1 %collective-permute-start.9 = (bf16[4,128,128]{2,1,0:T(8,128)(2,1)S(1)}, bf16[4,128,128]{2,1,0:T(8,128)(2,1)S(1)}, u32[]{:S(2)}, u32[]{:S(2)}) collective-permute-start(bf16[4,128,128]{2,1,0:T(8,128)(2,1)S(1)} %get-tuple-element.70), channel_id=1, source_target_pairs={{0,1},{1,0},{2,3},{3,2},{4,5},{5,4},{6,7},{7,6},{8,9},{9,8},{10,11... | collective-permute-start | bytes 393224 | tf_op jit(solution)/shard_map/ppermute | solution.py:365
